TPU v7x, 256 devices: a whole 4x4x8 slice. The times are simulated.
256 devices in a mesh: seq: 32 (over z, x_hi, core), kv: 8 (over x_lo, y).
Axes of the slice: x: 4 (x_hi: 2, x_lo: 2; x = x_hi * 2 + x_lo), y: 4, z: 8, core: 2. Of those that a mesh axis runs over, the one named last changes fastest.
Arguments:
- queries: bfloat16 [4096, 8192], P('seq', 'kv'), may hold values from -60 to 60
- keys: bfloat16 [4096, 1024], P('seq', 'kv'), may hold values from -8 to 8
- values: bfloat16 [4096, 1024], P('seq', 'kv'), may hold values from -6 to 6
- out_weight: bfloat16 [8192, 8192], P(None, ('kv', 'seq')), may hold values from -0.0625 to 0.0625
- out_grad: bfloat16 [4096, 8192], P('seq', 'kv'), may hold values from -6 to 6
- doc_ids: int32 [4096], P('seq'), may hold values from 0 to 6, never falling along the last dimension, each value on 1 to 1152 neighbouring positions
- block_mask: int32 [32, 32], P('seq'), may hold values 0 or 1
- positions: int32 [3, 4096], P(None, 'seq'), may hold values from 0 to 1023
Outputs:
- layer_out: bfloat16 [4096, 8192], P('seq', 'kv')
- query_grad: bfloat16 [4096, 8192], P('seq', 'kv')
- key_grad: bfloat16 [4096, 1024], P('seq', 'kv')
- value_grad: bfloat16 [4096, 1024], P('seq', 'kv')
Inputs may be any that keep to these rules, and one draw needn't show every extreme that they name: `doc_ids`: every document has at most 1152 tokens, and one has exactly 1152.
All inputs are finite; a program needn't handle non-finite values. No bound on the sum of `block_mask` on one device may be relied on, other than what follows from the above.
Results may differ from a plain program's by a relative error of at most 0.017.
Values may be sent and summed in bfloat16 or wider, within the bound.
A program may use at most 128 MiB of HBM per device.

v0:
```python
import math

import jax
import jax.numpy as jnp
from jax import lax
from jax.sharding import Mesh
from jax.sharding import PartitionSpec as P

HD = 128
BLK = 128
REACH = 9

SEQ = ("sz", "core")

rope_base = 1000000.0


def seq_size():
    return lax.axis_size("sz") * lax.axis_size("core")


def seq_index():
    return lax.axis_index("sz") * lax.axis_size("core") + lax.axis_index("core")


def shifted(block, distance):
    count = seq_size()
    devices = range(count)
    route = [(i - distance, i) for i in devices if i - distance in devices]
    return lax.ppermute(block, SEQ, route)


def rope_tables(positions):
    pairs = HD // 2
    index = jnp.arange(pairs)
    inv_freq = jnp.exp(index.astype(jnp.float32) * (-2.0 * math.log(rope_base) / HD))
    temporal = HD // 8
    which = jnp.where(index >= pairs - temporal, 0, jnp.where(index % 2 == 0, 1, 2))
    places = positions.astype(jnp.float32)
    chosen = jnp.where((which == 0)[:, None], places[0][None, :], 0.0)
    chosen = chosen + jnp.where((which == 1)[:, None], places[1][None, :], 0.0)
    chosen = chosen + jnp.where((which == 2)[:, None], places[2][None, :], 0.0)
    angle = chosen.T * inv_freq[None, :]
    return (jnp.cos(angle), jnp.sin(angle))


def rotate(block, cosine, sine, sign):
    half = HD // 2
    first = block[..., :half]
    second = block[..., half:]
    cos_part = cosine[:, None, :]
    sin_part = sine[:, None, :] * sign
    return jnp.concatenate(
        [first * cos_part - second * sin_part, second * cos_part + first * sin_part], axis=-1
    )


def allowed_mask(shard, doc_query, doc_key, mask_rows):
    length = doc_query.shape[0]
    width = doc_key.shape[0]
    query_pos = shard * length + jnp.arange(length, dtype=jnp.int32)
    key_pos = (shard - REACH) * length + jnp.arange(width, dtype=jnp.int32)
    near = jnp.repeat(jnp.repeat(mask_rows, BLK, axis=0), BLK, axis=1) > 0
    same_block = query_pos[:, None] // BLK == key_pos[None, :] // BLK
    return (
        (doc_query[:, None] == doc_key[None, :])
        & (key_pos[None, :] <= query_pos[:, None])
        & (key_pos[None, :] >= 0)
        & (near | same_block)
    )


def attend(query, key_win, value_win, allowed, grad_out):
    scale = HD ** (-0.5)
    contract = (((1,), (1,)), ((), ()))
    columns = (((0,), (0,)), ((), ()))
    scores = lax.dot_general(query, key_win, contract, preferred_element_type=jnp.float32) * scale
    scores = jnp.where(allowed, scores, -1e30)
    top = jnp.max(scores, axis=1, keepdims=True)
    expo = jnp.exp(scores - top)
    weights = (expo / jnp.sum(expo, axis=1, keepdims=True)).astype(jnp.bfloat16)
    output = jnp.dot(weights, value_win, preferred_element_type=jnp.float32).astype(jnp.bfloat16)
    delta = jnp.sum(
        grad_out.astype(jnp.float32) * output.astype(jnp.float32), axis=1, keepdims=True
    )
    dprob = lax.dot_general(grad_out, value_win, contract, preferred_element_type=jnp.float32)
    dscore = (weights.astype(jnp.float32) * (dprob - delta)).astype(jnp.bfloat16)
    dquery = jnp.dot(dscore, key_win, preferred_element_type=jnp.float32) * scale
    dkey = lax.dot_general(dscore, query, columns, preferred_element_type=jnp.float32) * scale
    dvalue = lax.dot_general(weights, grad_out, columns, preferred_element_type=jnp.float32)
    return (output, dquery, dkey, dvalue)


def gather_window(packed):
    one = jnp.concatenate([shifted(packed, 1), packed], axis=0)
    two = jnp.concatenate([shifted(one, 2), one], axis=0)
    four = jnp.concatenate([shifted(two, 4), two], axis=0)
    far = shifted(one, 8)
    return jnp.concatenate([far, four], axis=0)


def return_window(pieces):
    far = shifted(pieces[:2].astype(jnp.bfloat16), -8).astype(jnp.float32)
    four = pieces[2:]
    two = four[4:] + shifted(four[:4].astype(jnp.bfloat16), -4).astype(jnp.float32)
    one = two[2:] + shifted(two[:2].astype(jnp.bfloat16), -2).astype(jnp.float32) + far
    return one[1] + shifted(one[:1].astype(jnp.bfloat16), -1).astype(jnp.float32)[0]


def per_device(queries, keys, values, out_weight, out_grad, doc_ids, block_mask, positions):
    length = queries.shape[0]
    groups = keys.shape[1] // HD
    heads = queries.shape[1] // HD
    per_group = heads // groups
    n_sz = lax.axis_size("sz")
    n_core = lax.axis_size("core")
    shard = seq_index()
    cosine, sine = rope_tables(positions)
    q_rot = (
        rotate(queries.astype(jnp.float32).reshape(length, heads, HD), cosine, sine, 1.0)
        .astype(jnp.bfloat16)
        .reshape(length, heads * HD)
    )
    k_rot = (
        rotate(keys.astype(jnp.float32).reshape(length, groups, HD), cosine, sine, 1.0)
        .astype(jnp.bfloat16)
        .reshape(length, groups * HD)
    )
    kv_count = lax.axis_size("kv")
    kv_me = lax.axis_index("kv")
    col_w = out_weight.shape[1]
    n_seq = seq_size()
    pieces = lax.all_to_all(out_weight, "kv", split_axis=0, concat_axis=1, tiled=True)
    stripes = lax.all_gather(pieces, SEQ, axis=1, tiled=True)
    og_list = [out_grad.reshape(length, n_seq, col_w)]
    for j in range(1, kv_count):
        got = lax.ppermute(out_grad, "kv", [(i, (i - j) % kv_count) for i in range(kv_count)])
        og_list.append(got.reshape(length, n_seq, col_w))
    og_stack = jnp.stack(og_list, axis=2)
    og_perm = jnp.roll(og_stack, kv_me, axis=2).reshape(length, -1)
    contract = (((1,), (1,)), ((), ()))
    head_grad = lax.dot_general(
        og_perm, stripes, contract, preferred_element_type=jnp.float32
    ).astype(jnp.bfloat16)
    width = keys.shape[1]
    doc_row = jnp.zeros((1, 2 * width), jnp.bfloat16).at[0, :length].set(
        doc_ids.astype(jnp.bfloat16)
    )
    packed = jnp.concatenate(
        [jnp.concatenate([k_rot, values], axis=1), doc_row], axis=0
    )[None]
    win = gather_window(packed)
    key_win = win[:, :length, :width].reshape(-1, width)
    value_win = win[:, :length, width:].reshape(-1, width)
    doc_win = win[:, length, :length].reshape(-1).astype(jnp.int32)
    blocks_dev = length // BLK
    mask_pad = jnp.pad(block_mask, ((0, 0), (REACH * blocks_dev, 0)))
    mask_rows = lax.dynamic_slice_in_dim(mask_pad, shard * blocks_dev, (REACH + 1) * blocks_dev, 1)
    allowed = allowed_mask(shard, doc_ids, doc_win, mask_rows)
    scale = HD ** (-0.5)
    q_grp = q_rot.reshape(length, per_group, HD)
    g_grp = head_grad.reshape(length, per_group, HD)
    scores = jnp.einsum("thd,ud->htu", q_grp, key_win, preferred_element_type=jnp.float32) * scale
    scores = jnp.where(allowed[None], scores, -1e30)
    top = jnp.max(scores, axis=2, keepdims=True)
    expo = jnp.exp(scores - top)
    weights = (expo / jnp.sum(expo, axis=2, keepdims=True)).astype(jnp.bfloat16)
    out_grp = jnp.einsum(
        "htu,ud->thd", weights, value_win, preferred_element_type=jnp.float32
    ).astype(jnp.bfloat16)
    delta = jnp.sum(g_grp.astype(jnp.float32) * out_grp.astype(jnp.float32), axis=2)
    dprob = jnp.einsum("thd,ud->htu", g_grp, value_win, preferred_element_type=jnp.float32)
    dscore = (weights.astype(jnp.float32) * (dprob - delta.T[:, :, None])).astype(jnp.bfloat16)
    dq_rot = jnp.einsum("htu,ud->thd", dscore, key_win, preferred_element_type=jnp.float32) * scale
    dkey_sum = jnp.einsum("htu,thd->ud", dscore, q_grp, preferred_element_type=jnp.float32) * scale
    dvalue_sum = jnp.einsum("htu,thd->ud", weights, g_grp, preferred_element_type=jnp.float32)
    attn = out_grp.reshape(length, per_group * HD)
    lo_part = jnp.dot(attn, stripes, preferred_element_type=jnp.float32).astype(jnp.bfloat16)
    lo_part = lo_part.reshape(length, n_seq, kv_count, col_w)
    total = lax.dynamic_index_in_dim(lo_part, kv_me, 2, keepdims=False).astype(jnp.float32)
    for j in range(1, kv_count):
        dest = (kv_me + j) % kv_count
        piece = lax.dynamic_index_in_dim(lo_part, dest, 2, keepdims=False)
        got = lax.ppermute(piece, "kv", [(i, (i + j) % kv_count) for i in range(kv_count)])
        total = total + got.astype(jnp.float32)
    layer_out = total.reshape(length, n_seq * col_w).astype(jnp.bfloat16)
    dkv = jnp.concatenate([dkey_sum, dvalue_sum], axis=1).reshape(REACH + 1, length, 2 * HD)
    dkv_total = return_window(dkv)
    dk_total = dkv_total[:, :HD]
    dv_total = dkv_total[:, HD:]
    query_grad = rotate(dq_rot, cosine, sine, -1.0).astype(jnp.bfloat16).reshape(length, heads * HD)
    key_grad = (
        rotate(dk_total.reshape(length, groups, HD), cosine, sine, -1.0)
        .astype(jnp.bfloat16)
        .reshape(length, groups * HD)
    )
    value_grad = dv_total.astype(jnp.bfloat16)
    return (layer_out, query_grad, key_grad, value_grad)


def solution(mesh):
    n_seq, n_kv = mesh.devices.shape
    cores = 2 if n_seq % 2 == 0 else 1
    grid = Mesh(mesh.devices.reshape(n_seq // cores, cores, n_kv), ("sz", "core", "kv"))
    in_specs = (
        P(SEQ, "kv"),
        P(SEQ, "kv"),
        P(SEQ, "kv"),
        P(None, ("kv",) + SEQ),
        P(SEQ, "kv"),
        P(SEQ),
        P(SEQ, None),
        P(None, SEQ),
    )
    out_specs = (P(SEQ, "kv"), P(SEQ, "kv"), P(SEQ, "kv"), P(SEQ, "kv"))
    return jax.shard_map(
        per_device, mesh=grid, in_specs=in_specs, out_specs=out_specs, check_vma=False
    )
```

profile of v0, /device:TPU:64, one launch (start us, length us, event | category | flops | bytes accessed | tf_op | source)
XLA Modules:
  0.0 266.6 jit_solution(8853894389698526556)
XLA Ops:
  7.2 1.1 copy.133
  8.3 15.4 %all_to_all.19 = bf16[8,1024,32]{1,2,0:T(8,128)(2,1)} all-to-all(bf16[8,1024,32]{1,2,0:T(8,128)(2,1)S(1)} %bitcast.136), channel_id=1, replica_groups=mesh['sz'=16,'core'=2,'kv'=8] {'kv'}, dimensions={0} | all-to-all | bytes 1048576 | tf_op jit(solution)/shard_map/all_to_all | solution.py:133
  23.7 1.1 copy.92
  24.8 1.5 collective-permute-start.11
  26.4 1.5 collective-permute-start.12
  29.5 1.3 fusion.34
  32.8 1.9 collective-permute-start
  34.8 1.1 copy.85
  37.3 1.0 broadcast_multiply_fusion
  38.4 3.0 %collective-permute-done = bf16[1,129,256]{2,1,0:T(8,128)(2,1)S(1)} collective-permute-done((bf16[1,129,256]{2,1,0:T(8,128)(2,1)S(1)}, bf16[1,129,256]{2,1,0:T(8,128)(2,1)S(1)}, u32[]{:S(2)}, u32[]{:S(2)}) %collective-permute-start) | collective-permute-done | bytes 66080 | tf_op jit(solution)/shard_map/ppermute | solution.py:30
  41.5 14.8 %collective-permute-start.2 = (bf16[2,129,256]{2,1,0:T(8,128)(2,1)S(1)}, bf16[2,129,256]{2,1,0:T(8,128)(2,1)S(1)}, u32[]{:S(2)}, u32[]{:S(2)}) collective-permute-start(bf16[2,129,256]{2,1,0:T(8,128)(2,1)S(1)} %pad_maximum_fusion.4), channel_id=1, source_target_pairs={{0,16},{8,24},{16,32},{24,40},{32,48},{40,56},{48,64},{56,72},{64,... | collective-permute-start | bytes 396296 | tf_op jit(solution)/shard_map/ppermute | solution.py:30
  56.3 6.4 %collective-permute-start.1 = (bf16[2,129,256]{2,1,0:T(8,128)(2,1)S(1)}, bf16[2,129,256]{2,1,0:T(8,128)(2,1)S(1)}, u32[]{:S(2)}, u32[]{:S(2)}) collective-permute-start(bf16[2,129,256]{2,1,0:T(8,128)(2,1)S(1)} %pad_maximum_fusion.4), channel_id=1, source_target_pairs={{0,64},{8,72},{16,80},{24,88},{32,96},{40,104},{48,112},{56,120},{... | collective-permute-start | bytes 396296 | tf_op jit(solution)/shard_map/ppermute | solution.py:30
  63.4 1.4 collective-permute-start.14
  64.9 4.6 %collective-permute-done.1 = bf16[2,129,256]{2,1,0:T(8,128)(2,1)S(1)} collective-permute-done((bf16[2,129,256]{2,1,0:T(8,128)(2,1)S(1)}, bf16[2,129,256]{2,1,0:T(8,128)(2,1)S(1)}, u32[]{:S(2)}, u32[]{:S(2)}) %collective-permute-start.1) | collective-permute-done | bytes 132128 | tf_op jit(solution)/shard_map/ppermute | solution.py:30
  70.3 1.3 collective-permute-start.17
  72.3 2.7 %collective-permute-start.3 = (bf16[4,129,256]{2,1,0:T(8,128)(2,1)S(1)}, bf16[4,129,256]{2,1,0:T(8,128)(2,1)S(1)}, u32[]{:S(2)}, u32[]{:S(2)}) collective-permute-start(bf16[4,129,256]{2,1,0:T(8,128)(2,1)S(1)} %pad_maximum_fusion.1), channel_id=1, source_target_pairs={{0,32},{8,40},{16,48},{24,56},{32,64},{40,72},{48,80},{56,88},{64,... | collective-permute-start | bytes 792584 | tf_op jit(solution)/shard_map/ppermute | solution.py:30
  77.6 1.9 collective-permute-done.16
  80.2 2.1 collective-permute-done.17
  88.8 2.2 constant_dynamic-slice_fusion
  91.0 1.9 copy.100
  93.4 1.6 or_and_fusion
  95.0 4.2 %exponential_reduce_fusion = (f32[8,128]{1,0:T(8,128)S(1)}, f32[8,128,1280]{1,2,0:T(8,128)}) fusion(bf16[1280,128,1]{1,0,2:T(8,128)(2,1)S(1)} %bitcast.138, pred[128,1280]{0,1:T(8,128)(4,1)S(1)} %or_and_fusion, bf16[128,8,64]{2,0,1:T(8,128)(2,1)S(1)} %get-tuple-element.36, bf16[128,8,64]{2,0,1:T(8,128)(2,1)S(1)} %get-tuple-element.35), kind=kOutput, calls=%fused_computation.8 | convolution fusion | flops 341312768 | bytes 6000640 | tf_op jit(solution)/shard_map/sub | solution.py:166
  99.2 3.2 %divide_convert_fusion = bf16[8,128,1280]{1,2,0:T(8,128)(2,1)S(1)} fusion(f32[8,128,1280]{1,2,0:T(8,128)} %get-tuple-element.54, f32[8,128]{1,0:T(8,128)S(1)} %get-tuple-element.53), kind=kLoop, calls=%fused_computation.7 | loop fusion | flops 2621440 | bytes 7868416 | tf_op jit(solution)/shard_map/convert_element_type | solution.py:167
  102.4 66.9 %all-gather.2.cloned.1.call-done = bf16[1024,8192]{0,1:T(8,128)(2,1)} async-done(((bf16[1024,256]{0,1:T(8,128)(2,1)}), bf16[1024,8192]{0,1:T(8,128)(2,1)}) %all-gather.2.cloned.1.call-update) | async-done | bytes 16777232 | tf_op jit(solution)/shard_map/all_gather | solution.py:134
  169.3 8.8 %convolution_convert_fusion.2 = bf16[128,1024]{1,0:T(8,128)(2,1)S(1)} fusion(bf16[128,8192]{0,1:T(8,128)(2,1)} %bitcast.124, bf16[1024,8192]{0,1:T(8,128)(2,1)} %all-gather.2.cloned.1.call-done), kind=kOutput, calls=%fused_computation.19 | convolution fusion | flops 2147614720 | bytes 19136512 | tf_op jit(solution)/shard_map/dot_general | solution.py:142
  178.8 1.0 convolution_bitcast_fusion
  180.8 1.1 fusion.4
  182.9 12.8 %convolution_convert_fusion = bf16[128,8192]{1,0:T(8,128)(2,1)} fusion(bf16[128,1024]{0,1:T(8,128)(2,1)S(1)} %bitcast.137, bf16[1024,8192]{0,1:T(8,128)(2,1)} %all-gather.2.cloned.1.call-done), kind=kOutput, calls=%fused_computation.1 | convolution fusion | flops 2148532224 | bytes 19136512 | tf_op jit(solution)/shard_map/dot_general | solution.py:178
  195.7 4.4 %copy.91 = bf16[128,8192]{0,1:T(8,128)(2,1)} copy(bf16[128,8192]{1,0:T(8,128)(2,1)} %convolution_convert_fusion) | data formatting | bytes 4194304 | tf_op jit(solution)/shard_map/convert_element_type | solution.py:178
  200.1 2.7 %dynamic-slice_bitcast_fusion.6 = (bf16[128,32,32]{0,2,1:T(8,128)(2,1)}, bf16[128,32,32]{0,2,1:T(8,128)(2,1)}, bf16[128,32,32]{0,2,1:T(8,128)(2,1)}, bf16[128,32...) fusion(bf16[128,32,8,32]{0,3,2,1:T(8,128)(2,1)} %bitcast.125, ...), kind=kLoop, calls=%fused_computation.49 | loop fusion | bytes 3670044 | tf_op jit(solution)/shard_map/jit(dynamic_index_in_dim)/squeeze | solution.py:183
  202.8 2.8 %collective-permute-start.10 = (bf16[128,32,32]{0,2,1:T(8,128)(2,1)}, bf16[128,32,32]{0,2,1:T(8,128)(2,1)}, u32[]{:S(2)}, u32[]{:S(2)}) collective-permute-start(bf16[128,32,32]{0,2,1:T(8,128)(2,1)} %get-tuple-element.29), channel_id=1, source_target_pairs={{0,7},{1,0},{2,1},{3,2},{4,3},{5,4},{6,5},{7,6},{8,15},{9,8},{10,9... | collective-permute-start | bytes 786440 | tf_op jit(solution)/shard_map/ppermute | solution.py:184
  206.4 1.8 collective-permute-start.8
  208.2 1.0 copy.126
  210.0 2.2 collective-permute-start.18
  212.9 3.1 %collective-permute-start.20 = (bf16[2,128,256]{2,1,0:T(8,128)(2,1)}, bf16[2,128,256]{2,1,0:T(8,128)(2,1)S(1)}, u32[]{:S(2)}, u32[]{:S(2)}) collective-permute-start(bf16[2,128,256]{2,1,0:T(8,128)(2,1)} %bitcast.158), channel_id=1, source_target_pairs={{64,0},{72,8},{80,16},{88,24},{96,32},{104,40},{112,48},{120,56},{... | collective-permute-start | bytes 393224 | tf_op jit(solution)/shard_map/ppermute | solution.py:30
  216.1 2.1 fusion.6
  218.2 3.8 %collective-permute-done.18 = bf16[4,128,256]{2,1,0:T(8,128)(2,1)} collective-permute-done((bf16[4,128,256]{2,1,0:T(8,128)(2,1)}, bf16[4,128,256]{2,1,0:T(8,128)(2,1)}, u32[]{:S(2)}, u32[]{:S(2)}) %collective-permute-start.18) | collective-permute-done | bytes 262176 | tf_op jit(solution)/shard_map/ppermute | solution.py:30
  222.0 1.0 convert_add_fusion.1
  223.0 2.4 collective-permute-start.19
  225.7 2.9 %collective-permute-done.20 = bf16[2,128,256]{2,1,0:T(8,128)(2,1)S(1)} collective-permute-done((bf16[2,128,256]{2,1,0:T(8,128)(2,1)}, bf16[2,128,256]{2,1,0:T(8,128)(2,1)S(1)}, u32[]{:S(2)}, u32[]{:S(2)}) %collective-permute-start.20) | collective-permute-done | bytes 131104 | tf_op jit(solution)/shard_map/ppermute | solution.py:30
  229.2 2.7 %collective-permute-start.6 = (bf16[128,32,32]{0,2,1:T(8,128)(2,1)}, bf16[128,32,32]{0,2,1:T(8,128)(2,1)S(1)}, u32[]{:S(2)}, u32[]{:S(2)}) collective-permute-start(bf16[128,32,32]{0,2,1:T(8,128)(2,1)} %get-tuple-element.33), channel_id=1, source_target_pairs={{0,3},{1,4},{2,5},{3,6},{4,7},{5,0},{6,1},{7,2},{8,11},{9,12},{10,... | collective-permute-start | bytes 786440 | tf_op jit(solution)/shard_map/ppermute | solution.py:184
  231.9 2.0 collective-permute-start.5
  234.0 1.8 collective-permute-done.19
  237.9 1.9 collective-permute-start.21
  240.0 3.5 %collective-permute-done.6 = bf16[128,32,32]{0,2,1:T(8,128)(2,1)S(1)} collective-permute-done((bf16[128,32,32]{0,2,1:T(8,128)(2,1)}, bf16[128,32,32]{0,2,1:T(8,128)(2,1)S(1)}, u32[]{:S(2)}, u32[]{:S(2)}) %collective-permute-start.6) | collective-permute-done | bytes 262176 | tf_op jit(solution)/shard_map/ppermute | solution.py:184
  243.5 7.9 %collective-permute-done.5 = bf16[128,32,32]{0,2,1:T(8,128)(2,1)S(1)} collective-permute-done((bf16[128,32,32]{0,2,1:T(8,128)(2,1)}, bf16[128,32,32]{0,2,1:T(8,128)(2,1)S(1)}, u32[]{:S(2)}, u32[]{:S(2)}) %collective-permute-start.5) | collective-permute-done | bytes 262176 | tf_op jit(solution)/shard_map/ppermute | solution.py:184
  251.3 4.3 %collective-permute-done.4 = bf16[128,32,32]{0,2,1:T(8,128)(2,1)S(1)} collective-permute-done((bf16[128,32,32]{0,2,1:T(8,128)(2,1)S(1)}, bf16[128,32,32]{0,2,1:T(8,128)(2,1)S(1)}, u32[]{:S(2)}, u32[]{:S(2)}) %collective-permute-start.4) | collective-permute-done | bytes 262176 | tf_op jit(solution)/shard_map/ppermute | solution.py:184
  255.7 1.5 fusion.14
  (133 shorter events, 28.3 us)
Async XLA Ops:
  7.2 29.2 %copy-start.22 = (s32[1,32]{1,0:T(1,128)S(1)}, s32[1,32]{1,0:T(1,128)}, u32[]{:S(2)}) copy-start(s32[1,32]{1,0:T(1,128)} %param.16) | copy-start | bytes 388
  7.2 162.1 %all-gather.2.cloned.1.call-start = ((), (), s32[]{:S(2)}) async-start(), calls=%async_computation.1 | async-start | bytes 17301504 | tf_op jit(solution)/shard_map/all_gather | solution.py:134
  24.8 44.6 %collective-permute-start.11 = (bf16[128,1024]{0,1:T(8,128)(2,1)S(1)}, bf16[128,1024]{0,1:T(8,128)(2,1)S(1)}, u32[]{:S(2)}, u32[]{:S(2)}) collective-permute-start(bf16[128,1024]{0,1:T(8,128)(2,1)S(1)} %copy.92), channel_id=1, source_target_pairs={{0,7},{1,0},{2,1},{3,2},{4,3},{5,4},{6,5},{7,6},{8,15},{9,8},{10,9... | collective-permute-start | bytes 786440 | tf_op jit(solution)/shard_map/ppermute | solution.py:137
  26.4 43.9 %collective-permute-start.12 = (bf16[128,1024]{0,1:T(8,128)(2,1)S(1)}, bf16[128,1024]{0,1:T(8,128)(2,1)S(1)}, u32[]{:S(2)}, u32[]{:S(2)}) collective-permute-start(bf16[128,1024]{0,1:T(8,128)(2,1)S(1)} %copy.92), channel_id=1, source_target_pairs={{0,6},{1,7},{2,0},{3,1},{4,2},{5,3},{6,4},{7,5},{8,14},{9,15},{10,... | collective-permute-start | bytes 786440 | tf_op jit(solution)/shard_map/ppermute | solution.py:137
  27.8 44.5 %collective-permute-start.13 = (bf16[128,1024]{0,1:T(8,128)(2,1)S(1)}, bf16[128,1024]{0,1:T(8,128)(2,1)S(1)}, u32[]{:S(2)}, u32[]{:S(2)}) collective-permute-start(bf16[128,1024]{0,1:T(8,128)(2,1)S(1)} %copy.92), channel_id=1, source_target_pairs={{0,5},{1,6},{2,7},{3,0},{4,1},{5,2},{6,3},{7,4},{8,13},{9,14},{10,... | collective-permute-start | bytes 786440 | tf_op jit(solution)/shard_map/ppermute | solution.py:137
  29.5 12.0 %copy-start.15 = (pred[64]{0:T(512)(128)(4,1)}, pred[64]{0:T(512)(128)(4,1)S(1)}, u32[]{:S(2)}) copy-start(pred[64]{0:T(512)(128)(4,1)S(1)} %broadcast_compare_fusion.2) | copy-start | bytes 196
  29.5 12.0 %copy-start.17 = (pred[64]{0:T(512)(128)(4,1)}, pred[64]{0:T(512)(128)(4,1)S(1)}, u32[]{:S(2)}) copy-start(pred[64]{0:T(512)(128)(4,1)S(1)} %get-tuple-element.57) | copy-start | bytes 196
  29.5 12.0 %copy-start.19 = (pred[64]{0:T(512)(128)(4,1)}, pred[64]{0:T(512)(128)(4,1)S(1)}, u32[]{:S(2)}) copy-start(pred[64]{0:T(512)(128)(4,1)S(1)} %get-tuple-element.58) | copy-start | bytes 196
  32.8 8.6 %collective-permute-start = (bf16[1,129,256]{2,1,0:T(8,128)(2,1)S(1)}, bf16[1,129,256]{2,1,0:T(8,128)(2,1)S(1)}, u32[]{:S(2)}, u32[]{:S(2)}) collective-permute-start(bf16[1,129,256]{2,1,0:T(8,128)(2,1)S(1)} %fusion.19), channel_id=1, source_target_pairs={{0,8},{8,16},{16,24},{24,32},{32,40},{40,48},{48,56},{56,64},{64,7... | collective-permute-start | bytes 198152 | tf_op jit(solution)/shard_map/ppermute | solution.py:30
  38.2 3.2 %copy-start.9 = (f32[128,64]{1,0:T(8,128)}, f32[128,64]{1,0:T(8,128)S(1)}, u32[]{:S(2)}) copy-start(f32[128,64]{1,0:T(8,128)S(1)} %get-tuple-element.49) | copy-start | bytes 98308
  38.4 56.6 %copy-start.5 = (bf16[128,8,64]{2,0,1:T(8,128)(2,1)}, bf16[128,8,64]{2,0,1:T(8,128)(2,1)S(1)}, u32[]{:S(2)}) copy-start(bf16[128,8,64]{2,0,1:T(8,128)(2,1)S(1)} %get-tuple-element.35) | copy-start | bytes 393220
  38.4 56.6 %copy-start.7 = (bf16[128,8,64]{2,0,1:T(8,128)(2,1)}, bf16[128,8,64]{2,0,1:T(8,128)(2,1)S(1)}, u32[]{:S(2)}) copy-start(bf16[128,8,64]{2,0,1:T(8,128)(2,1)S(1)} %get-tuple-element.36) | copy-start | bytes 393220
  41.5 21.9 %collective-permute-start.2 = (bf16[2,129,256]{2,1,0:T(8,128)(2,1)S(1)}, bf16[2,129,256]{2,1,0:T(8,128)(2,1)S(1)}, u32[]{:S(2)}, u32[]{:S(2)}) collective-permute-start(bf16[2,129,256]{2,1,0:T(8,128)(2,1)S(1)} %pad_maximum_fusion.4), channel_id=1, source_target_pairs={{0,16},{8,24},{16,32},{24,40},{32,48},{40,56},{48,64},{56,72},{64,... | collective-permute-start | bytes 396296 | tf_op jit(solution)/shard_map/ppermute | solution.py:30
  56.3 13.2 %collective-permute-start.1 = (bf16[2,129,256]{2,1,0:T(8,128)(2,1)S(1)}, bf16[2,129,256]{2,1,0:T(8,128)(2,1)S(1)}, u32[]{:S(2)}, u32[]{:S(2)}) collective-permute-start(bf16[2,129,256]{2,1,0:T(8,128)(2,1)S(1)} %pad_maximum_fusion.4), channel_id=1, source_target_pairs={{0,64},{8,72},{16,80},{24,88},{32,96},{40,104},{48,112},{56,120},{... | collective-permute-start | bytes 396296 | tf_op jit(solution)/shard_map/ppermute | solution.py:30
  63.4 12.4 %collective-permute-start.14 = (bf16[128,1024]{0,1:T(8,128)(2,1)S(1)}, bf16[128,1024]{0,1:T(8,128)(2,1)S(1)}, u32[]{:S(2)}, u32[]{:S(2)}) collective-permute-start(bf16[128,1024]{0,1:T(8,128)(2,1)S(1)} %copy.92), channel_id=1, source_target_pairs={{0,4},{1,5},{2,6},{3,7},{4,0},{5,1},{6,2},{7,3},{8,12},{9,13},{10,... | collective-permute-start | bytes 786440 | tf_op jit(solution)/shard_map/ppermute | solution.py:137
  69.4 7.4 %collective-permute-start.15 = (bf16[128,1024]{0,1:T(8,128)(2,1)S(1)}, bf16[128,1024]{0,1:T(8,128)(2,1)S(1)}, u32[]{:S(2)}, u32[]{:S(2)}) collective-permute-start(bf16[128,1024]{0,1:T(8,128)(2,1)S(1)} %copy.92), channel_id=1, source_target_pairs={{0,3},{1,4},{2,5},{3,6},{4,7},{5,0},{6,1},{7,2},{8,11},{9,12},{10,... | collective-permute-start | bytes 786440 | tf_op jit(solution)/shard_map/ppermute | solution.py:137
  69.5 10.0 %collective-permute-start.16 = (bf16[128,1024]{0,1:T(8,128)(2,1)S(1)}, bf16[128,1024]{0,1:T(8,128)(2,1)S(1)}, u32[]{:S(2)}, u32[]{:S(2)}) collective-permute-start(bf16[128,1024]{0,1:T(8,128)(2,1)S(1)} %copy.92), channel_id=1, source_target_pairs={{0,2},{1,3},{2,4},{3,5},{4,6},{5,7},{6,0},{7,1},{8,10},{9,11},{10,... | collective-permute-start | bytes 786440 | tf_op jit(solution)/shard_map/ppermute | solution.py:137
  70.3 12.0 %collective-permute-start.17 = (bf16[128,1024]{0,1:T(8,128)(2,1)S(1)}, bf16[128,1024]{0,1:T(8,128)(2,1)S(1)}, u32[]{:S(2)}, u32[]{:S(2)}) collective-permute-start(bf16[128,1024]{0,1:T(8,128)(2,1)S(1)} %copy.92), channel_id=1, source_target_pairs={{0,1},{1,2},{2,3},{3,4},{4,5},{5,6},{6,7},{7,0},{8,9},{9,10},{10,1... | collective-permute-start | bytes 786440 | tf_op jit(solution)/shard_map/ppermute | solution.py:137
  72.3 20.7 %collective-permute-start.3 = (bf16[4,129,256]{2,1,0:T(8,128)(2,1)S(1)}, bf16[4,129,256]{2,1,0:T(8,128)(2,1)S(1)}, u32[]{:S(2)}, u32[]{:S(2)}) collective-permute-start(bf16[4,129,256]{2,1,0:T(8,128)(2,1)S(1)} %pad_maximum_fusion.1), channel_id=1, source_target_pairs={{0,32},{8,40},{16,48},{24,56},{32,64},{40,72},{48,80},{56,88},{64,... | collective-permute-start | bytes 792584 | tf_op jit(solution)/shard_map/ppermute | solution.py:30
  88.8 4.3 %copy-start.14 = (bf16[128,128]{1,0:T(8,128)(2,1)S(1)}, bf16[128,128]{1,0:T(8,128)(2,1)}, u32[]{:S(2)}) copy-start(bf16[128,128]{1,0:T(8,128)(2,1)} %param.12) | copy-start | bytes 98308
  91.0 2.3 copy-start.21
  93.3 5.9 %copy-start.4 = (bf16[10,128,128]{2,1,0:T(8,128)(2,1)}, bf16[10,128,128]{2,1,0:T(8,128)(2,1)S(1)}, u32[]{:S(2)}) copy-start(bf16[10,128,128]{2,1,0:T(8,128)(2,1)S(1)} %get-tuple-element.37) | copy-start | bytes 983044
  179.8 1.0 copy-start.6
  179.8 1.0 copy-start.8
  180.8 1.5 copy-start
  182.0 0.9 copy-start.3
  195.7 13.5 %slice-start = ((bf16[1280,256]{0,1:T(8,128)(2,1)}), bf16[512,256]{0,1:T(8,128)(2,1)S(1)}, s32[]{:S(2)}) async-start(bf16[1280,256]{0,1:T(8,128)(2,1)} %copy-done.3), calls=%async_computation.2 | async-start | bytes 524288 | tf_op jit(solution)/shard_map/slice | solution.py:105
  195.7 16.5 %slice-start.1 = ((bf16[1280,256]{0,1:T(8,128)(2,1)}), bf16[256,256]{0,1:T(8,128)(2,1)S(1)}, s32[]{:S(2)}) async-start(bf16[1280,256]{0,1:T(8,128)(2,1)} %copy-done.3), calls=%async_computation.3 | async-start | bytes 262144 | tf_op jit(solution)/shard_map/slice | solution.py:103
  195.7 20.4 %copy-start.1 = (bf16[8,128,1280]{1,2,0:T(8,128)(2,1)S(1)}, bf16[8,128,1280]{1,2,0:T(8,128)(2,1)}, u32[]{:S(2)}) copy-start(bf16[8,128,1280]{1,2,0:T(8,128)(2,1)} %copy-done) | copy-start | bytes 7864324
  202.8 26.4 %collective-permute-start.10 = (bf16[128,32,32]{0,2,1:T(8,128)(2,1)}, bf16[128,32,32]{0,2,1:T(8,128)(2,1)}, u32[]{:S(2)}, u32[]{:S(2)}) collective-permute-start(bf16[128,32,32]{0,2,1:T(8,128)(2,1)} %get-tuple-element.29), channel_id=1, source_target_pairs={{0,7},{1,0},{2,1},{3,2},{4,3},{5,4},{6,5},{7,6},{8,15},{9,8},{10,9... | collective-permute-start | bytes 786440 | tf_op jit(solution)/shard_map/ppermute | solution.py:184
  205.6 26.4 %collective-permute-start.9 = (bf16[128,32,32]{0,2,1:T(8,128)(2,1)}, bf16[128,32,32]{0,2,1:T(8,128)(2,1)}, u32[]{:S(2)}, u32[]{:S(2)}) collective-permute-start(bf16[128,32,32]{0,2,1:T(8,128)(2,1)} %get-tuple-element.30), channel_id=1, source_target_pairs={{0,6},{1,7},{2,0},{3,1},{4,2},{5,3},{6,4},{7,5},{8,14},{9,15},{10,... | collective-permute-start | bytes 786440 | tf_op jit(solution)/shard_map/ppermute | solution.py:184
  206.4 31.5 %collective-permute-start.8 = (bf16[128,32,32]{0,2,1:T(8,128)(2,1)}, bf16[128,32,32]{0,2,1:T(8,128)(2,1)}, u32[]{:S(2)}, u32[]{:S(2)}) collective-permute-start(bf16[128,32,32]{0,2,1:T(8,128)(2,1)} %get-tuple-element.31), channel_id=1, source_target_pairs={{0,5},{1,6},{2,7},{3,0},{4,1},{5,2},{6,3},{7,4},{8,13},{9,14},{10,... | collective-permute-start | bytes 786440 | tf_op jit(solution)/shard_map/ppermute | solution.py:184
  209.2 12.8 %copy-start.2 = (f32[512,256]{1,0:T(8,128)S(1)}, f32[512,256]{1,0:T(8,128)}, u32[]{:S(2)}) copy-start(f32[512,256]{1,0:T(8,128)} %copy.126) | copy-start | bytes 1572868
  210.0 15.4 %copy-start.10 = (f32[128,64]{1,0:T(8,128)S(1)}, f32[128,64]{1,0:T(8,128)}, u32[]{:S(2)}) copy-start(f32[128,64]{1,0:T(8,128)} %copy-done.9) | copy-start | bytes 98308
  210.0 12.0 %collective-permute-start.18 = (bf16[4,128,256]{2,1,0:T(8,128)(2,1)}, bf16[4,128,256]{2,1,0:T(8,128)(2,1)}, u32[]{:S(2)}, u32[]{:S(2)}) collective-permute-start(bf16[4,128,256]{2,1,0:T(8,128)(2,1)} %bitcast.157), channel_id=1, source_target_pairs={{32,0},{40,8},{48,16},{56,24},{64,32},{72,40},{80,48},{88,56},{96,... | collective-permute-start | bytes 786440 | tf_op jit(solution)/shard_map/ppermute | solution.py:30
  212.9 12.5 %copy-start.12 = (f32[128,64]{1,0:T(8,128)S(1)}, f32[128,64]{1,0:T(8,128)}, u32[]{:S(2)}) copy-start(f32[128,64]{1,0:T(8,128)} %get-tuple-element.47) | copy-start | bytes 98308
  212.9 22.8 %copy-start.11 = (bf16[128,32,32]{0,2,1:T(8,128)(2,1)S(1)}, bf16[128,32,32]{0,2,1:T(8,128)(2,1)}, u32[]{:S(2)}) copy-start(bf16[128,32,32]{0,2,1:T(8,128)(2,1)} %get-tuple-element.28) | copy-start | bytes 786436
  212.9 15.7 %collective-permute-start.20 = (bf16[2,128,256]{2,1,0:T(8,128)(2,1)}, bf16[2,128,256]{2,1,0:T(8,128)(2,1)S(1)}, u32[]{:S(2)}, u32[]{:S(2)}) collective-permute-start(bf16[2,128,256]{2,1,0:T(8,128)(2,1)} %bitcast.158), channel_id=1, source_target_pairs={{64,0},{72,8},{80,16},{88,24},{96,32},{104,40},{112,48},{120,56},{... | collective-permute-start | bytes 393224 | tf_op jit(solution)/shard_map/ppermute | solution.py:30
  223.0 35.7 %copy-start.16 = (pred[64]{0:T(512)(128)(4,1)S(1)}, pred[64]{0:T(512)(128)(4,1)}, u32[]{:S(2)}) copy-start(pred[64]{0:T(512)(128)(4,1)} %copy-done.15) | copy-start | bytes 196
  223.0 35.6 %copy-start.18 = (pred[64]{0:T(512)(128)(4,1)S(1)}, pred[64]{0:T(512)(128)(4,1)}, u32[]{:S(2)}) copy-start(pred[64]{0:T(512)(128)(4,1)} %copy-done.17) | copy-start | bytes 196
  223.0 35.6 %copy-start.20 = (pred[64]{0:T(512)(128)(4,1)S(1)}, pred[64]{0:T(512)(128)(4,1)}, u32[]{:S(2)}) copy-start(pred[64]{0:T(512)(128)(4,1)} %copy-done.19) | copy-start | bytes 196
  223.0 12.7 %collective-permute-start.19 = (bf16[2,128,256]{2,1,0:T(8,128)(2,1)S(1)}, bf16[2,128,256]{2,1,0:T(8,128)(2,1)S(1)}, u32[]{:S(2)}, u32[]{:S(2)}) collective-permute-start(bf16[2,128,256]{2,1,0:T(8,128)(2,1)S(1)} %slice.194), channel_id=1, source_target_pairs={{16,0},{24,8},{32,16},{40,24},{48,32},{56,40},{64,48},{72,56},{80,... | collective-permute-start | bytes 393224 | tf_op jit(solution)/shard_map/ppermute | solution.py:30
  228.6 7.1 %copy-start.13 = (bf16[2,128,256]{2,1,0:T(8,128)(2,1)}, bf16[2,128,256]{2,1,0:T(8,128)(2,1)S(1)}, u32[]{:S(2)}) copy-start(bf16[2,128,256]{2,1,0:T(8,128)(2,1)S(1)} %collective-permute-done.20) | copy-start | bytes 393220
  228.6 11.4 %collective-permute-start.7 = (bf16[128,32,32]{0,2,1:T(8,128)(2,1)}, bf16[128,32,32]{0,2,1:T(8,128)(2,1)S(1)}, u32[]{:S(2)}, u32[]{:S(2)}) collective-permute-start(bf16[128,32,32]{0,2,1:T(8,128)(2,1)} %get-tuple-element.32), channel_id=1, source_target_pairs={{0,4},{1,5},{2,6},{3,7},{4,0},{5,1},{6,2},{7,3},{8,12},{9,13},{10,... | collective-permute-start | bytes 786440 | tf_op jit(solution)/shard_map/ppermute | solution.py:184
  229.2 14.3 %collective-permute-start.6 = (bf16[128,32,32]{0,2,1:T(8,128)(2,1)}, bf16[128,32,32]{0,2,1:T(8,128)(2,1)S(1)}, u32[]{:S(2)}, u32[]{:S(2)}) collective-permute-start(bf16[128,32,32]{0,2,1:T(8,128)(2,1)} %get-tuple-element.33), channel_id=1, source_target_pairs={{0,3},{1,4},{2,5},{3,6},{4,7},{5,0},{6,1},{7,2},{8,11},{9,12},{10,... | collective-permute-start | bytes 786440 | tf_op jit(solution)/shard_map/ppermute | solution.py:184
  231.9 19.4 %collective-permute-start.5 = (bf16[128,32,32]{0,2,1:T(8,128)(2,1)}, bf16[128,32,32]{0,2,1:T(8,128)(2,1)S(1)}, u32[]{:S(2)}, u32[]{:S(2)}) collective-permute-start(bf16[128,32,32]{0,2,1:T(8,128)(2,1)} %get-tuple-element.34), channel_id=1, source_target_pairs={{0,2},{1,3},{2,4},{3,5},{4,6},{5,7},{6,0},{7,1},{8,10},{9,11},{10,... | collective-permute-start | bytes 786440 | tf_op jit(solution)/shard_map/ppermute | solution.py:184
  235.8 19.9 %collective-permute-start.4 = (bf16[128,32,32]{0,2,1:T(8,128)(2,1)S(1)}, bf16[128,32,32]{0,2,1:T(8,128)(2,1)S(1)}, u32[]{:S(2)}, u32[]{:S(2)}) collective-permute-start(bf16[128,32,32]{0,2,1:T(8,128)(2,1)S(1)} %copy-done.11), channel_id=1, source_target_pairs={{0,1},{1,2},{2,3},{3,4},{4,5},{5,6},{6,7},{7,0},{8,9},{9,10},{10,1... | collective-permute-start | bytes 786440 | tf_op jit(solution)/shard_map/ppermute | solution.py:184
  237.9 20.1 %collective-permute-start.21 = (bf16[1,128,256]{2,1,0:T(8,128)(2,1)S(1)}, bf16[1,128,256]{2,1,0:T(8,128)(2,1)S(1)}, u32[]{:S(2)}, u32[]{:S(2)}) collective-permute-start(bf16[1,128,256]{2,1,0:T(8,128)(2,1)S(1)} %slice.195), channel_id=1, source_target_pairs={{8,0},{16,8},{24,16},{32,24},{40,32},{48,40},{56,48},{64,56},{72,6... | collective-permute-start | bytes 196616 | tf_op jit(solution)/shard_map/ppermute | solution.py:30
Sparse Core Ops, SparseCore 0:
  23.8 145.4 all-gather.1
where the time goes:
time: 268 us; the launch traced here: 267 us
  waiting for transfers between devices  104 us (39%)
  starting transfers between devices  52.2 us (19%)
  local copies, waits for them, and re-layouts  33.3 us (12%)
  matrix products  31.3 us (12%)
  other arithmetic  15.8 us (6%)
  blocking collectives  15.4 us (6%)
  between operations  14.8 us (6%)
    all_gather x1, waiting for transfers between devices, per_device(): stripes = lax.all_gather(pieces, SEQ, axis=1, tiled=True)  66.9 us
    ppermute x8, starting transfers between devices, shifted(): return lax.ppermute(block, SEQ, route)  35.4 us
    ppermute x8, waiting for transfers between devices, shifted(): return lax.ppermute(block, SEQ, route)  16.6 us
    unnamed x71, local copies, waits for them, and re-layouts  16.3 us
    ppermute x7, waiting for transfers between devices, per_device(): lax.ppermute(piece, 'kv', [(i, (i + j) % kv_count) for i in range(kv_coun...  15.8 us
    all_to_all x1, blocking collectives, per_device(): lax.all_to_all(out_weight, 'kv', split_axis=0, concat_axis=1, tiled=True)  15.4 us
    dot_general x1, matrix products, per_device(): jnp.dot(attn, stripes, preferred_element_type=jnp.float32)  12.8 us
    ppermute x7, starting transfers between devices, per_device(): lax.ppermute(piece, 'kv', [(i, (i + j) % kv_count) for i in range(kv_coun...  10.7 us
  transfers between devices with their start and end apart: 23, of which 14 were waited for; matrix products, arithmetic and copies ran while one was open for 17% of the time, Pallas kernels for 0%

commit v1 on v0

--- a/solution.py
+++ b/solution.py
@@ -175,16 +175,21 @@
     dkey_sum = jnp.einsum("htu,thd->ud", dscore, q_grp, preferred_element_type=jnp.float32) * scale
     dvalue_sum = jnp.einsum("htu,thd->ud", weights, g_grp, preferred_element_type=jnp.float32)
     attn = out_grp.reshape(length, per_group * HD)
-    lo_part = jnp.dot(attn, stripes, preferred_element_type=jnp.float32).astype(jnp.bfloat16)
-    lo_part = lo_part.reshape(length, n_seq, kv_count, col_w)
-    total = lax.dynamic_index_in_dim(lo_part, kv_me, 2, keepdims=False).astype(jnp.float32)
+    dkv = jnp.concatenate([dkey_sum, dvalue_sum], axis=1).reshape(REACH + 1, length, 2 * HD)
+    attn, dkv = lax.optimization_barrier((attn, dkv))
+    lo_part = jnp.einsum(
+        "tr,rskj->ktsj",
+        attn,
+        stripes.reshape(attn.shape[1], n_seq, kv_count, col_w),
+        preferred_element_type=jnp.float32,
+    ).astype(jnp.bfloat16)
+    total = lax.dynamic_index_in_dim(lo_part, kv_me, 0, keepdims=False).astype(jnp.float32)
     for j in range(1, kv_count):
         dest = (kv_me + j) % kv_count
-        piece = lax.dynamic_index_in_dim(lo_part, dest, 2, keepdims=False)
+        piece = lax.dynamic_index_in_dim(lo_part, dest, 0, keepdims=False)
         got = lax.ppermute(piece, "kv", [(i, (i + j) % kv_count) for i in range(kv_count)])
         total = total + got.astype(jnp.float32)
     layer_out = total.reshape(length, n_seq * col_w).astype(jnp.bfloat16)
-    dkv = jnp.concatenate([dkey_sum, dvalue_sum], axis=1).reshape(REACH + 1, length, 2 * HD)
     dkv_total = return_window(dkv)
     dk_total = dkv_total[:, :HD]
     dv_total = dkv_total[:, HD:]

time: 268 us -> 252 us (0.940)
  the two profiles are of different devices: /device:TPU:64 before, /device:TPU:97 now
where the time goes in v1:
time: 252 us; the launch traced here: 250 us
  waiting for transfers between devices  93.7 us (37%)
  starting transfers between devices  58 us (23%)
  local copies, waits for them, and re-layouts  26.5 us (11%)
  matrix products  26.5 us (11%)
  other arithmetic  16.9 us (7%)
  between operations  14.8 us (6%)
  blocking collectives  13.7 us (5%)
    all_gather x1, waiting for transfers between devices, per_device(): stripes = lax.all_gather(pieces, SEQ, axis=1, tiled=True)  71.7 us
    ppermute x8, starting transfers between devices, shifted(): return lax.ppermute(block, SEQ, route)  32.4 us
    ppermute x7, starting transfers between devices, per_device(): lax.ppermute(piece, 'kv', [(i, (i + j) % kv_count) for i in range(kv_coun...  20.8 us
    ppermute x8, waiting for transfers between devices, shifted(): return lax.ppermute(block, SEQ, route)  17.7 us
    unnamed x65, local copies, waits for them, and re-layouts  16.8 us
    all_to_all x1, blocking collectives, per_device(): lax.all_to_all(out_weight, 'kv', split_axis=0, concat_axis=1, tiled=True)  13.7 us
    dot_general x1, matrix products, per_device(): lax.dot_general(og_perm, stripes, contract, preferred_element_type=jnp.fl...  8.76 us
    unnamed x1, matrix products  8.26 us
  transfers between devices with their start and end apart: 23, of which 8 were waited for; matrix products, arithmetic and copies ran while one was open for 20% of the time, Pallas kernels for 0%

profile of v1, /device:TPU:97, one launch (start us, length us, event | category | flops | bytes accessed | tf_op | source)
XLA Modules:
  0.0 250.0 jit_solution(17131883260783320780)
XLA Ops:
  7.2 1.1 copy.127
  8.3 13.7 %all_to_all.19 = bf16[8,1024,32]{1,2,0:T(8,128)(2,1)} all-to-all(bf16[8,1024,32]{1,2,0:T(8,128)(2,1)S(1)} %bitcast.137), channel_id=1, replica_groups=mesh['sz'=16,'core'=2,'kv'=8] {'kv'}, dimensions={0} | all-to-all | bytes 1048576 | tf_op jit(solution)/shard_map/all_to_all | solution.py:133
  22.0 1.1 copy.88
  23.1 1.9 collective-permute-start.4
  25.0 1.2 collective-permute-start.5
  27.6 1.3 fusion.32
  30.9 6.8 %collective-permute-start = (bf16[1,129,256]{2,1,0:T(8,128)(2,1)S(1)}, bf16[1,129,256]{2,1,0:T(8,128)(2,1)S(1)}, u32[]{:S(2)}, u32[]{:S(2)}) collective-permute-start(bf16[1,129,256]{2,1,0:T(8,128)(2,1)S(1)} %fusion.17), channel_id=1, source_target_pairs={{0,8},{8,16},{16,24},{24,32},{32,40},{40,48},{48,56},{56,64},{64,7... | collective-permute-start | bytes 198152 | tf_op jit(solution)/shard_map/ppermute | solution.py:30
  37.8 1.1 copy.83
  40.2 1.0 broadcast_multiply_fusion
  41.4 9.2 %collective-permute-done = bf16[1,129,256]{2,1,0:T(8,128)(2,1)S(1)} collective-permute-done((bf16[1,129,256]{2,1,0:T(8,128)(2,1)S(1)}, bf16[1,129,256]{2,1,0:T(8,128)(2,1)S(1)}, u32[]{:S(2)}, u32[]{:S(2)}) %collective-permute-start) | collective-permute-done | bytes 66080 | tf_op jit(solution)/shard_map/ppermute | solution.py:30
  50.6 1.9 collective-permute-start.2
  52.6 5.2 %collective-permute-start.1 = (bf16[2,129,256]{2,1,0:T(8,128)(2,1)S(1)}, bf16[2,129,256]{2,1,0:T(8,128)(2,1)S(1)}, u32[]{:S(2)}, u32[]{:S(2)}) collective-permute-start(bf16[2,129,256]{2,1,0:T(8,128)(2,1)S(1)} %pad_maximum_fusion.4), channel_id=1, source_target_pairs={{0,64},{8,72},{16,80},{24,88},{32,96},{40,104},{48,112},{56,120},{... | collective-permute-start | bytes 396296 | tf_op jit(solution)/shard_map/ppermute | solution.py:30
  57.9 5.3 %collective-permute-done.2 = bf16[2,129,256]{2,1,0:T(8,128)(2,1)S(1)} collective-permute-done((bf16[2,129,256]{2,1,0:T(8,128)(2,1)S(1)}, bf16[2,129,256]{2,1,0:T(8,128)(2,1)S(1)}, u32[]{:S(2)}, u32[]{:S(2)}) %collective-permute-start.2) | collective-permute-done | bytes 132128 | tf_op jit(solution)/shard_map/ppermute | solution.py:30
  63.2 1.1 collective-permute-done.1
  65.2 1.6 collective-permute-start.10
  67.6 6.1 %collective-permute-start.3 = (bf16[4,129,256]{2,1,0:T(8,128)(2,1)S(1)}, bf16[4,129,256]{2,1,0:T(8,128)(2,1)S(1)}, u32[]{:S(2)}, u32[]{:S(2)}) collective-permute-start(bf16[4,129,256]{2,1,0:T(8,128)(2,1)S(1)} %pad_maximum_fusion.1), channel_id=1, source_target_pairs={{0,32},{8,40},{16,48},{24,56},{32,64},{40,72},{48,80},{56,88},{64,... | collective-permute-start | bytes 792584 | tf_op jit(solution)/shard_map/ppermute | solution.py:30
  76.6 2.1 collective-permute-done.10
  85.3 2.0 constant_dynamic-slice_fusion
  87.3 1.9 copy.96
  89.7 1.4 or_and_fusion
  91.1 4.2 %exponential_reduce_fusion = (f32[8,128]{1,0:T(8,128)S(1)}, f32[8,128,1280]{1,2,0:T(8,128)}) fusion(bf16[1280,128,1]{1,0,2:T(8,128)(2,1)S(1)} %bitcast.138, pred[128,1280]{0,1:T(8,128)(4,1)S(1)} %or_and_fusion, bf16[128,8,64]{2,0,1:T(8,128)(2,1)S(1)} %get-tuple-element.44, bf16[128,8,64]{2,0,1:T(8,128)(2,1)S(1)} %get-tuple-element.43), kind=kOutput, calls=%fused_computation.7 | convolution fusion | flops 341312768 | bytes 6000640 | tf_op jit(solution)/shard_map/sub | solution.py:166
  95.3 3.2 %divide_convert_fusion = bf16[8,128,1280]{1,2,0:T(8,128)(2,1)S(1)} fusion(f32[8,128,1280]{1,2,0:T(8,128)} %get-tuple-element.62, f32[8,128]{1,0:T(8,128)S(1)} %get-tuple-element.61), kind=kLoop, calls=%fused_computation.6 | loop fusion | flops 2621440 | bytes 7868416 | tf_op jit(solution)/shard_map/convert_element_type | solution.py:167
  98.5 71.7 %all-gather.2.cloned.1.call-done = bf16[1024,8192]{0,1:T(8,128)(2,1)} async-done(((bf16[1024,256]{0,1:T(8,128)(2,1)}), bf16[1024,8192]{0,1:T(8,128)(2,1)}) %all-gather.2.cloned.1.call-update) | async-done | bytes 16777232 | tf_op jit(solution)/shard_map/all_gather | solution.py:134
  170.2 8.8 %convolution_convert_fusion.1 = bf16[128,1024]{1,0:T(8,128)(2,1)S(1)} fusion(bf16[128,8192]{0,1:T(8,128)(2,1)} %bitcast.126, bf16[1024,8192]{0,1:T(8,128)(2,1)} %all-gather.2.cloned.1.call-done), kind=kOutput, calls=%fused_computation.15 | convolution fusion | flops 2147614720 | bytes 19136512 | tf_op jit(solution)/shard_map/dot_general | solution.py:142
  179.2 1.3 multiply_reduce_fusion
  180.4 1.0 convolution_bitcast_fusion
  182.3 1.5 copy-done
  183.7 1.1 fusion.4
  185.5 1.9 collective-permute-start.18
  187.4 3.0 %collective-permute-start.20 = (bf16[2,128,256]{2,1,0:T(8,128)(2,1)S(1)}, bf16[2,128,256]{2,1,0:T(8,128)(2,1)S(1)}, u32[]{:S(2)}, u32[]{:S(2)}) collective-permute-start(bf16[2,128,256]{2,1,0:T(8,128)(2,1)S(1)} %slice.128), channel_id=1, source_target_pairs={{64,0},{72,8},{80,16},{88,24},{96,32},{104,40},{112,48},{120,56},{... | collective-permute-start | bytes 393224 | tf_op jit(solution)/shard_map/ppermute | solution.py:30
  190.4 8.3 %fusion.38 = f32[128,8192]{0,1:S(1)} fusion(bf16[1024,8192]{0,1:T(8,128)(2,1)} %all-gather.2.cloned.1.call-done, bf16[128,1024]{0,1:T(8,128)(2,1)S(1)} %bitcast.140), kind=kOutput, calls=%fused_computation.134 | convolution fusion | flops 2147483648 | bytes 21233664
  199.3 1.2 dynamic-slice_bitcast_fusion.6
  200.5 1.2 collective-permute-start.11
  201.7 2.4 collective-permute-start.12
  204.1 1.2 collective-permute-start.13
  205.3 1.1 fusion.5
  206.4 0.9 convert_add_fusion.1
  207.3 1.0 slice.180
  208.3 2.8 %collective-permute-start.19 = (bf16[2,128,256]{2,1,0:T(8,128)(2,1)S(1)}, bf16[2,128,256]{2,1,0:T(8,128)(2,1)S(1)}, u32[]{:S(2)}, u32[]{:S(2)}) collective-permute-start(bf16[2,128,256]{2,1,0:T(8,128)(2,1)S(1)} %slice.180), channel_id=1, source_target_pairs={{16,0},{24,8},{32,16},{40,24},{48,32},{56,40},{64,48},{72,56},{80,... | collective-permute-start | bytes 393224 | tf_op jit(solution)/shard_map/ppermute | solution.py:30
  212.9 1.2 collective-permute-done.12
  214.2 2.3 collective-permute-start.16
  216.5 12.9 %collective-permute-start.17 = (bf16[128,32,32]{0,2,1:T(8,128)(2,1)}, bf16[128,32,32]{0,2,1:T(8,128)(2,1)}, u32[]{:S(2)}, u32[]{:S(2)}) collective-permute-start(bf16[128,32,32]{0,2,1:T(8,128)(2,1)} %get-tuple-element.37), channel_id=1, source_target_pairs={{0,7},{1,0},{2,1},{3,2},{4,3},{5,4},{6,5},{7,6},{8,15},{9,8},{10,9... | collective-permute-start | bytes 786440 | tf_op jit(solution)/shard_map/ppermute | solution.py:190
  229.8 0.9 copy.110
  230.6 1.1 fusion.13
  231.8 4.5 %collective-permute-start.21 = (bf16[1,128,256]{2,1,0:T(8,128)(2,1)S(1)}, bf16[1,128,256]{2,1,0:T(8,128)(2,1)S(1)}, u32[]{:S(2)}, u32[]{:S(2)}) collective-permute-start(bf16[1,128,256]{2,1,0:T(8,128)(2,1)S(1)} %slice.181), channel_id=1, source_target_pairs={{8,0},{16,8},{24,16},{32,24},{40,32},{48,40},{56,48},{64,56},{72,6... | collective-permute-start | bytes 196616 | tf_op jit(solution)/shard_map/ppermute | solution.py:30
  236.3 1.5 fusion.12
  238.7 2.1 collective-permute-done.21
  241.4 1.0 fusion.25
  (123 shorter events, 22.9 us)
Async XLA Ops:
  7.2 32.2 %copy-start.19 = (s32[1,32]{1,0:T(1,128)S(1)}, s32[1,32]{1,0:T(1,128)}, u32[]{:S(2)}) copy-start(s32[1,32]{1,0:T(1,128)} %param.16) | copy-start | bytes 388
  7.2 163.0 %all-gather.2.cloned.1.call-start = ((), (), s32[]{:S(2)}) async-start(), calls=%async_computation.1 | async-start | bytes 17301504 | tf_op jit(solution)/shard_map/all_gather | solution.py:134
  23.1 41.3 %collective-permute-start.4 = (bf16[128,1024]{0,1:T(8,128)(2,1)S(1)}, bf16[128,1024]{0,1:T(8,128)(2,1)S(1)}, u32[]{:S(2)}, u32[]{:S(2)}) collective-permute-start(bf16[128,1024]{0,1:T(8,128)(2,1)S(1)} %copy.88), channel_id=1, source_target_pairs={{0,7},{1,0},{2,1},{3,2},{4,3},{5,4},{6,5},{7,6},{8,15},{9,8},{10,9... | collective-permute-start | bytes 786440 | tf_op jit(solution)/shard_map/ppermute | solution.py:137
  25.0 40.3 %collective-permute-start.5 = (bf16[128,1024]{0,1:T(8,128)(2,1)S(1)}, bf16[128,1024]{0,1:T(8,128)(2,1)S(1)}, u32[]{:S(2)}, u32[]{:S(2)}) collective-permute-start(bf16[128,1024]{0,1:T(8,128)(2,1)S(1)} %copy.88), channel_id=1, source_target_pairs={{0,6},{1,7},{2,0},{3,1},{4,2},{5,3},{6,4},{7,5},{8,14},{9,15},{10,... | collective-permute-start | bytes 786440 | tf_op jit(solution)/shard_map/ppermute | solution.py:137
  26.2 41.4 %collective-permute-start.6 = (bf16[128,1024]{0,1:T(8,128)(2,1)S(1)}, bf16[128,1024]{0,1:T(8,128)(2,1)S(1)}, u32[]{:S(2)}, u32[]{:S(2)}) collective-permute-start(bf16[128,1024]{0,1:T(8,128)(2,1)S(1)} %copy.88), channel_id=1, source_target_pairs={{0,5},{1,6},{2,7},{3,0},{4,1},{5,2},{6,3},{7,4},{8,13},{9,14},{10,... | collective-permute-start | bytes 786440 | tf_op jit(solution)/shard_map/ppermute | solution.py:137
  27.5 23.1 %copy-start.15 = (f32[64]{0:T(128)}, f32[64]{0:T(128)S(1)}, u32[]{:S(2)}) copy-start(f32[64]{0:T(128)S(1)} %multiply_exponential_fusion) | copy-start | bytes 772
  27.6 40.0 %copy-start.16 = (pred[64]{0:T(512)(128)(4,1)}, pred[64]{0:T(512)(128)(4,1)S(1)}, u32[]{:S(2)}) copy-start(pred[64]{0:T(512)(128)(4,1)S(1)} %get-tuple-element.65) | copy-start | bytes 196
  27.6 40.0 %copy-start.17 = (pred[64]{0:T(512)(128)(4,1)}, pred[64]{0:T(512)(128)(4,1)S(1)}, u32[]{:S(2)}) copy-start(pred[64]{0:T(512)(128)(4,1)S(1)} %get-tuple-element.66) | copy-start | bytes 196
  30.9 19.7 %collective-permute-start = (bf16[1,129,256]{2,1,0:T(8,128)(2,1)S(1)}, bf16[1,129,256]{2,1,0:T(8,128)(2,1)S(1)}, u32[]{:S(2)}, u32[]{:S(2)}) collective-permute-start(bf16[1,129,256]{2,1,0:T(8,128)(2,1)S(1)} %fusion.17), channel_id=1, source_target_pairs={{0,8},{8,16},{16,24},{24,32},{32,40},{40,48},{48,56},{56,64},{64,7... | collective-permute-start | bytes 198152 | tf_op jit(solution)/shard_map/ppermute | solution.py:30
  41.4 49.7 %copy-start.5 = (bf16[128,8,64]{2,0,1:T(8,128)(2,1)}, bf16[128,8,64]{2,0,1:T(8,128)(2,1)S(1)}, u32[]{:S(2)}) copy-start(bf16[128,8,64]{2,0,1:T(8,128)(2,1)S(1)} %get-tuple-element.43) | copy-start | bytes 393220
  41.4 49.7 %copy-start.7 = (bf16[128,8,64]{2,0,1:T(8,128)(2,1)}, bf16[128,8,64]{2,0,1:T(8,128)(2,1)S(1)}, u32[]{:S(2)}) copy-start(bf16[128,8,64]{2,0,1:T(8,128)(2,1)S(1)} %get-tuple-element.44) | copy-start | bytes 393220
  50.6 12.6 %collective-permute-start.2 = (bf16[2,129,256]{2,1,0:T(8,128)(2,1)S(1)}, bf16[2,129,256]{2,1,0:T(8,128)(2,1)S(1)}, u32[]{:S(2)}, u32[]{:S(2)}) collective-permute-start(bf16[2,129,256]{2,1,0:T(8,128)(2,1)S(1)} %pad_maximum_fusion.4), channel_id=1, source_target_pairs={{0,16},{8,24},{16,32},{24,40},{32,48},{40,56},{48,64},{56,72},{64,... | collective-permute-start | bytes 396296 | tf_op jit(solution)/shard_map/ppermute | solution.py:30
  52.6 11.8 %collective-permute-start.1 = (bf16[2,129,256]{2,1,0:T(8,128)(2,1)S(1)}, bf16[2,129,256]{2,1,0:T(8,128)(2,1)S(1)}, u32[]{:S(2)}, u32[]{:S(2)}) collective-permute-start(bf16[2,129,256]{2,1,0:T(8,128)(2,1)S(1)} %pad_maximum_fusion.4), channel_id=1, source_target_pairs={{0,64},{8,72},{16,80},{24,88},{32,96},{40,104},{48,112},{56,120},{... | collective-permute-start | bytes 396296 | tf_op jit(solution)/shard_map/ppermute | solution.py:30
  63.2 11.2 %collective-permute-start.7 = (bf16[128,1024]{0,1:T(8,128)(2,1)S(1)}, bf16[128,1024]{0,1:T(8,128)(2,1)S(1)}, u32[]{:S(2)}, u32[]{:S(2)}) collective-permute-start(bf16[128,1024]{0,1:T(8,128)(2,1)S(1)} %copy.88), channel_id=1, source_target_pairs={{0,4},{1,5},{2,6},{3,7},{4,0},{5,1},{6,2},{7,3},{8,12},{9,13},{10,... | collective-permute-start | bytes 786440 | tf_op jit(solution)/shard_map/ppermute | solution.py:137
  64.4 10.8 %collective-permute-start.8 = (bf16[128,1024]{0,1:T(8,128)(2,1)S(1)}, bf16[128,1024]{0,1:T(8,128)(2,1)S(1)}, u32[]{:S(2)}, u32[]{:S(2)}) collective-permute-start(bf16[128,1024]{0,1:T(8,128)(2,1)S(1)} %copy.88), channel_id=1, source_target_pairs={{0,3},{1,4},{2,5},{3,6},{4,7},{5,0},{6,1},{7,2},{8,11},{9,12},{10,... | collective-permute-start | bytes 786440 | tf_op jit(solution)/shard_map/ppermute | solution.py:137
  64.4 11.5 %collective-permute-start.9 = (bf16[128,1024]{0,1:T(8,128)(2,1)S(1)}, bf16[128,1024]{0,1:T(8,128)(2,1)S(1)}, u32[]{:S(2)}, u32[]{:S(2)}) collective-permute-start(bf16[128,1024]{0,1:T(8,128)(2,1)S(1)} %copy.88), channel_id=1, source_target_pairs={{0,2},{1,3},{2,4},{3,5},{4,6},{5,7},{6,0},{7,1},{8,10},{9,11},{10,... | collective-permute-start | bytes 786440 | tf_op jit(solution)/shard_map/ppermute | solution.py:137
  65.2 13.5 %collective-permute-start.10 = (bf16[128,1024]{0,1:T(8,128)(2,1)S(1)}, bf16[128,1024]{0,1:T(8,128)(2,1)S(1)}, u32[]{:S(2)}, u32[]{:S(2)}) collective-permute-start(bf16[128,1024]{0,1:T(8,128)(2,1)S(1)} %copy.88), channel_id=1, source_target_pairs={{0,1},{1,2},{2,3},{3,4},{4,5},{5,6},{6,7},{7,0},{8,9},{9,10},{10,1... | collective-permute-start | bytes 786440 | tf_op jit(solution)/shard_map/ppermute | solution.py:137
  67.6 21.7 %collective-permute-start.3 = (bf16[4,129,256]{2,1,0:T(8,128)(2,1)S(1)}, bf16[4,129,256]{2,1,0:T(8,128)(2,1)S(1)}, u32[]{:S(2)}, u32[]{:S(2)}) collective-permute-start(bf16[4,129,256]{2,1,0:T(8,128)(2,1)S(1)} %pad_maximum_fusion.1), channel_id=1, source_target_pairs={{0,32},{8,40},{16,48},{24,56},{32,64},{40,72},{48,80},{56,88},{64,... | collective-permute-start | bytes 792584 | tf_op jit(solution)/shard_map/ppermute | solution.py:30
  85.3 4.1 %copy-start.14 = (bf16[128,128]{1,0:T(8,128)(2,1)S(1)}, bf16[128,128]{1,0:T(8,128)(2,1)}, u32[]{:S(2)}) copy-start(bf16[128,128]{1,0:T(8,128)(2,1)} %param.12) | copy-start | bytes 98308
  87.3 2.3 copy-start.18
  89.7 5.7 %copy-start.2 = (bf16[10,128,128]{2,1,0:T(8,128)(2,1)}, bf16[10,128,128]{2,1,0:T(8,128)(2,1)S(1)}, u32[]{:S(2)}) copy-start(bf16[10,128,128]{2,1,0:T(8,128)(2,1)S(1)} %get-tuple-element.45) | copy-start | bytes 983044
  181.4 2.3 copy-start.6
  181.4 2.3 copy-start.8
  182.3 1.5 copy-start
  184.8 5.6 %copy-start.4 = (bf16[128,8,128]{2,0,1:T(8,128)(2,1)S(1)}, bf16[128,8,128]{2,0,1:T(8,128)(2,1)}, u32[]{:S(2)}) copy-start(bf16[128,8,128]{2,0,1:T(8,128)(2,1)} %get-tuple-element.64) | copy-start | bytes 786436
  185.5 21.0 %collective-permute-start.18 = (bf16[4,128,256]{2,1,0:T(8,128)(2,1)S(1)}, bf16[4,128,256]{2,1,0:T(8,128)(2,1)S(1)}, u32[]{:S(2)}, u32[]{:S(2)}) collective-permute-start(bf16[4,128,256]{2,1,0:T(8,128)(2,1)S(1)} %slice.125), channel_id=1, source_target_pairs={{32,0},{40,8},{48,16},{56,24},{64,32},{72,40},{80,48},{88,56},{96,... | collective-permute-start | bytes 786440 | tf_op jit(solution)/shard_map/ppermute | solution.py:30
  187.4 24.0 %collective-permute-start.20 = (bf16[2,128,256]{2,1,0:T(8,128)(2,1)S(1)}, bf16[2,128,256]{2,1,0:T(8,128)(2,1)S(1)}, u32[]{:S(2)}, u32[]{:S(2)}) collective-permute-start(bf16[2,128,256]{2,1,0:T(8,128)(2,1)S(1)} %slice.128), channel_id=1, source_target_pairs={{64,0},{72,8},{80,16},{88,24},{96,32},{104,40},{112,48},{120,56},{... | collective-permute-start | bytes 393224 | tf_op jit(solution)/shard_map/ppermute | solution.py:30
  198.7 6.6 %copy-start.1 = (bf16[8,128,1280]{1,2,0:T(8,128)(2,1)S(1)}, bf16[8,128,1280]{1,2,0:T(8,128)(2,1)}, u32[]{:S(2)}) copy-start(bf16[8,128,1280]{1,2,0:T(8,128)(2,1)} %copy-done) | copy-start | bytes 7864324
  198.7 6.6 %copy-start.3 = (bf16[10,128,128]{2,1,0:T(8,128)(2,1)S(1)}, bf16[10,128,128]{2,1,0:T(8,128)(2,1)}, u32[]{:S(2)}) copy-start(bf16[10,128,128]{2,1,0:T(8,128)(2,1)} %copy-done.2) | copy-start | bytes 983044
  199.3 11.8 %copy-start.11 = (f32[128,64]{1,0:T(8,128)S(1)}, f32[128,64]{1,0:T(8,128)}, u32[]{:S(2)}) copy-start(f32[128,64]{1,0:T(8,128)} %get-tuple-element.55) | copy-start | bytes 98308
  200.5 12.1 %collective-permute-start.11 = (bf16[128,32,32]{0,2,1:T(8,128)(2,1)S(1)}, bf16[128,32,32]{0,2,1:T(8,128)(2,1)S(1)}, u32[]{:S(2)}, u32[]{:S(2)}) collective-permute-start(bf16[128,32,32]{0,2,1:T(8,128)(2,1)S(1)} %get-tuple-element.36), channel_id=1, source_target_pairs={{0,1},{1,2},{2,3},{3,4},{4,5},{5,6},{6,7},{7,0},{8,9},{9,10},{10,1... | collective-permute-start | bytes 786440 | tf_op jit(solution)/shard_map/ppermute | solution.py:190
  201.7 12.5 %collective-permute-start.12 = (bf16[128,32,32]{0,2,1:T(8,128)(2,1)S(1)}, bf16[128,32,32]{0,2,1:T(8,128)(2,1)S(1)}, u32[]{:S(2)}, u32[]{:S(2)}) collective-permute-start(bf16[128,32,32]{0,2,1:T(8,128)(2,1)S(1)} %get-tuple-element.42), channel_id=1, source_target_pairs={{0,2},{1,3},{2,4},{3,5},{4,6},{5,7},{6,0},{7,1},{8,10},{9,11},{10,... | collective-permute-start | bytes 786440 | tf_op jit(solution)/shard_map/ppermute | solution.py:190
  204.1 27.6 %collective-permute-start.13 = (bf16[128,32,32]{0,2,1:T(8,128)(2,1)}, bf16[128,32,32]{0,2,1:T(8,128)(2,1)}, u32[]{:S(2)}, u32[]{:S(2)}) collective-permute-start(bf16[128,32,32]{0,2,1:T(8,128)(2,1)} %get-tuple-element.41), channel_id=1, source_target_pairs={{0,3},{1,4},{2,5},{3,6},{4,7},{5,0},{6,1},{7,2},{8,11},{9,12},{10,... | collective-permute-start | bytes 786440 | tf_op jit(solution)/shard_map/ppermute | solution.py:190
  208.3 8.3 %collective-permute-start.19 = (bf16[2,128,256]{2,1,0:T(8,128)(2,1)S(1)}, bf16[2,128,256]{2,1,0:T(8,128)(2,1)S(1)}, u32[]{:S(2)}, u32[]{:S(2)}) collective-permute-start(bf16[2,128,256]{2,1,0:T(8,128)(2,1)S(1)} %slice.180), channel_id=1, source_target_pairs={{16,0},{24,8},{32,16},{40,24},{48,32},{56,40},{64,48},{72,56},{80,... | collective-permute-start | bytes 393224 | tf_op jit(solution)/shard_map/ppermute | solution.py:30
  211.4 18.1 %copy-start.12 = (bf16[2,128,256]{2,1,0:T(8,128)(2,1)}, bf16[2,128,256]{2,1,0:T(8,128)(2,1)S(1)}, u32[]{:S(2)}) copy-start(bf16[2,128,256]{2,1,0:T(8,128)(2,1)S(1)} %collective-permute-done.20) | copy-start | bytes 393220
  211.4 24.9 %collective-permute-start.14 = (bf16[128,32,32]{0,2,1:T(8,128)(2,1)}, bf16[128,32,32]{0,2,1:T(8,128)(2,1)S(1)}, u32[]{:S(2)}, u32[]{:S(2)}) collective-permute-start(bf16[128,32,32]{0,2,1:T(8,128)(2,1)} %get-tuple-element.40), channel_id=1, source_target_pairs={{0,4},{1,5},{2,6},{3,7},{4,0},{5,1},{6,2},{7,3},{8,12},{9,13},{10,... | collective-permute-start | bytes 786440 | tf_op jit(solution)/shard_map/ppermute | solution.py:190
  212.6 16.9 %copy-start.9 = (bf16[128,32,32]{0,2,1:T(8,128)(2,1)}, bf16[128,32,32]{0,2,1:T(8,128)(2,1)S(1)}, u32[]{:S(2)}) copy-start(bf16[128,32,32]{0,2,1:T(8,128)(2,1)S(1)} %collective-permute-done.11) | copy-start | bytes 786436
  212.6 23.7 %collective-permute-start.15 = (bf16[128,32,32]{0,2,1:T(8,128)(2,1)}, bf16[128,32,32]{0,2,1:T(8,128)(2,1)S(1)}, u32[]{:S(2)}, u32[]{:S(2)}) collective-permute-start(bf16[128,32,32]{0,2,1:T(8,128)(2,1)} %get-tuple-element.39), channel_id=1, source_target_pairs={{0,5},{1,6},{2,7},{3,0},{4,1},{5,2},{6,3},{7,4},{8,13},{9,14},{10,... | collective-permute-start | bytes 786440 | tf_op jit(solution)/shard_map/ppermute | solution.py:190
  214.2 15.3 %copy-start.10 = (bf16[128,32,32]{0,2,1:T(8,128)(2,1)}, bf16[128,32,32]{0,2,1:T(8,128)(2,1)S(1)}, u32[]{:S(2)}) copy-start(bf16[128,32,32]{0,2,1:T(8,128)(2,1)S(1)} %collective-permute-done.12) | copy-start | bytes 786436
  214.2 22.1 %collective-permute-start.16 = (bf16[128,32,32]{0,2,1:T(8,128)(2,1)}, bf16[128,32,32]{0,2,1:T(8,128)(2,1)S(1)}, u32[]{:S(2)}, u32[]{:S(2)}) collective-permute-start(bf16[128,32,32]{0,2,1:T(8,128)(2,1)} %get-tuple-element.38), channel_id=1, source_target_pairs={{0,6},{1,7},{2,0},{3,1},{4,2},{5,3},{6,4},{7,5},{8,14},{9,15},{10,... | collective-permute-start | bytes 786440 | tf_op jit(solution)/shard_map/ppermute | solution.py:190
  216.5 12.9 %copy-start.13 = (bf16[2,128,256]{2,1,0:T(8,128)(2,1)}, bf16[2,128,256]{2,1,0:T(8,128)(2,1)S(1)}, u32[]{:S(2)}) copy-start(bf16[2,128,256]{2,1,0:T(8,128)(2,1)S(1)} %collective-permute-done.19) | copy-start | bytes 393220
  216.5 19.8 %collective-permute-start.17 = (bf16[128,32,32]{0,2,1:T(8,128)(2,1)}, bf16[128,32,32]{0,2,1:T(8,128)(2,1)}, u32[]{:S(2)}, u32[]{:S(2)}) collective-permute-start(bf16[128,32,32]{0,2,1:T(8,128)(2,1)} %get-tuple-element.37), channel_id=1, source_target_pairs={{0,7},{1,0},{2,1},{3,2},{4,3},{5,4},{6,5},{7,6},{8,15},{9,8},{10,9... | collective-permute-start | bytes 786440 | tf_op jit(solution)/shard_map/ppermute | solution.py:190
  231.8 9.0 %collective-permute-start.21 = (bf16[1,128,256]{2,1,0:T(8,128)(2,1)S(1)}, bf16[1,128,256]{2,1,0:T(8,128)(2,1)S(1)}, u32[]{:S(2)}, u32[]{:S(2)}) collective-permute-start(bf16[1,128,256]{2,1,0:T(8,128)(2,1)S(1)} %slice.181), channel_id=1, source_target_pairs={{8,0},{16,8},{24,16},{32,24},{40,32},{48,40},{56,48},{64,56},{72,6... | collective-permute-start | bytes 196616 | tf_op jit(solution)/shard_map/ppermute | solution.py:30
Sparse Core Ops, SparseCore 0:
  22.1 148.0 all-gather.1

commit v2 on v1

--- a/solution.py
+++ b/solution.py
@@ -100,11 +100,11 @@
 
 
 def return_window(pieces):
-    far = shifted(pieces[:2].astype(jnp.bfloat16), -8).astype(jnp.float32)
-    four = pieces[2:]
-    two = four[4:] + shifted(four[:4].astype(jnp.bfloat16), -4).astype(jnp.float32)
-    one = two[2:] + shifted(two[:2].astype(jnp.bfloat16), -2).astype(jnp.float32) + far
-    return one[1] + shifted(one[:1].astype(jnp.bfloat16), -1).astype(jnp.float32)[0]
+    total = pieces[REACH]
+    for reach in range(1, REACH + 1):
+        back = shifted(pieces[REACH - reach].astype(jnp.bfloat16), -reach)
+        total = total + back.astype(jnp.float32)
+    return total
 
 
 def per_device(queries, keys, values, out_weight, out_grad, doc_ids, block_mask, positions):

time: 252 us -> 281 us (1.12)
  the two profiles are of different devices: /device:TPU:97 before, /device:TPU:233 now
where the time goes in v2:
time: 281 us; the launch traced here: 280 us
  waiting for transfers between devices  108 us (38%)
  starting transfers between devices  70.3 us (25%)
  local copies, waits for them, and re-layouts  29.8 us (11%)
  matrix products  28.1 us (10%)
  other arithmetic  16.7 us (6%)
  between operations  14.7 us (5%)
  blocking collectives  12.3 us (4%)
    all_gather x1, waiting for transfers between devices, per_device(): stripes = lax.all_gather(pieces, SEQ, axis=1, tiled=True)  74.1 us
    ppermute x13, starting transfers between devices, shifted(): return lax.ppermute(block, SEQ, route)  44.1 us
    ppermute x7, waiting for transfers between devices, per_device(): lax.ppermute(piece, 'kv', [(i, (i + j) % kv_count) for i in range(kv_coun...  22.7 us
    unnamed x87, local copies, waits for them, and re-layouts  17.2 us
    ppermute x7, starting transfers between devices, per_device(): lax.ppermute(out_grad, 'kv', [(i, (i - j) % kv_count) for i in range(kv_c...  13.4 us
    ppermute x7, starting transfers between devices, per_device(): lax.ppermute(piece, 'kv', [(i, (i + j) % kv_count) for i in range(kv_coun...  12.7 us
    all_to_all x1, blocking collectives, per_device(): lax.all_to_all(out_weight, 'kv', split_axis=0, concat_axis=1, tiled=True)  12.3 us
    ppermute x13, waiting for transfers between devices, shifted(): return lax.ppermute(block, SEQ, route)  9.77 us
  transfers between devices with their start and end apart: 28, of which 8 were waited for; matrix products, arithmetic and copies ran while one was open for 19% of the time, Pallas kernels for 0%

profile of v2, /device:TPU:233, one launch (start us, length us, event | category | flops | bytes accessed | tf_op | source)
XLA Modules:
  0.0 280.1 jit_solution(18061832756587406469)
XLA Ops:
  7.2 1.1 copy.127
  8.3 12.3 %all_to_all.19 = bf16[8,1024,32]{1,2,0:T(8,128)(2,1)} all-to-all(bf16[8,1024,32]{1,2,0:T(8,128)(2,1)S(1)} %bitcast.171), channel_id=1, replica_groups=mesh['sz'=16,'core'=2,'kv'=8] {'kv'}, dimensions={0} | all-to-all | bytes 1048576 | tf_op jit(solution)/shard_map/all_to_all | solution.py:133
  20.7 1.1 copy.88
  21.8 1.6 collective-permute-start.4
  24.3 2.0 collective-permute-start.6
  27.8 1.3 fusion.38
  31.1 7.1 %collective-permute-start = (bf16[1,129,256]{2,1,0:T(8,128)(2,1)S(1)}, bf16[1,129,256]{2,1,0:T(8,128)(2,1)S(1)}, u32[]{:S(2)}, u32[]{:S(2)}) collective-permute-start(bf16[1,129,256]{2,1,0:T(8,128)(2,1)S(1)} %fusion.23), channel_id=1, source_target_pairs={{0,8},{8,16},{16,24},{24,32},{32,40},{40,48},{48,56},{56,64},{64,7... | collective-permute-start | bytes 198152 | tf_op jit(solution)/shard_map/ppermute | solution.py:30
  38.2 1.1 copy.83
  42.9 1.9 collective-permute-start.2
  45.4 1.3 collective-permute-start.1
  47.2 8.0 %collective-permute-done.2 = bf16[2,129,256]{2,1,0:T(8,128)(2,1)S(1)} collective-permute-done((bf16[2,129,256]{2,1,0:T(8,128)(2,1)S(1)}, bf16[2,129,256]{2,1,0:T(8,128)(2,1)S(1)}, u32[]{:S(2)}, u32[]{:S(2)}) %collective-permute-start.2) | collective-permute-done | bytes 132128 | tf_op jit(solution)/shard_map/ppermute | solution.py:30
  55.2 1.8 collective-permute-done.1
  57.0 7.6 %collective-permute-start.8 = (bf16[128,1024]{0,1:T(8,128)(2,1)S(1)}, bf16[128,1024]{0,1:T(8,128)(2,1)S(1)}, u32[]{:S(2)}, u32[]{:S(2)}) collective-permute-start(bf16[128,1024]{0,1:T(8,128)(2,1)S(1)} %copy.88), channel_id=1, source_target_pairs={{0,3},{1,4},{2,5},{3,6},{4,7},{5,0},{6,1},{7,2},{8,11},{9,12},{10,... | collective-permute-start | bytes 786440 | tf_op jit(solution)/shard_map/ppermute | solution.py:137
  65.4 1.2 collective-permute-start.10
  67.3 1.5 collective-permute-start.3
  71.0 1.6 collective-permute-done.9
  79.8 2.0 constant_dynamic-slice_fusion
  81.9 2.0 copy.96
  84.3 1.4 or_and_fusion
  85.8 4.2 %exponential_reduce_fusion = (f32[8,128]{1,0:T(8,128)S(1)}, f32[8,128,1280]{1,2,0:T(8,128)}) fusion(bf16[1280,128,1]{1,0,2:T(8,128)(2,1)S(1)} %bitcast.172, pred[128,1280]{0,1:T(8,128)(4,1)S(1)} %or_and_fusion, bf16[128,8,64]{2,0,1:T(8,128)(2,1)S(1)} %get-tuple-element.44, bf16[128,8,64]{2,0,1:T(8,128)(2,1)S(1)} %get-tuple-element.43), kind=kOutput, calls=%fused_computation.7 | convolution fusion | flops 341312768 | bytes 6000640 | tf_op jit(solution)/shard_map/sub | solution.py:166
  90.0 3.2 %divide_convert_fusion = bf16[8,128,1280]{1,2,0:T(8,128)(2,1)S(1)} fusion(f32[8,128,1280]{1,2,0:T(8,128)} %get-tuple-element.71, f32[8,128]{1,0:T(8,128)S(1)} %get-tuple-element.70), kind=kLoop, calls=%fused_computation.6 | loop fusion | flops 2621440 | bytes 7868416 | tf_op jit(solution)/shard_map/convert_element_type | solution.py:167
  93.2 74.1 %all-gather.2.cloned.1.call-done = bf16[1024,8192]{0,1:T(8,128)(2,1)} async-done(((bf16[1024,256]{0,1:T(8,128)(2,1)}), bf16[1024,8192]{0,1:T(8,128)(2,1)}) %all-gather.2.cloned.1.call-update) | async-done | bytes 16777232 | tf_op jit(solution)/shard_map/all_gather | solution.py:134
  167.2 9.5 %convolution_convert_fusion.1 = bf16[128,1024]{1,0:T(8,128)(2,1)} fusion(bf16[128,8192]{0,1:T(8,128)(2,1)} %bitcast.160, bf16[1024,8192]{0,1:T(8,128)(2,1)} %all-gather.2.cloned.1.call-done), kind=kOutput, calls=%fused_computation.15 | convolution fusion | flops 2147614720 | bytes 19136512 | tf_op jit(solution)/shard_map/dot_general | solution.py:142
  176.7 1.1 copy.98
  177.8 1.3 multiply_reduce_fusion
  181.1 1.1 fusion.4
  182.2 2.0 fusion.5
  185.4 2.2 collective-permute-start.18
  187.6 3.0 %collective-permute-start.19 = (bf16[128,256]{1,0:T(8,128)(2,1)S(1)}, bf16[128,256]{1,0:T(8,128)(2,1)S(1)}, u32[]{:S(2)}, u32[]{:S(2)}) collective-permute-start(bf16[128,256]{1,0:T(8,128)(2,1)S(1)} %get-tuple-element.55), channel_id=1, source_target_pairs={{16,0},{24,8},{32,16},{40,24},{48,32},{56,40},{64,48},{72,56},{80,... | collective-permute-start | bytes 196616 | tf_op jit(solution)/shard_map/ppermute | solution.py:30
  190.6 6.0 %collective-permute-start.20 = (bf16[128,256]{1,0:T(8,128)(2,1)S(1)}, bf16[128,256]{1,0:T(8,128)(2,1)S(1)}, u32[]{:S(2)}, u32[]{:S(2)}) collective-permute-start(bf16[128,256]{1,0:T(8,128)(2,1)S(1)} %get-tuple-element.54), channel_id=1, source_target_pairs={{24,0},{32,8},{40,16},{48,24},{56,32},{64,40},{72,48},{80,56},{88,... | collective-permute-start | bytes 196616 | tf_op jit(solution)/shard_map/ppermute | solution.py:30
  196.6 2.2 collective-permute-start.21
  198.8 2.8 %collective-permute-start.22 = (bf16[128,256]{1,0:T(8,128)(2,1)}, bf16[128,256]{1,0:T(8,128)(2,1)}, u32[]{:S(2)}, u32[]{:S(2)}) collective-permute-start(bf16[128,256]{1,0:T(8,128)(2,1)} %get-tuple-element.52), channel_id=1, source_target_pairs={{40,0},{48,8},{56,16},{64,24},{72,32},{80,40},{88,48},{96,56},{104... | collective-permute-start | bytes 196616 | tf_op jit(solution)/shard_map/ppermute | solution.py:30
  201.6 8.3 %fusion.44 = f32[128,8192]{0,1:S(1)} fusion(bf16[1024,8192]{0,1:T(8,128)(2,1)} %all-gather.2.cloned.1.call-done, bf16[128,1024]{0,1:T(8,128)(2,1)S(1)} %bitcast.174), kind=kOutput, calls=%fused_computation.145 | convolution fusion | flops 2147483648 | bytes 21233664
  211.2 1.2 dynamic-slice_bitcast_fusion.6
  212.5 6.6 %collective-permute-start.23 = (bf16[128,256]{1,0:T(8,128)(2,1)}, bf16[128,256]{1,0:T(8,128)(2,1)}, u32[]{:S(2)}, u32[]{:S(2)}) collective-permute-start(bf16[128,256]{1,0:T(8,128)(2,1)} %get-tuple-element.51), channel_id=1, source_target_pairs={{48,0},{56,8},{64,16},{72,24},{80,32},{88,40},{96,48},{104,56},{11... | collective-permute-start | bytes 196616 | tf_op jit(solution)/shard_map/ppermute | solution.py:30
  219.0 5.8 %collective-permute-start.24 = (bf16[128,256]{1,0:T(8,128)(2,1)}, bf16[128,256]{1,0:T(8,128)(2,1)}, u32[]{:S(2)}, u32[]{:S(2)}) collective-permute-start(bf16[128,256]{1,0:T(8,128)(2,1)} %get-tuple-element.50), channel_id=1, source_target_pairs={{56,0},{64,8},{72,16},{80,24},{88,32},{96,40},{104,48},{112,56},{1... | collective-permute-start | bytes 196616 | tf_op jit(solution)/shard_map/ppermute | solution.py:30
  224.8 1.9 collective-permute-start.25
  226.7 1.9 collective-permute-start.26
  229.5 1.8 copy.108
  231.3 1.8 copy.110
  233.1 1.2 collective-permute-start.11
  235.1 1.9 collective-permute-start.13
  237.0 1.2 collective-permute-start.14
  238.7 1.2 fusion.21
  241.2 7.1 %collective-permute-start.16 = (bf16[128,32,32]{0,2,1:T(8,128)(2,1)}, bf16[128,32,32]{0,2,1:T(8,128)(2,1)S(1)}, u32[]{:S(2)}, u32[]{:S(2)}) collective-permute-start(bf16[128,32,32]{0,2,1:T(8,128)(2,1)} %get-tuple-element.38), channel_id=1, source_target_pairs={{0,6},{1,7},{2,0},{3,1},{4,2},{5,3},{6,4},{7,5},{8,14},{9,15},{10,... | collective-permute-start | bytes 786440 | tf_op jit(solution)/shard_map/ppermute | solution.py:190
  248.3 7.3 %collective-permute-done.12 = bf16[128,32,32]{0,2,1:T(8,128)(2,1)S(1)} collective-permute-done((bf16[128,32,32]{0,2,1:T(8,128)(2,1)}, bf16[128,32,32]{0,2,1:T(8,128)(2,1)S(1)}, u32[]{:S(2)}, u32[]{:S(2)}) %collective-permute-start.12) | collective-permute-done | bytes 262176 | tf_op jit(solution)/shard_map/ppermute | solution.py:190
  257.4 9.2 %collective-permute-done.16 = bf16[128,32,32]{0,2,1:T(8,128)(2,1)S(1)} collective-permute-done((bf16[128,32,32]{0,2,1:T(8,128)(2,1)}, bf16[128,32,32]{0,2,1:T(8,128)(2,1)S(1)}, u32[]{:S(2)}, u32[]{:S(2)}) %collective-permute-start.16) | collective-permute-done | bytes 262176 | tf_op jit(solution)/shard_map/ppermute | solution.py:190
  266.6 5.5 %collective-permute-done.17 = bf16[128,32,32]{0,2,1:T(8,128)(2,1)S(1)} collective-permute-done((bf16[128,32,32]{0,2,1:T(8,128)(2,1)}, bf16[128,32,32]{0,2,1:T(8,128)(2,1)S(1)}, u32[]{:S(2)}, u32[]{:S(2)}) %collective-permute-start.17) | collective-permute-done | bytes 262176 | tf_op jit(solution)/shard_map/ppermute | solution.py:190
  (150 shorter events, 31.2 us)
Async XLA Ops:
  7.2 32.6 %copy-start.30 = (s32[1,32]{1,0:T(1,128)S(1)}, s32[1,32]{1,0:T(1,128)}, u32[]{:S(2)}) copy-start(s32[1,32]{1,0:T(1,128)} %param.16) | copy-start | bytes 388
  7.2 160.1 %all-gather.2.cloned.1.call-start = ((), (), s32[]{:S(2)}) async-start(), calls=%async_computation.1 | async-start | bytes 17301504 | tf_op jit(solution)/shard_map/all_gather | solution.py:134
  21.8 42.8 %collective-permute-start.4 = (bf16[128,1024]{0,1:T(8,128)(2,1)S(1)}, bf16[128,1024]{0,1:T(8,128)(2,1)S(1)}, u32[]{:S(2)}, u32[]{:S(2)}) collective-permute-start(bf16[128,1024]{0,1:T(8,128)(2,1)S(1)} %copy.88), channel_id=1, source_target_pairs={{0,7},{1,0},{2,1},{3,2},{4,3},{5,4},{6,5},{7,6},{8,15},{9,8},{10,9... | collective-permute-start | bytes 786440 | tf_op jit(solution)/shard_map/ppermute | solution.py:137
  23.4 42.1 %collective-permute-start.5 = (bf16[128,1024]{0,1:T(8,128)(2,1)S(1)}, bf16[128,1024]{0,1:T(8,128)(2,1)S(1)}, u32[]{:S(2)}, u32[]{:S(2)}) collective-permute-start(bf16[128,1024]{0,1:T(8,128)(2,1)S(1)} %copy.88), channel_id=1, source_target_pairs={{0,6},{1,7},{2,0},{3,1},{4,2},{5,3},{6,4},{7,5},{8,14},{9,15},{10,... | collective-permute-start | bytes 786440 | tf_op jit(solution)/shard_map/ppermute | solution.py:137
  24.3 43.0 %collective-permute-start.6 = (bf16[128,1024]{0,1:T(8,128)(2,1)S(1)}, bf16[128,1024]{0,1:T(8,128)(2,1)S(1)}, u32[]{:S(2)}, u32[]{:S(2)}) collective-permute-start(bf16[128,1024]{0,1:T(8,128)(2,1)S(1)} %copy.88), channel_id=1, source_target_pairs={{0,5},{1,6},{2,7},{3,0},{4,1},{5,2},{6,3},{7,4},{8,13},{9,14},{10,... | collective-permute-start | bytes 786440 | tf_op jit(solution)/shard_map/ppermute | solution.py:137
  27.7 14.7 %copy-start.22 = (pred[64]{0:T(512)(128)(4,1)}, pred[64]{0:T(512)(128)(4,1)S(1)}, u32[]{:S(2)}) copy-start(pred[64]{0:T(512)(128)(4,1)S(1)} %broadcast_compare_fusion.2) | copy-start | bytes 196
  27.7 14.7 %copy-start.24 = (f32[64]{0:T(128)}, f32[64]{0:T(128)S(1)}, u32[]{:S(2)}) copy-start(f32[64]{0:T(128)S(1)} %multiply_exponential_fusion) | copy-start | bytes 772
  27.7 14.7 %copy-start.25 = (pred[64]{0:T(512)(128)(4,1)}, pred[64]{0:T(512)(128)(4,1)S(1)}, u32[]{:S(2)}) copy-start(pred[64]{0:T(512)(128)(4,1)S(1)} %get-tuple-element.74) | copy-start | bytes 196
  27.7 14.7 %copy-start.26 = (pred[64]{0:T(512)(128)(4,1)}, pred[64]{0:T(512)(128)(4,1)S(1)}, u32[]{:S(2)}) copy-start(pred[64]{0:T(512)(128)(4,1)S(1)} %get-tuple-element.75) | copy-start | bytes 196
  29.1 13.4 %copy-start.14 = (f32[128]{0:T(128)}, f32[128]{0:T(128)S(1)}, u32[]{:S(2)}) copy-start(f32[128]{0:T(128)S(1)} %get-tuple-element.67) | copy-start | bytes 1540
  29.1 13.4 %copy-start.16 = (f32[128]{0:T(128)}, f32[128]{0:T(128)S(1)}, u32[]{:S(2)}) copy-start(f32[128]{0:T(128)S(1)} %get-tuple-element.68) | copy-start | bytes 1540
  29.1 13.4 %copy-start.18 = (f32[128]{0:T(128)}, f32[128]{0:T(128)S(1)}, u32[]{:S(2)}) copy-start(f32[128]{0:T(128)S(1)} %get-tuple-element.69) | copy-start | bytes 1540
  31.1 11.4 %collective-permute-start = (bf16[1,129,256]{2,1,0:T(8,128)(2,1)S(1)}, bf16[1,129,256]{2,1,0:T(8,128)(2,1)S(1)}, u32[]{:S(2)}, u32[]{:S(2)}) collective-permute-start(bf16[1,129,256]{2,1,0:T(8,128)(2,1)S(1)} %fusion.23), channel_id=1, source_target_pairs={{0,8},{8,16},{16,24},{24,32},{32,40},{40,48},{48,56},{56,64},{64,7... | collective-permute-start | bytes 198152 | tf_op jit(solution)/shard_map/ppermute | solution.py:30
  42.4 43.4 %copy-start.2 = (bf16[128,8,64]{2,0,1:T(8,128)(2,1)}, bf16[128,8,64]{2,0,1:T(8,128)(2,1)S(1)}, u32[]{:S(2)}) copy-start(bf16[128,8,64]{2,0,1:T(8,128)(2,1)S(1)} %get-tuple-element.43) | copy-start | bytes 393220
  42.4 43.4 %copy-start.4 = (bf16[128,8,64]{2,0,1:T(8,128)(2,1)}, bf16[128,8,64]{2,0,1:T(8,128)(2,1)S(1)}, u32[]{:S(2)}) copy-start(bf16[128,8,64]{2,0,1:T(8,128)(2,1)S(1)} %get-tuple-element.44) | copy-start | bytes 393220
  42.9 12.3 %collective-permute-start.2 = (bf16[2,129,256]{2,1,0:T(8,128)(2,1)S(1)}, bf16[2,129,256]{2,1,0:T(8,128)(2,1)S(1)}, u32[]{:S(2)}, u32[]{:S(2)}) collective-permute-start(bf16[2,129,256]{2,1,0:T(8,128)(2,1)S(1)} %pad_maximum_fusion.4), channel_id=1, source_target_pairs={{0,16},{8,24},{16,32},{24,40},{32,48},{40,56},{48,64},{56,72},{64,... | collective-permute-start | bytes 396296 | tf_op jit(solution)/shard_map/ppermute | solution.py:30
  45.4 11.6 %collective-permute-start.1 = (bf16[2,129,256]{2,1,0:T(8,128)(2,1)S(1)}, bf16[2,129,256]{2,1,0:T(8,128)(2,1)S(1)}, u32[]{:S(2)}, u32[]{:S(2)}) collective-permute-start(bf16[2,129,256]{2,1,0:T(8,128)(2,1)S(1)} %pad_maximum_fusion.4), channel_id=1, source_target_pairs={{0,64},{8,72},{16,80},{24,88},{32,96},{40,104},{48,112},{56,120},{... | collective-permute-start | bytes 396296 | tf_op jit(solution)/shard_map/ppermute | solution.py:30
  55.2 14.3 %collective-permute-start.7 = (bf16[128,1024]{0,1:T(8,128)(2,1)S(1)}, bf16[128,1024]{0,1:T(8,128)(2,1)S(1)}, u32[]{:S(2)}, u32[]{:S(2)}) collective-permute-start(bf16[128,1024]{0,1:T(8,128)(2,1)S(1)} %copy.88), channel_id=1, source_target_pairs={{0,4},{1,5},{2,6},{3,7},{4,0},{5,1},{6,2},{7,3},{8,12},{9,13},{10,... | collective-permute-start | bytes 786440 | tf_op jit(solution)/shard_map/ppermute | solution.py:137
  57.0 13.3 %collective-permute-start.8 = (bf16[128,1024]{0,1:T(8,128)(2,1)S(1)}, bf16[128,1024]{0,1:T(8,128)(2,1)S(1)}, u32[]{:S(2)}, u32[]{:S(2)}) collective-permute-start(bf16[128,1024]{0,1:T(8,128)(2,1)S(1)} %copy.88), channel_id=1, source_target_pairs={{0,3},{1,4},{2,5},{3,6},{4,7},{5,0},{6,1},{7,2},{8,11},{9,12},{10,... | collective-permute-start | bytes 786440 | tf_op jit(solution)/shard_map/ppermute | solution.py:137
  64.6 8.0 %collective-permute-start.9 = (bf16[128,1024]{0,1:T(8,128)(2,1)S(1)}, bf16[128,1024]{0,1:T(8,128)(2,1)S(1)}, u32[]{:S(2)}, u32[]{:S(2)}) collective-permute-start(bf16[128,1024]{0,1:T(8,128)(2,1)S(1)} %copy.88), channel_id=1, source_target_pairs={{0,2},{1,3},{2,4},{3,5},{4,6},{5,7},{6,0},{7,1},{8,10},{9,11},{10,... | collective-permute-start | bytes 786440 | tf_op jit(solution)/shard_map/ppermute | solution.py:137
  65.4 7.9 %collective-permute-start.10 = (bf16[128,1024]{0,1:T(8,128)(2,1)S(1)}, bf16[128,1024]{0,1:T(8,128)(2,1)S(1)}, u32[]{:S(2)}, u32[]{:S(2)}) collective-permute-start(bf16[128,1024]{0,1:T(8,128)(2,1)S(1)} %copy.88), channel_id=1, source_target_pairs={{0,1},{1,2},{2,3},{3,4},{4,5},{5,6},{6,7},{7,0},{8,9},{9,10},{10,1... | collective-permute-start | bytes 786440 | tf_op jit(solution)/shard_map/ppermute | solution.py:137
  67.3 16.6 %collective-permute-start.3 = (bf16[4,129,256]{2,1,0:T(8,128)(2,1)S(1)}, bf16[4,129,256]{2,1,0:T(8,128)(2,1)S(1)}, u32[]{:S(2)}, u32[]{:S(2)}) collective-permute-start(bf16[4,129,256]{2,1,0:T(8,128)(2,1)S(1)} %pad_maximum_fusion.1), channel_id=1, source_target_pairs={{0,32},{8,40},{16,48},{24,56},{32,64},{40,72},{48,80},{56,88},{64,... | collective-permute-start | bytes 792584 | tf_op jit(solution)/shard_map/ppermute | solution.py:30
  79.8 4.1 %copy-start.9 = (bf16[128,128]{1,0:T(8,128)(2,1)S(1)}, bf16[128,128]{1,0:T(8,128)(2,1)}, u32[]{:S(2)}) copy-start(bf16[128,128]{1,0:T(8,128)(2,1)} %param.12) | copy-start | bytes 98308
  81.9 2.4 copy-start.20
  184.2 17.5 %copy-start.1 = (bf16[128,8,128]{2,0,1:T(8,128)(2,1)S(1)}, bf16[128,8,128]{2,0,1:T(8,128)(2,1)}, u32[]{:S(2)}) copy-start(bf16[128,8,128]{2,0,1:T(8,128)(2,1)} %get-tuple-element.73) | copy-start | bytes 786436
  185.4 27.0 %collective-permute-start.18 = (bf16[128,256]{1,0:T(8,128)(2,1)S(1)}, bf16[128,256]{1,0:T(8,128)(2,1)S(1)}, u32[]{:S(2)}, u32[]{:S(2)}) collective-permute-start(bf16[128,256]{1,0:T(8,128)(2,1)S(1)} %get-tuple-element.47), channel_id=1, source_target_pairs={{8,0},{16,8},{24,16},{32,24},{40,32},{48,40},{56,48},{64,56},{72,6... | collective-permute-start | bytes 196616 | tf_op jit(solution)/shard_map/ppermute | solution.py:30
  187.6 31.4 %collective-permute-start.19 = (bf16[128,256]{1,0:T(8,128)(2,1)S(1)}, bf16[128,256]{1,0:T(8,128)(2,1)S(1)}, u32[]{:S(2)}, u32[]{:S(2)}) collective-permute-start(bf16[128,256]{1,0:T(8,128)(2,1)S(1)} %get-tuple-element.55), channel_id=1, source_target_pairs={{16,0},{24,8},{32,16},{40,24},{48,32},{56,40},{64,48},{72,56},{80,... | collective-permute-start | bytes 196616 | tf_op jit(solution)/shard_map/ppermute | solution.py:30
  190.6 34.2 %collective-permute-start.20 = (bf16[128,256]{1,0:T(8,128)(2,1)S(1)}, bf16[128,256]{1,0:T(8,128)(2,1)S(1)}, u32[]{:S(2)}, u32[]{:S(2)}) collective-permute-start(bf16[128,256]{1,0:T(8,128)(2,1)S(1)} %get-tuple-element.54), channel_id=1, source_target_pairs={{24,0},{32,8},{40,16},{48,24},{56,32},{64,40},{72,48},{80,56},{88,... | collective-permute-start | bytes 196616 | tf_op jit(solution)/shard_map/ppermute | solution.py:30
  196.6 30.1 %collective-permute-start.21 = (bf16[128,256]{1,0:T(8,128)(2,1)S(1)}, bf16[128,256]{1,0:T(8,128)(2,1)S(1)}, u32[]{:S(2)}, u32[]{:S(2)}) collective-permute-start(bf16[128,256]{1,0:T(8,128)(2,1)S(1)} %get-tuple-element.53), channel_id=1, source_target_pairs={{32,0},{40,8},{48,16},{56,24},{64,32},{72,40},{80,48},{88,56},{96,... | collective-permute-start | bytes 196616 | tf_op jit(solution)/shard_map/ppermute | solution.py:30
  198.8 34.3 %collective-permute-start.22 = (bf16[128,256]{1,0:T(8,128)(2,1)}, bf16[128,256]{1,0:T(8,128)(2,1)}, u32[]{:S(2)}, u32[]{:S(2)}) collective-permute-start(bf16[128,256]{1,0:T(8,128)(2,1)} %get-tuple-element.52), channel_id=1, source_target_pairs={{40,0},{48,8},{56,16},{64,24},{72,32},{80,40},{88,48},{96,56},{104... | collective-permute-start | bytes 196616 | tf_op jit(solution)/shard_map/ppermute | solution.py:30
  210.5 45.1 %copy-start.15 = (f32[128]{0:T(128)S(1)}, f32[128]{0:T(128)}, u32[]{:S(2)}) copy-start(f32[128]{0:T(128)} %copy-done.14) | copy-start | bytes 1540
  210.5 45.1 %copy-start.17 = (f32[128]{0:T(128)S(1)}, f32[128]{0:T(128)}, u32[]{:S(2)}) copy-start(f32[128]{0:T(128)} %copy-done.16) | copy-start | bytes 1540
  210.5 45.1 %copy-start.19 = (f32[128]{0:T(128)S(1)}, f32[128]{0:T(128)}, u32[]{:S(2)}) copy-start(f32[128]{0:T(128)} %copy-done.18) | copy-start | bytes 1540
  210.5 45.1 %copy-start.23 = (pred[64]{0:T(512)(128)(4,1)S(1)}, pred[64]{0:T(512)(128)(4,1)}, u32[]{:S(2)}) copy-start(pred[64]{0:T(512)(128)(4,1)} %copy-done.22) | copy-start | bytes 196
  212.4 16.2 %copy-start.10 = (bf16[128,256]{1,0:T(8,128)(2,1)}, bf16[128,256]{1,0:T(8,128)(2,1)S(1)}, u32[]{:S(2)}) copy-start(bf16[128,256]{1,0:T(8,128)(2,1)S(1)} %collective-permute-done.18) | copy-start | bytes 196612
  212.5 21.8 %collective-permute-start.23 = (bf16[128,256]{1,0:T(8,128)(2,1)}, bf16[128,256]{1,0:T(8,128)(2,1)}, u32[]{:S(2)}, u32[]{:S(2)}) collective-permute-start(bf16[128,256]{1,0:T(8,128)(2,1)} %get-tuple-element.51), channel_id=1, source_target_pairs={{48,0},{56,8},{64,16},{72,24},{80,32},{88,40},{96,48},{104,56},{11... | collective-permute-start | bytes 196616 | tf_op jit(solution)/shard_map/ppermute | solution.py:30
  219.0 9.6 %copy-start.11 = (bf16[128,256]{1,0:T(8,128)(2,1)}, bf16[128,256]{1,0:T(8,128)(2,1)S(1)}, u32[]{:S(2)}) copy-start(bf16[128,256]{1,0:T(8,128)(2,1)S(1)} %collective-permute-done.19) | copy-start | bytes 196612
  219.0 16.1 %collective-permute-start.24 = (bf16[128,256]{1,0:T(8,128)(2,1)}, bf16[128,256]{1,0:T(8,128)(2,1)}, u32[]{:S(2)}, u32[]{:S(2)}) collective-permute-start(bf16[128,256]{1,0:T(8,128)(2,1)} %get-tuple-element.50), channel_id=1, source_target_pairs={{56,0},{64,8},{72,16},{80,24},{88,32},{96,40},{104,48},{112,56},{1... | collective-permute-start | bytes 196616 | tf_op jit(solution)/shard_map/ppermute | solution.py:30
  224.8 3.8 %copy-start.12 = (bf16[128,256]{1,0:T(8,128)(2,1)}, bf16[128,256]{1,0:T(8,128)(2,1)S(1)}, u32[]{:S(2)}) copy-start(bf16[128,256]{1,0:T(8,128)(2,1)S(1)} %collective-permute-done.20) | copy-start | bytes 196612
  224.8 12.2 %collective-permute-start.25 = (bf16[128,256]{1,0:T(8,128)(2,1)S(1)}, bf16[128,256]{1,0:T(8,128)(2,1)}, u32[]{:S(2)}, u32[]{:S(2)}) collective-permute-start(bf16[128,256]{1,0:T(8,128)(2,1)S(1)} %get-tuple-element.49), channel_id=1, source_target_pairs={{64,0},{72,8},{80,16},{88,24},{96,32},{104,40},{112,48},{120,56},{... | collective-permute-start | bytes 196616 | tf_op jit(solution)/shard_map/ppermute | solution.py:30
  226.7 11.4 %collective-permute-start.26 = (bf16[128,256]{1,0:T(8,128)(2,1)S(1)}, bf16[128,256]{1,0:T(8,128)(2,1)}, u32[]{:S(2)}, u32[]{:S(2)}) collective-permute-start(bf16[128,256]{1,0:T(8,128)(2,1)S(1)} %get-tuple-element.48), channel_id=1, source_target_pairs={{72,0},{80,8},{88,16},{96,24},{104,32},{112,40},{120,48},{128,56},... | collective-permute-start | bytes 196616 | tf_op jit(solution)/shard_map/ppermute | solution.py:30
  233.1 8.1 %collective-permute-start.11 = (bf16[128,32,32]{0,2,1:T(8,128)(2,1)}, bf16[128,32,32]{0,2,1:T(8,128)(2,1)S(1)}, u32[]{:S(2)}, u32[]{:S(2)}) collective-permute-start(bf16[128,32,32]{0,2,1:T(8,128)(2,1)} %get-tuple-element.36), channel_id=1, source_target_pairs={{0,1},{1,2},{2,3},{3,4},{4,5},{5,6},{6,7},{7,0},{8,9},{9,10},{10,1... | collective-permute-start | bytes 786440 | tf_op jit(solution)/shard_map/ppermute | solution.py:190
  234.3 21.3 %collective-permute-start.12 = (bf16[128,32,32]{0,2,1:T(8,128)(2,1)}, bf16[128,32,32]{0,2,1:T(8,128)(2,1)S(1)}, u32[]{:S(2)}, u32[]{:S(2)}) collective-permute-start(bf16[128,32,32]{0,2,1:T(8,128)(2,1)} %get-tuple-element.42), channel_id=1, source_target_pairs={{0,2},{1,3},{2,4},{3,5},{4,6},{5,7},{6,0},{7,1},{8,10},{9,11},{10,... | collective-permute-start | bytes 786440 | tf_op jit(solution)/shard_map/ppermute | solution.py:190
  235.1 22.3 %collective-permute-start.13 = (bf16[128,32,32]{0,2,1:T(8,128)(2,1)}, bf16[128,32,32]{0,2,1:T(8,128)(2,1)S(1)}, u32[]{:S(2)}, u32[]{:S(2)}) collective-permute-start(bf16[128,32,32]{0,2,1:T(8,128)(2,1)} %get-tuple-element.41), channel_id=1, source_target_pairs={{0,3},{1,4},{2,5},{3,6},{4,7},{5,0},{6,1},{7,2},{8,11},{9,12},{10,... | collective-permute-start | bytes 786440 | tf_op jit(solution)/shard_map/ppermute | solution.py:190
  237.0 20.4 %collective-permute-start.14 = (bf16[128,32,32]{0,2,1:T(8,128)(2,1)}, bf16[128,32,32]{0,2,1:T(8,128)(2,1)S(1)}, u32[]{:S(2)}, u32[]{:S(2)}) collective-permute-start(bf16[128,32,32]{0,2,1:T(8,128)(2,1)} %get-tuple-element.40), channel_id=1, source_target_pairs={{0,4},{1,5},{2,6},{3,7},{4,0},{5,1},{6,2},{7,3},{8,12},{9,13},{10,... | collective-permute-start | bytes 786440 | tf_op jit(solution)/shard_map/ppermute | solution.py:190
  238.2 19.2 %collective-permute-start.15 = (bf16[128,32,32]{0,2,1:T(8,128)(2,1)}, bf16[128,32,32]{0,2,1:T(8,128)(2,1)S(1)}, u32[]{:S(2)}, u32[]{:S(2)}) collective-permute-start(bf16[128,32,32]{0,2,1:T(8,128)(2,1)} %get-tuple-element.39), channel_id=1, source_target_pairs={{0,5},{1,6},{2,7},{3,0},{4,1},{5,2},{6,3},{7,4},{8,13},{9,14},{10,... | collective-permute-start | bytes 786440 | tf_op jit(solution)/shard_map/ppermute | solution.py:190
  241.2 25.4 %collective-permute-start.16 = (bf16[128,32,32]{0,2,1:T(8,128)(2,1)}, bf16[128,32,32]{0,2,1:T(8,128)(2,1)S(1)}, u32[]{:S(2)}, u32[]{:S(2)}) collective-permute-start(bf16[128,32,32]{0,2,1:T(8,128)(2,1)} %get-tuple-element.38), channel_id=1, source_target_pairs={{0,6},{1,7},{2,0},{3,1},{4,2},{5,3},{6,4},{7,5},{8,14},{9,15},{10,... | collective-permute-start | bytes 786440 | tf_op jit(solution)/shard_map/ppermute | solution.py:190
  255.6 16.6 %collective-permute-start.17 = (bf16[128,32,32]{0,2,1:T(8,128)(2,1)}, bf16[128,32,32]{0,2,1:T(8,128)(2,1)S(1)}, u32[]{:S(2)}, u32[]{:S(2)}) collective-permute-start(bf16[128,32,32]{0,2,1:T(8,128)(2,1)} %get-tuple-element.37), channel_id=1, source_target_pairs={{0,7},{1,0},{2,1},{3,2},{4,3},{5,4},{6,5},{7,6},{8,15},{9,8},{10,9... | collective-permute-start | bytes 786440 | tf_op jit(solution)/shard_map/ppermute | solution.py:190
  (11 other events, 17.2 us)
Sparse Core Ops, SparseCore 0:
  20.8 146.3 all-gather.1

commit v3 on v1

--- a/solution.py
+++ b/solution.py
@@ -183,12 +183,8 @@
         stripes.reshape(attn.shape[1], n_seq, kv_count, col_w),
         preferred_element_type=jnp.float32,
     ).astype(jnp.bfloat16)
-    total = lax.dynamic_index_in_dim(lo_part, kv_me, 0, keepdims=False).astype(jnp.float32)
-    for j in range(1, kv_count):
-        dest = (kv_me + j) % kv_count
-        piece = lax.dynamic_index_in_dim(lo_part, dest, 0, keepdims=False)
-        got = lax.ppermute(piece, "kv", [(i, (i + j) % kv_count) for i in range(kv_count)])
-        total = total + got.astype(jnp.float32)
+    got = lax.all_to_all(lo_part, "kv", split_axis=0, concat_axis=0, tiled=True)
+    total = jnp.sum(got.astype(jnp.float32), axis=0)
     layer_out = total.reshape(length, n_seq * col_w).astype(jnp.bfloat16)
     dkv_total = return_window(dkv)
     dk_total = dkv_total[:, :HD]

time: 252 us -> 257 us (1.020)
  waiting for transfers between devices: 93.7 us -> 112 us
  starting transfers between devices: 58 us -> 39.8 us
  local copies, waits for them, and re-layouts: 26.5 us -> 29.8 us
    ppermute x7 -> x0, starting transfers between devices: 20.8 us -> none  [per_device(): lax.ppermute(piece, 'kv', [(i, (i + j) % kv_count) for i in range(kv_coun...]
    ppermute x8, waiting for transfers between devices: 17.7 us -> 38.1 us  [shifted(): return lax.ppermute(block, SEQ, route)]
    all_to_all x0 -> x1, starting transfers between devices: none -> 4.49 us  [per_device(): got = lax.all_to_all(lo_part, 'kv', split_axis=0, concat_axis=0, tiled=True)]
    all_gather x1, waiting for transfers between devices: 71.7 us -> 69.2 us  [per_device(): stripes = lax.all_gather(pieces, SEQ, axis=1, tiled=True)]
    unnamed x65 -> x89, local copies, waits for them, and re-layouts: 16.8 us -> 16.9 us
  transfers between devices with their start and end apart: 23 -> 17, of which waited for: 8 -> 8; matrix products, arithmetic and copies ran while one was open for 20% -> 21% of each run, Pallas kernels for 0% -> 0%
where the time goes in v3:
time: 257 us; the launch traced here: 255 us
  waiting for transfers between devices  112 us (44%)
  starting transfers between devices  39.8 us (15%)
  local copies, waits for them, and re-layouts  29.8 us (12%)
  matrix products  27.2 us (11%)
  other arithmetic  18 us (7%)
  between operations  14.9 us (6%)
  blocking collectives  13.7 us (5%)
    all_gather x1, waiting for transfers between devices, per_device(): stripes = lax.all_gather(pieces, SEQ, axis=1, tiled=True)  69.2 us
    ppermute x8, waiting for transfers between devices, shifted(): return lax.ppermute(block, SEQ, route)  38.1 us
    ppermute x8, starting transfers between devices, shifted(): return lax.ppermute(block, SEQ, route)  30.4 us
    unnamed x89, local copies, waits for them, and re-layouts  16.9 us
    all_to_all x1, blocking collectives, per_device(): lax.all_to_all(out_weight, 'kv', split_axis=0, concat_axis=1, tiled=True)  13.7 us
    dot_general x1, matrix products, per_device(): lax.dot_general(og_perm, stripes, contract, preferred_element_type=jnp.fl...  9.47 us
    unnamed x1, matrix products  8.26 us
  transfers between devices with their start and end apart: 17, of which 8 were waited for; matrix products, arithmetic and copies ran while one was open for 21% of the time, Pallas kernels for 0%

profile of v3, /device:TPU:97, one launch (start us, length us, event | category | flops | bytes accessed | tf_op | source)
XLA Modules:
  0.0 255.0 jit_solution(3362245134346575349)
XLA Ops:
  7.2 1.1 copy.128
  8.3 13.7 %all_to_all.24 = bf16[8,1024,32]{1,2,0:T(8,128)(2,1)} all-to-all(bf16[8,1024,32]{1,2,0:T(8,128)(2,1)S(1)} %bitcast.122), channel_id=1, replica_groups=mesh['sz'=16,'core'=2,'kv'=8] {'kv'}, dimensions={0} | all-to-all | bytes 1048576 | tf_op jit(solution)/shard_map/all_to_all | solution.py:133
  22.0 1.1 copy.88
  23.1 1.9 collective-permute-start.4
  25.0 1.2 collective-permute-start.5
  27.6 1.3 fusion.25
  30.1 0.9 fusion.10
  30.9 6.8 %collective-permute-start = (bf16[1,129,256]{2,1,0:T(8,128)(2,1)S(1)}, bf16[1,129,256]{2,1,0:T(8,128)(2,1)S(1)}, u32[]{:S(2)}, u32[]{:S(2)}) collective-permute-start(bf16[1,129,256]{2,1,0:T(8,128)(2,1)S(1)} %fusion.10), channel_id=1, source_target_pairs={{0,8},{8,16},{16,24},{24,32},{32,40},{40,48},{48,56},{56,64},{64,7... | collective-permute-start | bytes 198152 | tf_op jit(solution)/shard_map/ppermute | solution.py:30
  37.8 1.1 copy.83
  40.9 1.0 broadcast_multiply_fusion
  42.0 8.6 %collective-permute-done = bf16[1,129,256]{2,1,0:T(8,128)(2,1)S(1)} collective-permute-done((bf16[1,129,256]{2,1,0:T(8,128)(2,1)S(1)}, bf16[1,129,256]{2,1,0:T(8,128)(2,1)S(1)}, u32[]{:S(2)}, u32[]{:S(2)}) %collective-permute-start) | collective-permute-done | bytes 66080 | tf_op jit(solution)/shard_map/ppermute | solution.py:30
  50.7 1.9 collective-permute-start.2
  53.2 5.2 %collective-permute-start.1 = (bf16[2,129,256]{2,1,0:T(8,128)(2,1)S(1)}, bf16[2,129,256]{2,1,0:T(8,128)(2,1)S(1)}, u32[]{:S(2)}, u32[]{:S(2)}) collective-permute-start(bf16[2,129,256]{2,1,0:T(8,128)(2,1)S(1)} %pad_maximum_fusion.4), channel_id=1, source_target_pairs={{0,64},{8,72},{16,80},{24,88},{32,96},{40,104},{48,112},{56,120},{... | collective-permute-start | bytes 396296 | tf_op jit(solution)/shard_map/ppermute | solution.py:30
  59.0 4.3 %collective-permute-done.2 = bf16[2,129,256]{2,1,0:T(8,128)(2,1)S(1)} collective-permute-done((bf16[2,129,256]{2,1,0:T(8,128)(2,1)S(1)}, bf16[2,129,256]{2,1,0:T(8,128)(2,1)S(1)}, u32[]{:S(2)}, u32[]{:S(2)}) %collective-permute-start.2) | collective-permute-done | bytes 132128 | tf_op jit(solution)/shard_map/ppermute | solution.py:30
  63.3 1.1 collective-permute-done.1
  64.4 1.0 collective-permute-start.9
  67.7 5.5 %collective-permute-start.3 = (bf16[4,129,256]{2,1,0:T(8,128)(2,1)S(1)}, bf16[4,129,256]{2,1,0:T(8,128)(2,1)S(1)}, u32[]{:S(2)}, u32[]{:S(2)}) collective-permute-start(bf16[4,129,256]{2,1,0:T(8,128)(2,1)S(1)} %pad_maximum_fusion.1), channel_id=1, source_target_pairs={{0,32},{8,40},{16,48},{24,56},{32,64},{40,72},{48,80},{56,88},{64,... | collective-permute-start | bytes 792584 | tf_op jit(solution)/shard_map/ppermute | solution.py:30
  75.4 0.8 collective-permute-done.9
  76.9 3.6 %collective-permute-done.10 = bf16[128,1024]{0,1:T(8,128)(2,1)S(1)} collective-permute-done((bf16[128,1024]{0,1:T(8,128)(2,1)S(1)}, bf16[128,1024]{0,1:T(8,128)(2,1)S(1)}, u32[]{:S(2)}, u32[]{:S(2)}) %collective-permute-start.10) | collective-permute-done | bytes 262176 | tf_op jit(solution)/shard_map/ppermute | solution.py:137
  87.0 2.7 %constant_dynamic-slice_fusion = bf16[128,32,8,32]{0,3,1,2:T(8,128)(2,1)S(1)} fusion(bf16[128,32,16,32]{0,3,1,2:T(8,128)(2,1)} %constant_dynamic-update-slice_fusion.5, s32[]{:T(128)S(6)} %select_n.201), kind=kLoop, calls=%fused_computation.110 | loop fusion | bytes 4194308 | tf_op jit(solution)/shard_map/jit(_roll_dynamic)/dynamic_slice | solution.py:140
  89.7 1.9 copy.96
  92.1 1.4 or_and_fusion
  93.6 4.2 %exponential_reduce_fusion = (f32[8,128]{1,0:T(8,128)S(1)}, f32[8,128,1280]{1,2,0:T(8,128)}) fusion(bf16[1280,128,1]{1,0,2:T(8,128)(2,1)S(1)} %bitcast.123, pred[128,1280]{0,1:T(8,128)(4,1)S(1)} %or_and_fusion, bf16[128,8,64]{2,0,1:T(8,128)(2,1)S(1)} %get-tuple-element.33, bf16[128,8,64]{2,0,1:T(8,128)(2,1)S(1)} %get-tuple-element.32), kind=kOutput, calls=%fused_computation.7 | convolution fusion | flops 341312768 | bytes 6000640 | tf_op jit(solution)/shard_map/sub | solution.py:166
  97.8 3.2 %divide_convert_fusion = bf16[8,128,1280]{1,2,0:T(8,128)(2,1)S(1)} fusion(f32[8,128,1280]{1,2,0:T(8,128)} %get-tuple-element.51, f32[8,128]{1,0:T(8,128)S(1)} %get-tuple-element.50), kind=kLoop, calls=%fused_computation.6 | loop fusion | flops 2621440 | bytes 7868416 | tf_op jit(solution)/shard_map/convert_element_type | solution.py:167
  100.9 69.2 %all-gather.2.cloned.1.call-done = bf16[1024,8192]{0,1:T(8,128)(2,1)} async-done(((bf16[1024,256]{0,1:T(8,128)(2,1)}), bf16[1024,8192]{0,1:T(8,128)(2,1)}) %all-gather.2.cloned.1.call-update) | async-done | bytes 16777232 | tf_op jit(solution)/shard_map/all_gather | solution.py:134
  170.1 9.5 %convolution_convert_fusion.1 = bf16[128,1024]{1,0:T(8,128)(2,1)} fusion(bf16[128,8192]{0,1:T(8,128)(2,1)} %bitcast.111, bf16[1024,8192]{0,1:T(8,128)(2,1)} %all-gather.2.cloned.1.call-done), kind=kOutput, calls=%fused_computation.16 | convolution fusion | flops 2147614720 | bytes 19136512 | tf_op jit(solution)/shard_map/dot_general | solution.py:142
  179.6 1.1 copy.98
  180.7 1.3 multiply_reduce_fusion
  182.0 1.0 convolution_bitcast_fusion
  183.0 0.8 fusion.3
  183.8 1.5 copy-done
  185.3 1.1 fusion.4
  187.0 0.8 slice.125
  188.5 1.9 collective-permute-start.11
  190.4 3.0 %collective-permute-start.13 = (bf16[2,128,256]{2,1,0:T(8,128)(2,1)}, bf16[2,128,256]{2,1,0:T(8,128)(2,1)}, u32[]{:S(2)}, u32[]{:S(2)}) collective-permute-start(bf16[2,128,256]{2,1,0:T(8,128)(2,1)} %slice.128), channel_id=1, source_target_pairs={{64,0},{72,8},{80,16},{88,24},{96,32},{104,40},{112,48},{120,56},{... | collective-permute-start | bytes 393224 | tf_op jit(solution)/shard_map/ppermute | solution.py:30
  193.4 8.3 %fusion.31 = f32[128,8192]{0,1:S(1)} fusion(bf16[1024,8192]{0,1:T(8,128)(2,1)} %all-gather.2.cloned.1.call-done, bf16[128,1024]{0,1:T(8,128)(2,1)S(1)} %bitcast.125), kind=kOutput, calls=%fused_computation.119 | convolution fusion | flops 2147483648 | bytes 21233664
  202.3 1.8 copy.105
  204.1 4.5 %all-to-all-start.1 = ((bf16[8,128,32,32]{1,3,2,0:T(8,128)(2,1)}), bf16[8,128,32,32]{1,3,2,0:T(8,128)(2,1)}, u32[]{:S(2)}, u32[]{:S(2)}) async-start(bf16[8,128,32,32]{1,3,2,0:T(8,128)(2,1)} %copy.105), calls=%async_computation.1 | async-start | bytes 4194304 | tf_op jit(solution)/shard_map/all_to_all | solution.py:186
  208.6 1.1 fusion.5
  209.8 1.1 convert_add_fusion
  210.9 2.4 collective-permute-start.12
  213.6 21.9 %collective-permute-done.12 = bf16[2,128,256]{2,1,0:T(8,128)(2,1)S(1)} collective-permute-done((bf16[2,128,256]{2,1,0:T(8,128)(2,1)S(1)}, bf16[2,128,256]{2,1,0:T(8,128)(2,1)S(1)}, u32[]{:S(2)}, u32[]{:S(2)}) %collective-permute-start.12) | collective-permute-done | bytes 131104 | tf_op jit(solution)/shard_map/ppermute | solution.py:30
  235.5 0.9 fusion.6
  236.5 3.6 %collective-permute-start.14 = (bf16[1,128,256]{2,1,0:T(8,128)(2,1)S(1)}, bf16[1,128,256]{2,1,0:T(8,128)(2,1)S(1)}, u32[]{:S(2)}, u32[]{:S(2)}) collective-permute-start(bf16[1,128,256]{2,1,0:T(8,128)(2,1)S(1)} %slice.181), channel_id=1, source_target_pairs={{8,0},{16,8},{24,16},{32,24},{40,32},{48,40},{56,48},{64,56},{72,6... | collective-permute-start | bytes 196616 | tf_op jit(solution)/shard_map/ppermute | solution.py:30
  240.4 0.9 copy.111
  241.3 2.3 collective-permute-done.14
  245.4 2.0 reduce_sum.32
  247.3 0.9 copy.110
  (135 shorter events, 22.0 us)
Async XLA Ops:
  7.2 32.2 %copy-start.31 = (s32[1,32]{1,0:T(1,128)S(1)}, s32[1,32]{1,0:T(1,128)}, u32[]{:S(2)}) copy-start(s32[1,32]{1,0:T(1,128)} %param.16) | copy-start | bytes 388
  7.2 162.9 %all-gather.2.cloned.1.call-start = ((), (), s32[]{:S(2)}) async-start(), calls=%async_computation.2 | async-start | bytes 17301504 | tf_op jit(solution)/shard_map/all_gather | solution.py:134
  23.1 41.3 %collective-permute-start.4 = (bf16[128,1024]{0,1:T(8,128)(2,1)S(1)}, bf16[128,1024]{0,1:T(8,128)(2,1)S(1)}, u32[]{:S(2)}, u32[]{:S(2)}) collective-permute-start(bf16[128,1024]{0,1:T(8,128)(2,1)S(1)} %copy.88), channel_id=1, source_target_pairs={{0,7},{1,0},{2,1},{3,2},{4,3},{5,4},{6,5},{7,6},{8,15},{9,8},{10,9... | collective-permute-start | bytes 786440 | tf_op jit(solution)/shard_map/ppermute | solution.py:137
  25.0 41.2 %collective-permute-start.5 = (bf16[128,1024]{0,1:T(8,128)(2,1)S(1)}, bf16[128,1024]{0,1:T(8,128)(2,1)S(1)}, u32[]{:S(2)}, u32[]{:S(2)}) collective-permute-start(bf16[128,1024]{0,1:T(8,128)(2,1)S(1)} %copy.88), channel_id=1, source_target_pairs={{0,6},{1,7},{2,0},{3,1},{4,2},{5,3},{6,4},{7,5},{8,14},{9,15},{10,... | collective-permute-start | bytes 786440 | tf_op jit(solution)/shard_map/ppermute | solution.py:137
  26.2 41.5 %collective-permute-start.6 = (bf16[128,1024]{0,1:T(8,128)(2,1)S(1)}, bf16[128,1024]{0,1:T(8,128)(2,1)S(1)}, u32[]{:S(2)}, u32[]{:S(2)}) collective-permute-start(bf16[128,1024]{0,1:T(8,128)(2,1)S(1)} %copy.88), channel_id=1, source_target_pairs={{0,5},{1,6},{2,7},{3,0},{4,1},{5,2},{6,3},{7,4},{8,13},{9,14},{10,... | collective-permute-start | bytes 786440 | tf_op jit(solution)/shard_map/ppermute | solution.py:137
  27.5 23.1 %copy-start.20 = (pred[64]{0:T(512)(128)(4,1)}, pred[64]{0:T(512)(128)(4,1)S(1)}, u32[]{:S(2)}) copy-start(pred[64]{0:T(512)(128)(4,1)S(1)} %broadcast_compare_fusion.2) | copy-start | bytes 196
  27.6 23.1 %copy-start.22 = (f32[64]{0:T(128)}, f32[64]{0:T(128)S(1)}, u32[]{:S(2)}) copy-start(f32[64]{0:T(128)S(1)} %multiply_exponential_fusion) | copy-start | bytes 772
  27.6 23.0 %copy-start.24 = (pred[64]{0:T(512)(128)(4,1)}, pred[64]{0:T(512)(128)(4,1)S(1)}, u32[]{:S(2)}) copy-start(pred[64]{0:T(512)(128)(4,1)S(1)} %get-tuple-element.54) | copy-start | bytes 196
  27.6 23.0 %copy-start.26 = (pred[64]{0:T(512)(128)(4,1)}, pred[64]{0:T(512)(128)(4,1)S(1)}, u32[]{:S(2)}) copy-start(pred[64]{0:T(512)(128)(4,1)S(1)} %get-tuple-element.55) | copy-start | bytes 196
  28.9 21.7 %copy-start.12 = (f32[128]{0:T(128)}, f32[128]{0:T(128)S(1)}, u32[]{:S(2)}) copy-start(f32[128]{0:T(128)S(1)} %get-tuple-element.47) | copy-start | bytes 1540
  28.9 21.7 %copy-start.14 = (f32[128]{0:T(128)}, f32[128]{0:T(128)S(1)}, u32[]{:S(2)}) copy-start(f32[128]{0:T(128)S(1)} %get-tuple-element.48) | copy-start | bytes 1540
  28.9 21.7 %copy-start.16 = (f32[128]{0:T(128)}, f32[128]{0:T(128)S(1)}, u32[]{:S(2)}) copy-start(f32[128]{0:T(128)S(1)} %get-tuple-element.49) | copy-start | bytes 1540
  30.9 19.7 %collective-permute-start = (bf16[1,129,256]{2,1,0:T(8,128)(2,1)S(1)}, bf16[1,129,256]{2,1,0:T(8,128)(2,1)S(1)}, u32[]{:S(2)}, u32[]{:S(2)}) collective-permute-start(bf16[1,129,256]{2,1,0:T(8,128)(2,1)S(1)} %fusion.10), channel_id=1, source_target_pairs={{0,8},{8,16},{16,24},{24,32},{32,40},{40,48},{48,56},{56,64},{64,7... | collective-permute-start | bytes 198152 | tf_op jit(solution)/shard_map/ppermute | solution.py:30
  41.8 8.8 %copy-start.8 = (f32[128,64]{1,0:T(8,128)}, f32[128,64]{1,0:T(8,128)S(1)}, u32[]{:S(2)}) copy-start(f32[128,64]{1,0:T(8,128)S(1)} %get-tuple-element.46) | copy-start | bytes 98308
  42.0 51.5 %copy-start.4 = (bf16[128,8,64]{2,0,1:T(8,128)(2,1)}, bf16[128,8,64]{2,0,1:T(8,128)(2,1)S(1)}, u32[]{:S(2)}) copy-start(bf16[128,8,64]{2,0,1:T(8,128)(2,1)S(1)} %get-tuple-element.32) | copy-start | bytes 393220
  42.0 51.5 %copy-start.6 = (bf16[128,8,64]{2,0,1:T(8,128)(2,1)}, bf16[128,8,64]{2,0,1:T(8,128)(2,1)S(1)}, u32[]{:S(2)}) copy-start(bf16[128,8,64]{2,0,1:T(8,128)(2,1)S(1)} %get-tuple-element.33) | copy-start | bytes 393220
  50.7 12.6 %collective-permute-start.2 = (bf16[2,129,256]{2,1,0:T(8,128)(2,1)S(1)}, bf16[2,129,256]{2,1,0:T(8,128)(2,1)S(1)}, u32[]{:S(2)}, u32[]{:S(2)}) collective-permute-start(bf16[2,129,256]{2,1,0:T(8,128)(2,1)S(1)} %pad_maximum_fusion.4), channel_id=1, source_target_pairs={{0,16},{8,24},{16,32},{24,40},{32,48},{40,56},{48,64},{56,72},{64,... | collective-permute-start | bytes 396296 | tf_op jit(solution)/shard_map/ppermute | solution.py:30
  53.2 11.2 %collective-permute-start.1 = (bf16[2,129,256]{2,1,0:T(8,128)(2,1)S(1)}, bf16[2,129,256]{2,1,0:T(8,128)(2,1)S(1)}, u32[]{:S(2)}, u32[]{:S(2)}) collective-permute-start(bf16[2,129,256]{2,1,0:T(8,128)(2,1)S(1)} %pad_maximum_fusion.4), channel_id=1, source_target_pairs={{0,64},{8,72},{16,80},{24,88},{32,96},{40,104},{48,112},{56,120},{... | collective-permute-start | bytes 396296 | tf_op jit(solution)/shard_map/ppermute | solution.py:30
  63.3 10.6 %collective-permute-start.7 = (bf16[128,1024]{0,1:T(8,128)(2,1)S(1)}, bf16[128,1024]{0,1:T(8,128)(2,1)S(1)}, u32[]{:S(2)}, u32[]{:S(2)}) collective-permute-start(bf16[128,1024]{0,1:T(8,128)(2,1)S(1)} %copy.88), channel_id=1, source_target_pairs={{0,4},{1,5},{2,6},{3,7},{4,0},{5,1},{6,2},{7,3},{8,12},{9,13},{10,... | collective-permute-start | bytes 786440 | tf_op jit(solution)/shard_map/ppermute | solution.py:137
  64.4 10.2 %collective-permute-start.8 = (bf16[128,1024]{0,1:T(8,128)(2,1)S(1)}, bf16[128,1024]{0,1:T(8,128)(2,1)S(1)}, u32[]{:S(2)}, u32[]{:S(2)}) collective-permute-start(bf16[128,1024]{0,1:T(8,128)(2,1)S(1)} %copy.88), channel_id=1, source_target_pairs={{0,3},{1,4},{2,5},{3,6},{4,7},{5,0},{6,1},{7,2},{8,11},{9,12},{10,... | collective-permute-start | bytes 786440 | tf_op jit(solution)/shard_map/ppermute | solution.py:137
  64.4 11.7 %collective-permute-start.9 = (bf16[128,1024]{0,1:T(8,128)(2,1)S(1)}, bf16[128,1024]{0,1:T(8,128)(2,1)S(1)}, u32[]{:S(2)}, u32[]{:S(2)}) collective-permute-start(bf16[128,1024]{0,1:T(8,128)(2,1)S(1)} %copy.88), channel_id=1, source_target_pairs={{0,2},{1,3},{2,4},{3,5},{4,6},{5,7},{6,0},{7,1},{8,10},{9,11},{10,... | collective-permute-start | bytes 786440 | tf_op jit(solution)/shard_map/ppermute | solution.py:137
  66.2 14.3 %collective-permute-start.10 = (bf16[128,1024]{0,1:T(8,128)(2,1)S(1)}, bf16[128,1024]{0,1:T(8,128)(2,1)S(1)}, u32[]{:S(2)}, u32[]{:S(2)}) collective-permute-start(bf16[128,1024]{0,1:T(8,128)(2,1)S(1)} %copy.88), channel_id=1, source_target_pairs={{0,1},{1,2},{2,3},{3,4},{4,5},{5,6},{6,7},{7,0},{8,9},{9,10},{10,1... | collective-permute-start | bytes 786440 | tf_op jit(solution)/shard_map/ppermute | solution.py:137
  67.7 24.0 %collective-permute-start.3 = (bf16[4,129,256]{2,1,0:T(8,128)(2,1)S(1)}, bf16[4,129,256]{2,1,0:T(8,128)(2,1)S(1)}, u32[]{:S(2)}, u32[]{:S(2)}) collective-permute-start(bf16[4,129,256]{2,1,0:T(8,128)(2,1)S(1)} %pad_maximum_fusion.1), channel_id=1, source_target_pairs={{0,32},{8,40},{16,48},{24,56},{32,64},{40,72},{48,80},{56,88},{64,... | collective-permute-start | bytes 792584 | tf_op jit(solution)/shard_map/ppermute | solution.py:30
  87.0 4.8 %copy-start.11 = (bf16[128,128]{1,0:T(8,128)(2,1)S(1)}, bf16[128,128]{1,0:T(8,128)(2,1)}, u32[]{:S(2)}) copy-start(bf16[128,128]{1,0:T(8,128)(2,1)} %param.12) | copy-start | bytes 98308
  89.7 2.4 copy-start.18
  89.7 2.4 copy-start.19
  89.7 2.4 copy-start.28
  89.7 2.4 copy-start.29
  89.7 2.4 copy-start.30
  182.9 2.4 copy-start.5
  182.9 2.3 copy-start.7
  186.4 7.1 %copy-start.3 = (bf16[128,8,128]{2,0,1:T(8,128)(2,1)S(1)}, bf16[128,8,128]{2,0,1:T(8,128)(2,1)}, u32[]{:S(2)}) copy-start(bf16[128,8,128]{2,0,1:T(8,128)(2,1)} %get-tuple-element.53) | copy-start | bytes 786436
  186.9 14.8 %copy-start.2 = (f32[1280,256]{1,0:T(8,128)}, f32[1280,256]{1,0:T(8,128)S(1)}, u32[]{:S(2)}) copy-start(f32[1280,256]{1,0:T(8,128)S(1)} %copy.103) | copy-start | bytes 3932164
  188.5 21.3 %collective-permute-start.11 = (bf16[4,128,256]{2,1,0:T(8,128)(2,1)}, bf16[4,128,256]{2,1,0:T(8,128)(2,1)S(1)}, u32[]{:S(2)}, u32[]{:S(2)}) collective-permute-start(bf16[4,128,256]{2,1,0:T(8,128)(2,1)} %slice.125), channel_id=1, source_target_pairs={{32,0},{40,8},{48,16},{56,24},{64,32},{72,40},{80,48},{88,56},{96,... | collective-permute-start | bytes 786440 | tf_op jit(solution)/shard_map/ppermute | solution.py:30
  190.4 23.2 %collective-permute-start.13 = (bf16[2,128,256]{2,1,0:T(8,128)(2,1)}, bf16[2,128,256]{2,1,0:T(8,128)(2,1)}, u32[]{:S(2)}, u32[]{:S(2)}) collective-permute-start(bf16[2,128,256]{2,1,0:T(8,128)(2,1)} %slice.128), channel_id=1, source_target_pairs={{64,0},{72,8},{80,16},{88,24},{96,32},{104,40},{112,48},{120,56},{... | collective-permute-start | bytes 393224 | tf_op jit(solution)/shard_map/ppermute | solution.py:30
  202.3 6.3 %copy-start.1 = (bf16[8,128,1280]{1,2,0:T(8,128)(2,1)S(1)}, bf16[8,128,1280]{1,2,0:T(8,128)(2,1)}, u32[]{:S(2)}) copy-start(bf16[8,128,1280]{1,2,0:T(8,128)(2,1)} %copy-done) | copy-start | bytes 7864324
  204.1 9.3 %copy-start.9 = (f32[128,64]{1,0:T(8,128)S(1)}, f32[128,64]{1,0:T(8,128)}, u32[]{:S(2)}) copy-start(f32[128,64]{1,0:T(8,128)} %copy-done.8) | copy-start | bytes 98308
  204.1 9.3 %copy-start.10 = (f32[128,64]{1,0:T(8,128)S(1)}, f32[128,64]{1,0:T(8,128)}, u32[]{:S(2)}) copy-start(f32[128,64]{1,0:T(8,128)} %get-tuple-element.44) | copy-start | bytes 98308
  204.1 41.3 %all-to-all-start.1 = ((bf16[8,128,32,32]{1,3,2,0:T(8,128)(2,1)}), bf16[8,128,32,32]{1,3,2,0:T(8,128)(2,1)}, u32[]{:S(2)}, u32[]{:S(2)}) async-start(bf16[8,128,32,32]{1,3,2,0:T(8,128)(2,1)} %copy.105), calls=%async_computation.1 | async-start | bytes 4194304 | tf_op jit(solution)/shard_map/all_to_all | solution.py:186
  208.6 35.6 %copy-start.13 = (f32[128]{0:T(128)S(1)}, f32[128]{0:T(128)}, u32[]{:S(2)}) copy-start(f32[128]{0:T(128)} %copy-done.12) | copy-start | bytes 1540
  208.6 35.6 %copy-start.15 = (f32[128]{0:T(128)S(1)}, f32[128]{0:T(128)}, u32[]{:S(2)}) copy-start(f32[128]{0:T(128)} %copy-done.14) | copy-start | bytes 1540
  208.6 35.6 %copy-start.17 = (f32[128]{0:T(128)S(1)}, f32[128]{0:T(128)}, u32[]{:S(2)}) copy-start(f32[128]{0:T(128)} %copy-done.16) | copy-start | bytes 1540
  208.6 35.6 %copy-start.21 = (pred[64]{0:T(512)(128)(4,1)S(1)}, pred[64]{0:T(512)(128)(4,1)}, u32[]{:S(2)}) copy-start(pred[64]{0:T(512)(128)(4,1)} %copy-done.20) | copy-start | bytes 196
  209.7 34.5 %copy-start.23 = (f32[64]{0:T(128)S(1)}, f32[64]{0:T(128)}, u32[]{:S(2)}) copy-start(f32[64]{0:T(128)} %copy-done.22) | copy-start | bytes 772
  209.8 34.5 %copy-start.25 = (pred[64]{0:T(512)(128)(4,1)S(1)}, pred[64]{0:T(512)(128)(4,1)}, u32[]{:S(2)}) copy-start(pred[64]{0:T(512)(128)(4,1)} %copy-done.24) | copy-start | bytes 196
  209.8 34.5 %copy-start.27 = (pred[64]{0:T(512)(128)(4,1)S(1)}, pred[64]{0:T(512)(128)(4,1)}, u32[]{:S(2)}) copy-start(pred[64]{0:T(512)(128)(4,1)} %copy-done.26) | copy-start | bytes 196
  210.9 24.6 %collective-permute-start.12 = (bf16[2,128,256]{2,1,0:T(8,128)(2,1)S(1)}, bf16[2,128,256]{2,1,0:T(8,128)(2,1)S(1)}, u32[]{:S(2)}, u32[]{:S(2)}) collective-permute-start(bf16[2,128,256]{2,1,0:T(8,128)(2,1)S(1)} %slice.180), channel_id=1, source_target_pairs={{16,0},{24,8},{32,16},{40,24},{48,32},{56,40},{64,48},{72,56},{80,... | collective-permute-start | bytes 393224 | tf_op jit(solution)/shard_map/ppermute | solution.py:30
  236.5 7.1 %collective-permute-start.14 = (bf16[1,128,256]{2,1,0:T(8,128)(2,1)S(1)}, bf16[1,128,256]{2,1,0:T(8,128)(2,1)S(1)}, u32[]{:S(2)}, u32[]{:S(2)}) collective-permute-start(bf16[1,128,256]{2,1,0:T(8,128)(2,1)S(1)} %slice.181), channel_id=1, source_target_pairs={{8,0},{16,8},{24,16},{32,24},{40,32},{48,40},{56,48},{64,56},{72,6... | collective-permute-start | bytes 196616 | tf_op jit(solution)/shard_map/ppermute | solution.py:30
  (1 other events, 1.5 us)
Sparse Core Ops, SparseCore 0:
  22.1 147.9 all-gather.1

commit v4 on v2

--- a/solution.py
+++ b/solution.py
@@ -100,11 +100,14 @@
 
 
 def return_window(pieces):
-    total = pieces[REACH]
-    for reach in range(1, REACH + 1):
-        back = shifted(pieces[REACH - reach].astype(jnp.bfloat16), -reach)
-        total = total + back.astype(jnp.float32)
-    return total
+    def send(block, distance):
+        return shifted(block.astype(jnp.bfloat16), -distance).astype(jnp.float32)
+
+    acc = pieces[REACH - 2 : REACH + 1][::-1]
+    acc = acc + send(pieces[REACH - 5 : REACH - 2][::-1], 3)
+    acc = acc + send(pieces[REACH - 8 : REACH - 5][::-1], 6)
+    first = acc[0] + send(pieces[REACH - 9 : REACH - 8], 9)[0]
+    return first + send(acc[1], 1) + send(acc[2], 2)
 
 
 def per_device(queries, keys, values, out_weight, out_grad, doc_ids, block_mask, positions):

time: 281 us -> 276 us (0.982)
  the two profiles are of different devices: /device:TPU:233 before, /device:TPU:184 now
where the time goes in v4:
time: 276 us; the launch traced here: 275 us
  waiting for transfers between devices  111 us (40%)
  starting transfers between devices  54.5 us (20%)
  local copies, waits for them, and re-layouts  36.3 us (13%)
  matrix products  27.5 us (10%)
  other arithmetic  17.7 us (6%)
  between operations  14.7 us (5%)
  blocking collectives  13.2 us (5%)
    all_gather x1, waiting for transfers between devices, per_device(): stripes = lax.all_gather(pieces, SEQ, axis=1, tiled=True)  67.1 us
    ppermute x9, starting transfers between devices, shifted(): return lax.ppermute(block, SEQ, route)  29.7 us
    ppermute x7, waiting for transfers between devices, per_device(): lax.ppermute(piece, 'kv', [(i, (i + j) % kv_count) for i in range(kv_coun...  23.3 us
    ppermute x9, waiting for transfers between devices, shifted(): return lax.ppermute(block, SEQ, route)  20.1 us
    ppermute x7, starting transfers between devices, per_device(): lax.ppermute(out_grad, 'kv', [(i, (i - j) % kv_count) for i in range(kv_c...  18.3 us
    unnamed x57, local copies, waits for them, and re-layouts  16.8 us
    all_to_all x1, blocking collectives, per_device(): lax.all_to_all(out_weight, 'kv', split_axis=0, concat_axis=1, tiled=True)  13.2 us
    dot_general x1, matrix products, per_device(): lax.dot_general(og_perm, stripes, contract, preferred_element_type=jnp.fl...  8.76 us
  transfers between devices with their start and end apart: 24, of which 10 were waited for; matrix products, arithmetic and copies ran while one was open for 18% of the time, Pallas kernels for 0%

profile of v4, /device:TPU:184, one launch (start us, length us, event | category | flops | bytes accessed | tf_op | source)
XLA Modules:
  0.0 275.1 jit_solution(5830683781123552491)
XLA Ops:
  8.3 13.2 %all_to_all.19 = bf16[8,1024,32]{1,2,0:T(8,128)(2,1)} all-to-all(bf16[8,1024,32]{1,2,0:T(8,128)(2,1)S(1)} %bitcast.146), channel_id=1, replica_groups=mesh['sz'=16,'core'=2,'kv'=8] {'kv'}, dimensions={0} | all-to-all | bytes 1048576 | tf_op jit(solution)/shard_map/all_to_all | solution.py:136
  21.5 1.1 copy.90
  23.4 3.2 %collective-permute-start.5 = (bf16[128,1024]{0,1:T(8,128)(2,1)S(1)}, bf16[128,1024]{0,1:T(8,128)(2,1)S(1)}, u32[]{:S(2)}, u32[]{:S(2)}) collective-permute-start(bf16[128,1024]{0,1:T(8,128)(2,1)S(1)} %copy.90), channel_id=1, source_target_pairs={{0,6},{1,7},{2,0},{3,1},{4,2},{5,3},{6,4},{7,5},{8,14},{9,15},{10,... | collective-permute-start | bytes 786440 | tf_op jit(solution)/shard_map/ppermute | solution.py:140
  26.6 1.5 collective-permute-start.6
  29.4 1.3 fusion.33
  32.7 1.9 collective-permute-start
  34.7 1.1 copy.85
  38.4 3.8 %collective-permute-done = bf16[1,129,256]{2,1,0:T(8,128)(2,1)S(1)} collective-permute-done((bf16[1,129,256]{2,1,0:T(8,128)(2,1)S(1)}, bf16[1,129,256]{2,1,0:T(8,128)(2,1)S(1)}, u32[]{:S(2)}, u32[]{:S(2)}) %collective-permute-start) | collective-permute-done | bytes 66080 | tf_op jit(solution)/shard_map/ppermute | solution.py:30
  42.2 4.0 %collective-permute-start.2 = (bf16[2,129,256]{2,1,0:T(8,128)(2,1)S(1)}, bf16[2,129,256]{2,1,0:T(8,128)(2,1)S(1)}, u32[]{:S(2)}, u32[]{:S(2)}) collective-permute-start(bf16[2,129,256]{2,1,0:T(8,128)(2,1)S(1)} %pad_maximum_fusion.4), channel_id=1, source_target_pairs={{0,16},{8,24},{16,32},{24,40},{32,48},{40,56},{48,64},{56,72},{64,... | collective-permute-start | bytes 396296 | tf_op jit(solution)/shard_map/ppermute | solution.py:30
  46.2 3.4 %collective-permute-start.1 = (bf16[2,129,256]{2,1,0:T(8,128)(2,1)S(1)}, bf16[2,129,256]{2,1,0:T(8,128)(2,1)S(1)}, u32[]{:S(2)}, u32[]{:S(2)}) collective-permute-start(bf16[2,129,256]{2,1,0:T(8,128)(2,1)S(1)} %pad_maximum_fusion.4), channel_id=1, source_target_pairs={{0,64},{8,72},{16,80},{24,88},{32,96},{40,104},{48,112},{56,120},{... | collective-permute-start | bytes 396296 | tf_op jit(solution)/shard_map/ppermute | solution.py:30
  49.7 7.0 %collective-permute-done.2 = bf16[2,129,256]{2,1,0:T(8,128)(2,1)S(1)} collective-permute-done((bf16[2,129,256]{2,1,0:T(8,128)(2,1)S(1)}, bf16[2,129,256]{2,1,0:T(8,128)(2,1)S(1)}, u32[]{:S(2)}, u32[]{:S(2)}) %collective-permute-start.2) | collective-permute-done | bytes 132128 | tf_op jit(solution)/shard_map/ppermute | solution.py:30
  57.1 3.3 %collective-permute-done.1 = bf16[2,129,256]{2,1,0:T(8,128)(2,1)S(1)} collective-permute-done((bf16[2,129,256]{2,1,0:T(8,128)(2,1)S(1)}, bf16[2,129,256]{2,1,0:T(8,128)(2,1)S(1)}, u32[]{:S(2)}, u32[]{:S(2)}) %collective-permute-start.1) | collective-permute-done | bytes 132128 | tf_op jit(solution)/shard_map/ppermute | solution.py:30
  60.4 1.4 collective-permute-start.8
  61.8 11.1 %collective-permute-start.9 = (bf16[128,1024]{0,1:T(8,128)(2,1)S(1)}, bf16[128,1024]{0,1:T(8,128)(2,1)S(1)}, u32[]{:S(2)}, u32[]{:S(2)}) collective-permute-start(bf16[128,1024]{0,1:T(8,128)(2,1)S(1)} %copy.90), channel_id=1, source_target_pairs={{0,2},{1,3},{2,4},{3,5},{4,6},{5,7},{6,0},{7,1},{8,10},{9,11},{10,... | collective-permute-start | bytes 786440 | tf_op jit(solution)/shard_map/ppermute | solution.py:140
  74.3 2.1 collective-permute-start.3
  86.5 2.6 constant_dynamic-slice_fusion
  89.2 1.9 copy.98
  91.5 1.4 or_and_fusion
  93.0 4.2 %exponential_reduce_fusion = (f32[8,128]{1,0:T(8,128)S(1)}, f32[8,128,1280]{1,2,0:T(8,128)}) fusion(bf16[1280,128,1]{1,0,2:T(8,128)(2,1)S(1)} %bitcast.147, pred[128,1280]{0,1:T(8,128)(4,1)S(1)} %or_and_fusion, bf16[128,8,64]{2,0,1:T(8,128)(2,1)S(1)} %get-tuple-element.48, bf16[128,8,64]{2,0,1:T(8,128)(2,1)S(1)} %get-tuple-element.47), kind=kOutput, calls=%fused_computation.7 | convolution fusion | flops 341312768 | bytes 6000640 | tf_op jit(solution)/shard_map/sub | solution.py:169
  97.2 3.2 %divide_convert_fusion = bf16[8,128,1280]{1,2,0:T(8,128)(2,1)S(1)} fusion(f32[8,128,1280]{1,2,0:T(8,128)} %get-tuple-element.68, f32[8,128]{1,0:T(8,128)S(1)} %get-tuple-element.67), kind=kLoop, calls=%fused_computation.6 | loop fusion | flops 2621440 | bytes 7868416 | tf_op jit(solution)/shard_map/convert_element_type | solution.py:170
  100.3 67.1 %all-gather.2.cloned.1.call-done = bf16[1024,8192]{0,1:T(8,128)(2,1)} async-done(((bf16[1024,256]{0,1:T(8,128)(2,1)}), bf16[1024,8192]{0,1:T(8,128)(2,1)}) %all-gather.2.cloned.1.call-update) | async-done | bytes 16777232 | tf_op jit(solution)/shard_map/all_gather | solution.py:137
  167.5 8.8 %convolution_convert_fusion.1 = bf16[128,1024]{1,0:T(8,128)(2,1)S(1)} fusion(bf16[128,8192]{0,1:T(8,128)(2,1)} %bitcast.134, bf16[1024,8192]{0,1:T(8,128)(2,1)} %all-gather.2.cloned.1.call-done), kind=kOutput, calls=%fused_computation.15 | convolution fusion | flops 2147614720 | bytes 19136512 | tf_op jit(solution)/shard_map/dot_general | solution.py:145
  176.4 1.3 multiply_reduce_fusion
  179.5 1.5 copy-done
  181.0 1.1 fusion.4
  182.1 1.2 pad_maximum_fusion
  183.3 2.9 %copy.105 = f32[1280,256]{1,0:T(8,128)} copy(f32[1280,256]{0,1:T(8,128)} %pad_maximum_fusion) | data formatting | bytes 2621440 | tf_op jit(solution)/shard_map/concatenate | solution.py:181
  186.1 1.9 fusion.38
  189.1 1.5 slice.175
  190.6 2.1 fusion.5
  192.7 1.6 rev.16
  194.4 2.4 collective-permute-start.18
  196.7 1.6 rev.15
  198.4 4.1 %collective-permute-start.19 = (bf16[3,128,256]{2,1,0:T(8,128)(2,1)}, bf16[3,128,256]{2,1,0:T(8,128)(2,1)S(1)}, u32[]{:S(2)}, u32[]{:S(2)}) collective-permute-start(bf16[3,128,256]{2,1,0:T(8,128)(2,1)} %rev.15), channel_id=1, source_target_pairs={{48,0},{56,8},{64,16},{72,24},{80,32},{88,40},{96,48},{104,56},{11... | collective-permute-start | bytes 589832 | tf_op jit(solution)/shard_map/ppermute | solution.py:30
  202.4 5.4 %collective-permute-start.20 = (bf16[1,128,256]{2,1,0:T(8,128)(2,1)}, bf16[1,128,256]{2,1,0:T(8,128)(2,1)}, u32[]{:S(2)}, u32[]{:S(2)}) collective-permute-start(bf16[1,128,256]{2,1,0:T(8,128)(2,1)} %slice.175), channel_id=1, source_target_pairs={{72,0},{80,8},{88,16},{96,24},{104,32},{112,40},{120,48},{128,56},... | collective-permute-start | bytes 196616 | tf_op jit(solution)/shard_map/ppermute | solution.py:30
  207.8 8.3 %fusion.41 = f32[128,8192]{0,1:S(1)} fusion(bf16[1024,8192]{0,1:T(8,128)(2,1)} %all-gather.2.cloned.1.call-done, bf16[128,1024]{0,1:T(8,128)(2,1)} %bitcast.149), kind=kOutput, calls=%fused_computation.139 | convolution fusion | flops 2147483648 | bytes 21233664
  216.7 1.3 dynamic-slice_bitcast_fusion.6
  218.0 1.4 collective-permute-start.11
  219.4 2.4 collective-permute-start.12
  223.1 1.9 collective-permute-start.21
  225.0 4.6 %collective-permute-start.22 = (bf16[128,256]{1,0:T(8,128)(2,1)S(1)}, bf16[128,256]{1,0:T(8,128)(2,1)S(1)}, u32[]{:S(2)}, u32[]{:S(2)}) collective-permute-start(bf16[128,256]{1,0:T(8,128)(2,1)S(1)} %get-tuple-element.56), channel_id=1, source_target_pairs={{16,0},{24,8},{32,16},{40,24},{48,32},{56,40},{64,48},{72,56},{80,... | collective-permute-start | bytes 196616 | tf_op jit(solution)/shard_map/ppermute | solution.py:30
  230.8 1.4 collective-permute-start.14
  232.2 6.0 %collective-permute-done.22 = bf16[128,256]{1,0:T(8,128)(2,1)S(1)} collective-permute-done((bf16[128,256]{1,0:T(8,128)(2,1)S(1)}, bf16[128,256]{1,0:T(8,128)(2,1)S(1)}, u32[]{:S(2)}, u32[]{:S(2)}) %collective-permute-start.22) | collective-permute-done | bytes 65568 | tf_op jit(solution)/shard_map/ppermute | solution.py:30
  239.2 1.1 collective-permute-start.17
  242.1 4.8 %collective-permute-done.14 = bf16[128,32,32]{0,2,1:T(8,128)(2,1)S(1)} collective-permute-done((bf16[128,32,32]{0,2,1:T(8,128)(2,1)}, bf16[128,32,32]{0,2,1:T(8,128)(2,1)S(1)}, u32[]{:S(2)}, u32[]{:S(2)}) %collective-permute-start.14) | collective-permute-done | bytes 262176 | tf_op jit(solution)/shard_map/ppermute | solution.py:193
  246.9 6.4 %collective-permute-done.15 = bf16[128,32,32]{0,2,1:T(8,128)(2,1)S(1)} collective-permute-done((bf16[128,32,32]{0,2,1:T(8,128)(2,1)}, bf16[128,32,32]{0,2,1:T(8,128)(2,1)S(1)}, u32[]{:S(2)}, u32[]{:S(2)}) %collective-permute-start.15) | collective-permute-done | bytes 262176 | tf_op jit(solution)/shard_map/ppermute | solution.py:193
  253.2 11.7 %collective-permute-done.16 = bf16[128,32,32]{0,2,1:T(8,128)(2,1)S(1)} collective-permute-done((bf16[128,32,32]{0,2,1:T(8,128)(2,1)}, bf16[128,32,32]{0,2,1:T(8,128)(2,1)S(1)}, u32[]{:S(2)}, u32[]{:S(2)}) %collective-permute-start.16) | collective-permute-done | bytes 262176 | tf_op jit(solution)/shard_map/ppermute | solution.py:193
  265.4 1.3 fusion.12
  (117 shorter events, 30.8 us)
Async XLA Ops:
  7.2 29.1 %copy-start.15 = (s32[1,32]{1,0:T(1,128)S(1)}, s32[1,32]{1,0:T(1,128)}, u32[]{:S(2)}) copy-start(s32[1,32]{1,0:T(1,128)} %param.16) | copy-start | bytes 388
  7.2 160.3 %all-gather.2.cloned.1.call-start = ((), (), s32[]{:S(2)}) async-start(), calls=%async_computation.1 | async-start | bytes 17301504 | tf_op jit(solution)/shard_map/all_gather | solution.py:137
  22.6 39.2 %collective-permute-start.4 = (bf16[128,1024]{0,1:T(8,128)(2,1)S(1)}, bf16[128,1024]{0,1:T(8,128)(2,1)S(1)}, u32[]{:S(2)}, u32[]{:S(2)}) collective-permute-start(bf16[128,1024]{0,1:T(8,128)(2,1)S(1)} %copy.90), channel_id=1, source_target_pairs={{0,7},{1,0},{2,1},{3,2},{4,3},{5,4},{6,5},{7,6},{8,15},{9,8},{10,9... | collective-permute-start | bytes 786440 | tf_op jit(solution)/shard_map/ppermute | solution.py:140
  23.4 50.2 %collective-permute-start.5 = (bf16[128,1024]{0,1:T(8,128)(2,1)S(1)}, bf16[128,1024]{0,1:T(8,128)(2,1)S(1)}, u32[]{:S(2)}, u32[]{:S(2)}) collective-permute-start(bf16[128,1024]{0,1:T(8,128)(2,1)S(1)} %copy.90), channel_id=1, source_target_pairs={{0,6},{1,7},{2,0},{3,1},{4,2},{5,3},{6,4},{7,5},{8,14},{9,15},{10,... | collective-permute-start | bytes 786440 | tf_op jit(solution)/shard_map/ppermute | solution.py:140
  26.6 47.8 %collective-permute-start.6 = (bf16[128,1024]{0,1:T(8,128)(2,1)S(1)}, bf16[128,1024]{0,1:T(8,128)(2,1)S(1)}, u32[]{:S(2)}, u32[]{:S(2)}) collective-permute-start(bf16[128,1024]{0,1:T(8,128)(2,1)S(1)} %copy.90), channel_id=1, source_target_pairs={{0,5},{1,6},{2,7},{3,0},{4,1},{5,2},{6,3},{7,4},{8,13},{9,14},{10,... | collective-permute-start | bytes 786440 | tf_op jit(solution)/shard_map/ppermute | solution.py:140
  29.4 12.7 %copy-start.11 = (f32[64]{0:T(128)}, f32[64]{0:T(128)S(1)}, u32[]{:S(2)}) copy-start(f32[64]{0:T(128)S(1)} %multiply_exponential_fusion) | copy-start | bytes 772
  29.4 12.7 %copy-start.12 = (pred[64]{0:T(512)(128)(4,1)}, pred[64]{0:T(512)(128)(4,1)S(1)}, u32[]{:S(2)}) copy-start(pred[64]{0:T(512)(128)(4,1)S(1)} %get-tuple-element.71) | copy-start | bytes 196
  29.4 12.7 %copy-start.13 = (pred[64]{0:T(512)(128)(4,1)}, pred[64]{0:T(512)(128)(4,1)S(1)}, u32[]{:S(2)}) copy-start(pred[64]{0:T(512)(128)(4,1)S(1)} %get-tuple-element.72) | copy-start | bytes 196
  32.7 9.4 %collective-permute-start = (bf16[1,129,256]{2,1,0:T(8,128)(2,1)S(1)}, bf16[1,129,256]{2,1,0:T(8,128)(2,1)S(1)}, u32[]{:S(2)}, u32[]{:S(2)}) collective-permute-start(bf16[1,129,256]{2,1,0:T(8,128)(2,1)S(1)} %fusion.18), channel_id=1, source_target_pairs={{0,8},{8,16},{16,24},{24,32},{32,40},{40,48},{48,56},{56,64},{64,7... | collective-permute-start | bytes 198152 | tf_op jit(solution)/shard_map/ppermute | solution.py:30
  38.2 4.0 %copy-start.7 = (f32[128,64]{1,0:T(8,128)}, f32[128,64]{1,0:T(8,128)S(1)}, u32[]{:S(2)}) copy-start(f32[128,64]{1,0:T(8,128)S(1)} %get-tuple-element.63) | copy-start | bytes 98308
  38.3 54.6 %copy-start.3 = (bf16[128,8,64]{2,0,1:T(8,128)(2,1)}, bf16[128,8,64]{2,0,1:T(8,128)(2,1)S(1)}, u32[]{:S(2)}) copy-start(bf16[128,8,64]{2,0,1:T(8,128)(2,1)S(1)} %get-tuple-element.47) | copy-start | bytes 393220
  38.3 54.6 %copy-start.5 = (bf16[128,8,64]{2,0,1:T(8,128)(2,1)}, bf16[128,8,64]{2,0,1:T(8,128)(2,1)S(1)}, u32[]{:S(2)}) copy-start(bf16[128,8,64]{2,0,1:T(8,128)(2,1)S(1)} %get-tuple-element.48) | copy-start | bytes 393220
  42.2 14.5 %collective-permute-start.2 = (bf16[2,129,256]{2,1,0:T(8,128)(2,1)S(1)}, bf16[2,129,256]{2,1,0:T(8,128)(2,1)S(1)}, u32[]{:S(2)}, u32[]{:S(2)}) collective-permute-start(bf16[2,129,256]{2,1,0:T(8,128)(2,1)S(1)} %pad_maximum_fusion.4), channel_id=1, source_target_pairs={{0,16},{8,24},{16,32},{24,40},{32,48},{40,56},{48,64},{56,72},{64,... | collective-permute-start | bytes 396296 | tf_op jit(solution)/shard_map/ppermute | solution.py:30
  46.2 14.2 %collective-permute-start.1 = (bf16[2,129,256]{2,1,0:T(8,128)(2,1)S(1)}, bf16[2,129,256]{2,1,0:T(8,128)(2,1)S(1)}, u32[]{:S(2)}, u32[]{:S(2)}) collective-permute-start(bf16[2,129,256]{2,1,0:T(8,128)(2,1)S(1)} %pad_maximum_fusion.4), channel_id=1, source_target_pairs={{0,64},{8,72},{16,80},{24,88},{32,96},{40,104},{48,112},{56,120},{... | collective-permute-start | bytes 396296 | tf_op jit(solution)/shard_map/ppermute | solution.py:30
  56.7 20.5 %collective-permute-start.7 = (bf16[128,1024]{0,1:T(8,128)(2,1)S(1)}, bf16[128,1024]{0,1:T(8,128)(2,1)S(1)}, u32[]{:S(2)}, u32[]{:S(2)}) collective-permute-start(bf16[128,1024]{0,1:T(8,128)(2,1)S(1)} %copy.90), channel_id=1, source_target_pairs={{0,4},{1,5},{2,6},{3,7},{4,0},{5,1},{6,2},{7,3},{8,12},{9,13},{10,... | collective-permute-start | bytes 786440 | tf_op jit(solution)/shard_map/ppermute | solution.py:140
  60.4 17.5 %collective-permute-start.8 = (bf16[128,1024]{0,1:T(8,128)(2,1)S(1)}, bf16[128,1024]{0,1:T(8,128)(2,1)S(1)}, u32[]{:S(2)}, u32[]{:S(2)}) collective-permute-start(bf16[128,1024]{0,1:T(8,128)(2,1)S(1)} %copy.90), channel_id=1, source_target_pairs={{0,3},{1,4},{2,5},{3,6},{4,7},{5,0},{6,1},{7,2},{8,11},{9,12},{10,... | collective-permute-start | bytes 786440 | tf_op jit(solution)/shard_map/ppermute | solution.py:140
  61.8 16.8 %collective-permute-start.9 = (bf16[128,1024]{0,1:T(8,128)(2,1)S(1)}, bf16[128,1024]{0,1:T(8,128)(2,1)S(1)}, u32[]{:S(2)}, u32[]{:S(2)}) collective-permute-start(bf16[128,1024]{0,1:T(8,128)(2,1)S(1)} %copy.90), channel_id=1, source_target_pairs={{0,2},{1,3},{2,4},{3,5},{4,6},{5,7},{6,0},{7,1},{8,10},{9,11},{10,... | collective-permute-start | bytes 786440 | tf_op jit(solution)/shard_map/ppermute | solution.py:140
  73.6 6.4 %collective-permute-start.10 = (bf16[128,1024]{0,1:T(8,128)(2,1)S(1)}, bf16[128,1024]{0,1:T(8,128)(2,1)S(1)}, u32[]{:S(2)}, u32[]{:S(2)}) collective-permute-start(bf16[128,1024]{0,1:T(8,128)(2,1)S(1)} %copy.90), channel_id=1, source_target_pairs={{0,1},{1,2},{2,3},{3,4},{4,5},{5,6},{6,7},{7,0},{8,9},{9,10},{10,1... | collective-permute-start | bytes 786440 | tf_op jit(solution)/shard_map/ppermute | solution.py:140
  74.3 16.8 %collective-permute-start.3 = (bf16[4,129,256]{2,1,0:T(8,128)(2,1)S(1)}, bf16[4,129,256]{2,1,0:T(8,128)(2,1)S(1)}, u32[]{:S(2)}, u32[]{:S(2)}) collective-permute-start(bf16[4,129,256]{2,1,0:T(8,128)(2,1)S(1)} %pad_maximum_fusion.1), channel_id=1, source_target_pairs={{0,32},{8,40},{16,48},{24,56},{32,64},{40,72},{48,80},{56,88},{64,... | collective-permute-start | bytes 792584 | tf_op jit(solution)/shard_map/ppermute | solution.py:30
  86.5 4.7 %copy-start.10 = (bf16[128,128]{1,0:T(8,128)(2,1)S(1)}, bf16[128,128]{1,0:T(8,128)(2,1)}, u32[]{:S(2)}) copy-start(bf16[128,128]{1,0:T(8,128)(2,1)} %param.12) | copy-start | bytes 98308
  89.2 2.3 copy-start.14
  91.5 5.7 %copy-start.2 = (bf16[10,128,128]{2,1,0:T(8,128)(2,1)}, bf16[10,128,128]{2,1,0:T(8,128)(2,1)S(1)}, u32[]{:S(2)}) copy-start(bf16[10,128,128]{2,1,0:T(8,128)(2,1)S(1)} %get-tuple-element.49) | copy-start | bytes 983044
  178.7 2.3 copy-start.4
  178.7 2.3 copy-start.6
  179.5 1.5 copy-start
  182.1 8.6 %copy-start.1 = (bf16[8,128,1280]{1,2,0:T(8,128)(2,1)S(1)}, bf16[8,128,1280]{1,2,0:T(8,128)(2,1)}, u32[]{:S(2)}) copy-start(bf16[8,128,1280]{1,2,0:T(8,128)(2,1)} %copy-done) | copy-start | bytes 7864324
  194.4 27.7 %collective-permute-start.18 = (bf16[3,128,256]{2,1,0:T(8,128)(2,1)}, bf16[3,128,256]{2,1,0:T(8,128)(2,1)}, u32[]{:S(2)}, u32[]{:S(2)}) collective-permute-start(bf16[3,128,256]{2,1,0:T(8,128)(2,1)} %rev.16), channel_id=1, source_target_pairs={{24,0},{32,8},{40,16},{48,24},{56,32},{64,40},{72,48},{80,56},{88,... | collective-permute-start | bytes 589832 | tf_op jit(solution)/shard_map/ppermute | solution.py:30
  198.4 23.7 %collective-permute-start.19 = (bf16[3,128,256]{2,1,0:T(8,128)(2,1)}, bf16[3,128,256]{2,1,0:T(8,128)(2,1)S(1)}, u32[]{:S(2)}, u32[]{:S(2)}) collective-permute-start(bf16[3,128,256]{2,1,0:T(8,128)(2,1)} %rev.15), channel_id=1, source_target_pairs={{48,0},{56,8},{64,16},{72,24},{80,32},{88,40},{96,48},{104,56},{11... | collective-permute-start | bytes 589832 | tf_op jit(solution)/shard_map/ppermute | solution.py:30
  202.4 28.4 %collective-permute-start.20 = (bf16[1,128,256]{2,1,0:T(8,128)(2,1)}, bf16[1,128,256]{2,1,0:T(8,128)(2,1)}, u32[]{:S(2)}, u32[]{:S(2)}) collective-permute-start(bf16[1,128,256]{2,1,0:T(8,128)(2,1)} %slice.175), channel_id=1, source_target_pairs={{72,0},{80,8},{88,16},{96,24},{104,32},{112,40},{120,48},{128,56},... | collective-permute-start | bytes 196616 | tf_op jit(solution)/shard_map/ppermute | solution.py:30
  216.2 5.6 %copy-start.8 = (f32[128,64]{1,0:T(8,128)S(1)}, f32[128,64]{1,0:T(8,128)}, u32[]{:S(2)}) copy-start(f32[128,64]{1,0:T(8,128)} %copy-done.7) | copy-start | bytes 98308
  216.2 5.6 %copy-start.9 = (f32[128,64]{1,0:T(8,128)S(1)}, f32[128,64]{1,0:T(8,128)}, u32[]{:S(2)}) copy-start(f32[128,64]{1,0:T(8,128)} %get-tuple-element.61) | copy-start | bytes 98308
  218.0 21.1 %collective-permute-start.11 = (bf16[128,32,32]{0,2,1:T(8,128)(2,1)}, bf16[128,32,32]{0,2,1:T(8,128)(2,1)}, u32[]{:S(2)}, u32[]{:S(2)}) collective-permute-start(bf16[128,32,32]{0,2,1:T(8,128)(2,1)} %get-tuple-element.38), channel_id=1, source_target_pairs={{0,1},{1,2},{2,3},{3,4},{4,5},{5,6},{6,7},{7,0},{8,9},{9,10},{10,1... | collective-permute-start | bytes 786440 | tf_op jit(solution)/shard_map/ppermute | solution.py:193
  219.4 19.8 %collective-permute-start.12 = (bf16[128,32,32]{0,2,1:T(8,128)(2,1)}, bf16[128,32,32]{0,2,1:T(8,128)(2,1)}, u32[]{:S(2)}, u32[]{:S(2)}) collective-permute-start(bf16[128,32,32]{0,2,1:T(8,128)(2,1)} %get-tuple-element.44), channel_id=1, source_target_pairs={{0,2},{1,3},{2,4},{3,5},{4,6},{5,7},{6,0},{7,1},{8,10},{9,11},{10,... | collective-permute-start | bytes 786440 | tf_op jit(solution)/shard_map/ppermute | solution.py:193
  223.1 7.7 %collective-permute-start.21 = (bf16[128,256]{1,0:T(8,128)(2,1)S(1)}, bf16[128,256]{1,0:T(8,128)(2,1)S(1)}, u32[]{:S(2)}, u32[]{:S(2)}) collective-permute-start(bf16[128,256]{1,0:T(8,128)(2,1)S(1)} %get-tuple-element.55), channel_id=1, source_target_pairs={{8,0},{16,8},{24,16},{32,24},{40,32},{48,40},{56,48},{64,56},{72,6... | collective-permute-start | bytes 196616 | tf_op jit(solution)/shard_map/ppermute | solution.py:30
  225.0 13.2 %collective-permute-start.22 = (bf16[128,256]{1,0:T(8,128)(2,1)S(1)}, bf16[128,256]{1,0:T(8,128)(2,1)S(1)}, u32[]{:S(2)}, u32[]{:S(2)}) collective-permute-start(bf16[128,256]{1,0:T(8,128)(2,1)S(1)} %get-tuple-element.56), channel_id=1, source_target_pairs={{16,0},{24,8},{32,16},{40,24},{48,32},{56,40},{64,48},{72,56},{80,... | collective-permute-start | bytes 196616 | tf_op jit(solution)/shard_map/ppermute | solution.py:30
  230.8 11.3 %collective-permute-start.13 = (bf16[128,32,32]{0,2,1:T(8,128)(2,1)}, bf16[128,32,32]{0,2,1:T(8,128)(2,1)S(1)}, u32[]{:S(2)}, u32[]{:S(2)}) collective-permute-start(bf16[128,32,32]{0,2,1:T(8,128)(2,1)} %get-tuple-element.43), channel_id=1, source_target_pairs={{0,3},{1,4},{2,5},{3,6},{4,7},{5,0},{6,1},{7,2},{8,11},{9,12},{10,... | collective-permute-start | bytes 786440 | tf_op jit(solution)/shard_map/ppermute | solution.py:193
  230.8 16.1 %collective-permute-start.14 = (bf16[128,32,32]{0,2,1:T(8,128)(2,1)}, bf16[128,32,32]{0,2,1:T(8,128)(2,1)S(1)}, u32[]{:S(2)}, u32[]{:S(2)}) collective-permute-start(bf16[128,32,32]{0,2,1:T(8,128)(2,1)} %get-tuple-element.42), channel_id=1, source_target_pairs={{0,4},{1,5},{2,6},{3,7},{4,0},{5,1},{6,2},{7,3},{8,12},{9,13},{10,... | collective-permute-start | bytes 786440 | tf_op jit(solution)/shard_map/ppermute | solution.py:193
  238.2 15.0 %collective-permute-start.15 = (bf16[128,32,32]{0,2,1:T(8,128)(2,1)}, bf16[128,32,32]{0,2,1:T(8,128)(2,1)S(1)}, u32[]{:S(2)}, u32[]{:S(2)}) collective-permute-start(bf16[128,32,32]{0,2,1:T(8,128)(2,1)} %get-tuple-element.41), channel_id=1, source_target_pairs={{0,5},{1,6},{2,7},{3,0},{4,1},{5,2},{6,3},{7,4},{8,13},{9,14},{10,... | collective-permute-start | bytes 786440 | tf_op jit(solution)/shard_map/ppermute | solution.py:193
  239.1 25.8 %collective-permute-start.16 = (bf16[128,32,32]{0,2,1:T(8,128)(2,1)}, bf16[128,32,32]{0,2,1:T(8,128)(2,1)S(1)}, u32[]{:S(2)}, u32[]{:S(2)}) collective-permute-start(bf16[128,32,32]{0,2,1:T(8,128)(2,1)} %get-tuple-element.40), channel_id=1, source_target_pairs={{0,6},{1,7},{2,0},{3,1},{4,2},{5,3},{6,4},{7,5},{8,14},{9,15},{10,... | collective-permute-start | bytes 786440 | tf_op jit(solution)/shard_map/ppermute | solution.py:193
  239.2 26.2 %collective-permute-start.17 = (bf16[128,32,32]{0,2,1:T(8,128)(2,1)}, bf16[128,32,32]{0,2,1:T(8,128)(2,1)S(1)}, u32[]{:S(2)}, u32[]{:S(2)}) collective-permute-start(bf16[128,32,32]{0,2,1:T(8,128)(2,1)} %get-tuple-element.39), channel_id=1, source_target_pairs={{0,7},{1,0},{2,1},{3,2},{4,3},{5,4},{6,5},{7,6},{8,15},{9,8},{10,9... | collective-permute-start | bytes 786440 | tf_op jit(solution)/shard_map/ppermute | solution.py:193
Sparse Core Ops, SparseCore 0:
  21.6 145.8 all-gather.1

commit v5 on v1

--- a/solution.py
+++ b/solution.py
@@ -130,7 +130,12 @@
     kv_me = lax.axis_index("kv")
     col_w = out_weight.shape[1]
     n_seq = seq_size()
-    pieces = lax.all_to_all(out_weight, "kv", split_axis=0, concat_axis=1, tiled=True)
+    rows_w = out_weight.shape[0] // kv_count
+    w_got = [lax.dynamic_slice_in_dim(out_weight, kv_me * rows_w, rows_w, 0)]
+    for j in range(1, kv_count):
+        block = lax.dynamic_slice_in_dim(out_weight, ((kv_me + j) % kv_count) * rows_w, rows_w, 0)
+        w_got.append(lax.ppermute(block, "kv", [(i, (i + j) % kv_count) for i in range(kv_count)]))
+    pieces = jnp.roll(jnp.stack(w_got, axis=1)[:, ::-1], kv_me + 1, axis=1).reshape(rows_w, -1)
     stripes = lax.all_gather(pieces, SEQ, axis=1, tiled=True)
     og_list = [out_grad.reshape(length, n_seq, col_w)]
     for j in range(1, kv_count):

time: 252 us -> 258 us (1.024)
  blocking collectives: 13.7 us -> 0 us
  starting transfers between devices: 58 us -> 71.3 us
  waiting for transfers between devices: 93.7 us -> 100 us
  other arithmetic: 16.9 us -> 13.8 us
    all_to_all x1 -> x0, blocking collectives: 13.7 us -> none  [per_device(): lax.all_to_all(out_weight, 'kv', split_axis=0, concat_axis=1, tiled=True)]
    dot_general x0 -> x1, matrix products: none -> 10.3 us  [per_device(): jnp.einsum('tr,rskj->ktsj', attn, stripes.reshape(attn.shape[1], n_seq, k...]
    ppermute x0 -> x7, starting transfers between devices: none -> 10.3 us  [per_device(): lax.ppermute(block, 'kv', [(i, (i + j) % kv_count) for i in range(kv_coun...]
    unnamed x1 -> x0, matrix products: 8.26 us -> none
    all_gather x1, waiting for transfers between devices: 71.7 us -> 76.8 us  [per_device(): stripes = lax.all_gather(pieces, SEQ, axis=1, tiled=True)]
    ppermute x8, starting transfers between devices: 32.4 us -> 35.6 us  [shifted(): return lax.ppermute(block, SEQ, route)]
    unnamed x65 -> x80, local copies, waits for them, and re-layouts: 16.8 us -> 16.6 us
  transfers between devices with their start and end apart: 23 -> 30, of which waited for: 8 -> 9; matrix products, arithmetic and copies ran while one was open for 20% -> 19% of each run, Pallas kernels for 0% -> 0%
where the time goes in v5:
time: 258 us; the launch traced here: 255 us
  waiting for transfers between devices  100 us (39%)
  starting transfers between devices  71.3 us (28%)
  matrix products  29 us (11%)
  local copies, waits for them, and re-layouts  25.3 us (10%)
  between operations  15 us (6%)
  other arithmetic  13.8 us (5%)
    all_gather x1, waiting for transfers between devices, per_device(): stripes = lax.all_gather(pieces, SEQ, axis=1, tiled=True)  76.8 us
    ppermute x8, starting transfers between devices, shifted(): return lax.ppermute(block, SEQ, route)  35.6 us
    ppermute x7, starting transfers between devices, per_device(): lax.ppermute(piece, 'kv', [(i, (i + j) % kv_count) for i in range(kv_coun...  20.5 us
    ppermute x8, waiting for transfers between devices, shifted(): return lax.ppermute(block, SEQ, route)  17.8 us
    unnamed x80, local copies, waits for them, and re-layouts  16.6 us
    dot_general x1, matrix products, per_device(): jnp.einsum('tr,rskj->ktsj', attn, stripes.reshape(attn.shape[1], n_seq, k...  10.3 us
    ppermute x7, starting transfers between devices, per_device(): lax.ppermute(block, 'kv', [(i, (i + j) % kv_count) for i in range(kv_coun...  10.3 us
    dot_general x1, matrix products, per_device(): lax.dot_general(og_perm, stripes, contract, preferred_element_type=jnp.fl...  8.76 us
  transfers between devices with their start and end apart: 30, of which 9 were waited for; matrix products, arithmetic and copies ran while one was open for 19% of the time, Pallas kernels for 0%

profile of v5, /device:TPU:97, one launch (start us, length us, event | category | flops | bytes accessed | tf_op | source)
XLA Modules:
  0.0 254.7 jit_solution(15409444781340303640)
XLA Ops:
  7.4 1.1 constant_dynamic-slice_fusion.2
  8.5 1.4 collective-permute-start
  9.9 2.6 %collective-permute-start.1 = (bf16[1024,32]{0,1:T(8,128)(2,1)S(1)}, bf16[1024,32]{0,1:T(8,128)(2,1)S(1)}, u32[]{:S(2)}, u32[]{:S(2)}) collective-permute-start(bf16[1024,32]{0,1:T(8,128)(2,1)S(1)} %get-tuple-element.45), channel_id=1, source_target_pairs={{0,2},{1,3},{2,4},{3,5},{4,6},{5,7},{6,0},{7,1},{8,10},{9,11},{10,... | collective-permute-start | bytes 196616 | tf_op jit(solution)/shard_map/ppermute | solution.py:137
  12.5 2.0 collective-permute-start.2
  14.7 1.3 collective-permute-start.4
  16.9 1.2 collective-permute-start.5
  18.2 1.5 collective-permute-start.6
  19.7 2.3 collective-permute-done.5
  22.1 1.0 fusion.6
  23.4 3.5 %collective-permute-start.11 = (bf16[128,1024]{0,1:T(8,128)(2,1)S(1)}, bf16[128,1024]{0,1:T(8,128)(2,1)S(1)}, u32[]{:S(2)}, u32[]{:S(2)}) collective-permute-start(bf16[128,1024]{0,1:T(8,128)(2,1)S(1)} %copy.39), channel_id=1, source_target_pairs={{0,7},{1,0},{2,1},{3,2},{4,3},{5,4},{6,5},{7,6},{8,15},{9,8},{10,9... | collective-permute-start | bytes 786440 | tf_op jit(solution)/shard_map/ppermute | solution.py:142
  29.3 8.4 %collective-permute-start.7 = (bf16[1,129,256]{2,1,0:T(8,128)(2,1)S(1)}, bf16[1,129,256]{2,1,0:T(8,128)(2,1)S(1)}, u32[]{:S(2)}, u32[]{:S(2)}) collective-permute-start(bf16[1,129,256]{2,1,0:T(8,128)(2,1)S(1)} %fusion.19), channel_id=1, source_target_pairs={{0,8},{8,16},{16,24},{24,32},{32,40},{40,48},{48,56},{56,64},{64,7... | collective-permute-start | bytes 198152 | tf_op jit(solution)/shard_map/ppermute | solution.py:30
  39.3 1.0 broadcast_multiply_fusion
  40.5 9.9 %collective-permute-done.7 = bf16[1,129,256]{2,1,0:T(8,128)(2,1)S(1)} collective-permute-done((bf16[1,129,256]{2,1,0:T(8,128)(2,1)S(1)}, bf16[1,129,256]{2,1,0:T(8,128)(2,1)S(1)}, u32[]{:S(2)}, u32[]{:S(2)}) %collective-permute-start.7) | collective-permute-done | bytes 66080 | tf_op jit(solution)/shard_map/ppermute | solution.py:30
  50.4 1.9 collective-permute-start.9
  52.3 5.9 %collective-permute-start.8 = (bf16[2,129,256]{2,1,0:T(8,128)(2,1)S(1)}, bf16[2,129,256]{2,1,0:T(8,128)(2,1)S(1)}, u32[]{:S(2)}, u32[]{:S(2)}) collective-permute-start(bf16[2,129,256]{2,1,0:T(8,128)(2,1)S(1)} %pad_maximum_fusion.4), channel_id=1, source_target_pairs={{0,64},{8,72},{16,80},{24,88},{32,96},{40,104},{48,112},{56,120},{... | collective-permute-start | bytes 396296 | tf_op jit(solution)/shard_map/ppermute | solution.py:30
  58.3 4.5 %collective-permute-done.9 = bf16[2,129,256]{2,1,0:T(8,128)(2,1)S(1)} collective-permute-done((bf16[2,129,256]{2,1,0:T(8,128)(2,1)S(1)}, bf16[2,129,256]{2,1,0:T(8,128)(2,1)S(1)}, u32[]{:S(2)}, u32[]{:S(2)}) %collective-permute-start.9) | collective-permute-done | bytes 132128 | tf_op jit(solution)/shard_map/ppermute | solution.py:30
  62.9 2.2 collective-permute-done.8
  67.3 7.1 %collective-permute-start.10 = (bf16[4,129,256]{2,1,0:T(8,128)(2,1)S(1)}, bf16[4,129,256]{2,1,0:T(8,128)(2,1)S(1)}, u32[]{:S(2)}, u32[]{:S(2)}) collective-permute-start(bf16[4,129,256]{2,1,0:T(8,128)(2,1)S(1)} %pad_maximum_fusion.1), channel_id=1, source_target_pairs={{0,32},{8,40},{16,48},{24,56},{32,64},{40,72},{48,80},{56,88},{64,... | collective-permute-start | bytes 792584 | tf_op jit(solution)/shard_map/ppermute | solution.py:30
  83.9 2.0 constant_dynamic-slice_fusion
  85.9 2.0 copy.47
  88.2 1.4 or_and_fusion
  89.7 4.6 %exponential_reduce_fusion = (f32[8,128]{1,0:T(8,128)S(1)}, f32[8,128,1280]{1,2,0:T(8,128)}) fusion(bf16[1280,128,1]{1,0,2:T(8,128)(2,1)S(1)} %bitcast.189, pred[128,1280]{0,1:T(8,128)(4,1)S(1)} %or_and_fusion, bf16[128,8,64]{2,0,1:T(8,128)(2,1)S(1)} %get-tuple-element.36, bf16[128,8,64]{2,0,1:T(8,128)(2,1)S(1)} %get-tuple-element.35), kind=kOutput, calls=%fused_computation.7 | convolution fusion | flops 341312768 | bytes 6000640 | tf_op jit(solution)/shard_map/sub | solution.py:171
  94.3 3.2 %divide_convert_fusion = bf16[8,128,1280]{1,2,0:T(8,128)(2,1)S(1)} fusion(f32[8,128,1280]{1,2,0:T(8,128)} %get-tuple-element.61, f32[8,128]{1,0:T(8,128)S(1)} %get-tuple-element.60), kind=kLoop, calls=%fused_computation.6 | loop fusion | flops 2621440 | bytes 7868416 | tf_op jit(solution)/shard_map/convert_element_type | solution.py:172
  97.4 76.8 %all-gather.2.cloned.1.call-done = bf16[1024,8192]{0,1:T(8,128)(2,1)} async-done(((bf16[1024,256]{0,1:T(8,128)(2,1)}), bf16[1024,8192]{0,1:T(8,128)(2,1)}) %all-gather.2.cloned.1.call-update) | async-done | bytes 16777232 | tf_op jit(solution)/shard_map/all_gather | solution.py:139
  174.2 8.8 %convolution_convert_fusion.2 = bf16[128,1024]{1,0:T(8,128)(2,1)S(1)} fusion(bf16[128,8192]{0,1:T(8,128)(2,1)} %bitcast.178, bf16[1024,8192]{0,1:T(8,128)(2,1)} %all-gather.2.cloned.1.call-done), kind=kOutput, calls=%fused_computation.16 | convolution fusion | flops 2147614720 | bytes 19136512 | tf_op jit(solution)/shard_map/dot_general | solution.py:147
  183.1 1.3 multiply_reduce_fusion
  184.4 1.0 convolution_bitcast_fusion
  186.3 1.5 copy-done
  187.7 1.1 fusion.4
  189.4 1.9 collective-permute-start.25
  191.4 3.0 %collective-permute-start.27 = (bf16[2,128,256]{2,1,0:T(8,128)(2,1)S(1)}, bf16[2,128,256]{2,1,0:T(8,128)(2,1)S(1)}, u32[]{:S(2)}, u32[]{:S(2)}) collective-permute-start(bf16[2,128,256]{2,1,0:T(8,128)(2,1)S(1)} %slice.128), channel_id=1, source_target_pairs={{64,0},{72,8},{80,16},{88,24},{96,32},{104,40},{112,48},{120,56},{... | collective-permute-start | bytes 393224 | tf_op jit(solution)/shard_map/ppermute | solution.py:30
  194.4 10.3 %convolution_convert_fusion = bf16[32,8,32,128]{3,2,1,0:T(8,128)(2,1)S(1)} fusion(bf16[1024,32,8,32]{0,3,2,1:T(8,128)(2,1)} %bitcast.177, bf16[128,1024]{0,1:T(8,128)(2,1)} %bitcast.207), kind=kOutput, calls=%fused_computation.11 | convolution fusion | flops 2148532224 | bytes 19136512 | tf_op jit(solution)/shard_map/tr,rskj->ktsj/dot_general | solution.py:185
  204.8 1.2 dynamic-slice_bitcast_fusion.6
  206.0 1.2 collective-permute-start.18
  207.2 2.4 collective-permute-start.19
  209.6 1.2 collective-permute-start.20
  210.8 1.2 fusion.5
  212.9 2.8 %collective-permute-start.26 = (bf16[2,128,256]{2,1,0:T(8,128)(2,1)S(1)}, bf16[2,128,256]{2,1,0:T(8,128)(2,1)S(1)}, u32[]{:S(2)}, u32[]{:S(2)}) collective-permute-start(bf16[2,128,256]{2,1,0:T(8,128)(2,1)S(1)} %slice.180), channel_id=1, source_target_pairs={{16,0},{24,8},{32,16},{40,24},{48,32},{56,40},{64,48},{72,56},{80,... | collective-permute-start | bytes 393224 | tf_op jit(solution)/shard_map/ppermute | solution.py:30
  216.4 1.7 collective-permute-done.18
  218.1 1.6 collective-permute-done.19
  219.7 2.4 collective-permute-start.23
  222.1 12.9 %collective-permute-start.24 = (bf16[128,32,32]{0,2,1:T(8,128)(2,1)}, bf16[128,32,32]{0,2,1:T(8,128)(2,1)}, u32[]{:S(2)}, u32[]{:S(2)}) collective-permute-start(bf16[128,32,32]{0,2,1:T(8,128)(2,1)} %get-tuple-element.33), channel_id=1, source_target_pairs={{0,7},{1,0},{2,1},{3,2},{4,3},{5,4},{6,5},{7,6},{8,15},{9,8},{10,9... | collective-permute-start | bytes 786440 | tf_op jit(solution)/shard_map/ppermute | solution.py:195
  235.3 0.9 copy.67
  236.2 1.1 fusion.14
  237.3 4.5 %collective-permute-start.28 = (bf16[1,128,256]{2,1,0:T(8,128)(2,1)S(1)}, bf16[1,128,256]{2,1,0:T(8,128)(2,1)S(1)}, u32[]{:S(2)}, u32[]{:S(2)}) collective-permute-start(bf16[1,128,256]{2,1,0:T(8,128)(2,1)S(1)} %slice.181), channel_id=1, source_target_pairs={{8,0},{16,8},{24,16},{32,24},{40,32},{48,40},{56,48},{64,56},{72,6... | collective-permute-start | bytes 196616 | tf_op jit(solution)/shard_map/ppermute | solution.py:30
  241.9 1.5 fusion.13
  244.2 1.3 collective-permute-done.28
  246.1 1.1 fusion.27
  (153 shorter events, 23.4 us)
Async XLA Ops:
  7.2 16.0 %copy-start.11 = (bf16[128,1024]{1,0:T(8,128)(2,1)S(1)}, bf16[128,1024]{1,0:T(8,128)(2,1)}, u32[]{:S(2)}) copy-start(bf16[128,1024]{1,0:T(8,128)(2,1)} %param.14) | copy-start | bytes 786436
  7.2 20.3 %copy-start.21 = (s32[3,128]{1,0:T(4,128)S(1)}, s32[3,128]{1,0:T(4,128)}, u32[]{:S(2)}) copy-start(s32[3,128]{1,0:T(4,128)} %param.17) | copy-start | bytes 4612
  7.2 20.9 %copy-start.22 = (s32[128]{0:T(128)S(1)}, s32[128]{0:T(128)}, u32[]{:S(2)}) copy-start(s32[128]{0:T(128)} %param.15) | copy-start | bytes 1540
  7.2 21.6 %copy-start.17 = (bf16[128,128]{1,0:T(8,128)(2,1)S(1)}, bf16[128,128]{1,0:T(8,128)(2,1)}, u32[]{:S(2)}) copy-start(bf16[128,128]{1,0:T(8,128)(2,1)} %param.11) | copy-start | bytes 98308
  7.2 22.0 %copy-start.16 = (bf16[128,128]{1,0:T(8,128)(2,1)S(1)}, bf16[128,128]{1,0:T(8,128)(2,1)}, u32[]{:S(2)}) copy-start(bf16[128,128]{1,0:T(8,128)(2,1)} %param.12) | copy-start | bytes 98308
  7.2 30.5 %copy-start.12 = (bf16[128,1024]{1,0:T(8,128)(2,1)S(1)}, bf16[128,1024]{1,0:T(8,128)(2,1)}, u32[]{:S(2)}) copy-start(bf16[128,1024]{1,0:T(8,128)(2,1)} %param.10) | copy-start | bytes 786436
  7.2 167.0 %all-gather.2.cloned.1.call-start = ((), (), s32[]{:S(2)}) async-start(), calls=%async_computation | async-start | bytes 17301504 | tf_op jit(solution)/shard_map/all_gather | solution.py:139
  7.4 31.0 %copy-start.23 = (s32[1,32]{1,0:T(1,128)S(1)}, s32[1,32]{1,0:T(1,128)}, u32[]{:S(2)}) copy-start(s32[1,32]{1,0:T(1,128)} %param.16) | copy-start | bytes 388
  8.5 8.4 %collective-permute-start = (bf16[1024,32]{0,1:T(8,128)(2,1)S(1)}, bf16[1024,32]{0,1:T(8,128)(2,1)S(1)}, u32[]{:S(2)}, u32[]{:S(2)}) collective-permute-start(bf16[1024,32]{0,1:T(8,128)(2,1)S(1)} %get-tuple-element.46), channel_id=1, source_target_pairs={{0,1},{1,2},{2,3},{3,4},{4,5},{5,6},{6,7},{7,0},{8,9},{9,10},{10,1... | collective-permute-start | bytes 196616 | tf_op jit(solution)/shard_map/ppermute | solution.py:137
  9.9 8.3 %collective-permute-start.1 = (bf16[1024,32]{0,1:T(8,128)(2,1)S(1)}, bf16[1024,32]{0,1:T(8,128)(2,1)S(1)}, u32[]{:S(2)}, u32[]{:S(2)}) collective-permute-start(bf16[1024,32]{0,1:T(8,128)(2,1)S(1)} %get-tuple-element.45), channel_id=1, source_target_pairs={{0,2},{1,3},{2,4},{3,5},{4,6},{5,7},{6,0},{7,1},{8,10},{9,11},{10,... | collective-permute-start | bytes 196616 | tf_op jit(solution)/shard_map/ppermute | solution.py:137
  12.5 7.2 %collective-permute-start.2 = (bf16[1024,32]{0,1:T(8,128)(2,1)S(1)}, bf16[1024,32]{0,1:T(8,128)(2,1)S(1)}, u32[]{:S(2)}, u32[]{:S(2)}) collective-permute-start(bf16[1024,32]{0,1:T(8,128)(2,1)S(1)} %get-tuple-element.44), channel_id=1, source_target_pairs={{0,3},{1,4},{2,5},{3,6},{4,7},{5,0},{6,1},{7,2},{8,11},{9,12},{10,... | collective-permute-start | bytes 196616 | tf_op jit(solution)/shard_map/ppermute | solution.py:137
  14.5 5.2 %collective-permute-start.3 = (bf16[1024,32]{0,1:T(8,128)(2,1)S(1)}, bf16[1024,32]{0,1:T(8,128)(2,1)S(1)}, u32[]{:S(2)}, u32[]{:S(2)}) collective-permute-start(bf16[1024,32]{0,1:T(8,128)(2,1)S(1)} %get-tuple-element.43), channel_id=1, source_target_pairs={{0,4},{1,5},{2,6},{3,7},{4,0},{5,1},{6,2},{7,3},{8,12},{9,13},{10,... | collective-permute-start | bytes 196616 | tf_op jit(solution)/shard_map/ppermute | solution.py:137
  14.7 4.9 %collective-permute-start.4 = (bf16[1024,32]{0,1:T(8,128)(2,1)S(1)}, bf16[1024,32]{0,1:T(8,128)(2,1)S(1)}, u32[]{:S(2)}, u32[]{:S(2)}) collective-permute-start(bf16[1024,32]{0,1:T(8,128)(2,1)S(1)} %get-tuple-element.42), channel_id=1, source_target_pairs={{0,5},{1,6},{2,7},{3,0},{4,1},{5,2},{6,3},{7,4},{8,13},{9,14},{10,... | collective-permute-start | bytes 196616 | tf_op jit(solution)/shard_map/ppermute | solution.py:137
  16.9 5.1 %collective-permute-start.5 = (bf16[1024,32]{0,1:T(8,128)(2,1)S(1)}, bf16[1024,32]{0,1:T(8,128)(2,1)S(1)}, u32[]{:S(2)}, u32[]{:S(2)}) collective-permute-start(bf16[1024,32]{0,1:T(8,128)(2,1)S(1)} %get-tuple-element.47), channel_id=1, source_target_pairs={{0,6},{1,7},{2,0},{3,1},{4,2},{5,3},{6,4},{7,5},{8,14},{9,15},{10,... | collective-permute-start | bytes 196616 | tf_op jit(solution)/shard_map/ppermute | solution.py:137
  18.2 3.9 %collective-permute-start.6 = (bf16[1024,32]{0,1:T(8,128)(2,1)S(1)}, bf16[1024,32]{0,1:T(8,128)(2,1)S(1)}, u32[]{:S(2)}, u32[]{:S(2)}) collective-permute-start(bf16[1024,32]{0,1:T(8,128)(2,1)S(1)} %get-tuple-element.41), channel_id=1, source_target_pairs={{0,7},{1,0},{2,1},{3,2},{4,3},{5,4},{6,5},{7,6},{8,15},{9,8},{10,9... | collective-permute-start | bytes 196616 | tf_op jit(solution)/shard_map/ppermute | solution.py:137
  23.4 41.7 %collective-permute-start.11 = (bf16[128,1024]{0,1:T(8,128)(2,1)S(1)}, bf16[128,1024]{0,1:T(8,128)(2,1)S(1)}, u32[]{:S(2)}, u32[]{:S(2)}) collective-permute-start(bf16[128,1024]{0,1:T(8,128)(2,1)S(1)} %copy.39), channel_id=1, source_target_pairs={{0,7},{1,0},{2,1},{3,2},{4,3},{5,4},{6,5},{7,6},{8,15},{9,8},{10,9... | collective-permute-start | bytes 786440 | tf_op jit(solution)/shard_map/ppermute | solution.py:142
  26.9 39.2 %collective-permute-start.12 = (bf16[128,1024]{0,1:T(8,128)(2,1)S(1)}, bf16[128,1024]{0,1:T(8,128)(2,1)S(1)}, u32[]{:S(2)}, u32[]{:S(2)}) collective-permute-start(bf16[128,1024]{0,1:T(8,128)(2,1)S(1)} %copy.39), channel_id=1, source_target_pairs={{0,6},{1,7},{2,0},{3,1},{4,2},{5,3},{6,4},{7,5},{8,14},{9,15},{10,... | collective-permute-start | bytes 786440 | tf_op jit(solution)/shard_map/ppermute | solution.py:142
  26.9 40.5 %collective-permute-start.13 = (bf16[128,1024]{0,1:T(8,128)(2,1)S(1)}, bf16[128,1024]{0,1:T(8,128)(2,1)S(1)}, u32[]{:S(2)}, u32[]{:S(2)}) collective-permute-start(bf16[128,1024]{0,1:T(8,128)(2,1)S(1)} %copy.39), channel_id=1, source_target_pairs={{0,5},{1,6},{2,7},{3,0},{4,1},{5,2},{6,3},{7,4},{8,13},{9,14},{10,... | collective-permute-start | bytes 786440 | tf_op jit(solution)/shard_map/ppermute | solution.py:142
  28.1 12.2 %copy-start.18 = (f32[64]{0:T(128)}, f32[64]{0:T(128)S(1)}, u32[]{:S(2)}) copy-start(f32[64]{0:T(128)S(1)} %multiply_exponential_fusion) | copy-start | bytes 772
  28.1 12.1 %copy-start.19 = (pred[64]{0:T(512)(128)(4,1)}, pred[64]{0:T(512)(128)(4,1)S(1)}, u32[]{:S(2)}) copy-start(pred[64]{0:T(512)(128)(4,1)S(1)} %get-tuple-element.64) | copy-start | bytes 196
  28.1 12.1 %copy-start.20 = (pred[64]{0:T(512)(128)(4,1)}, pred[64]{0:T(512)(128)(4,1)S(1)}, u32[]{:S(2)}) copy-start(pred[64]{0:T(512)(128)(4,1)S(1)} %get-tuple-element.65) | copy-start | bytes 196
  29.3 21.0 %collective-permute-start.7 = (bf16[1,129,256]{2,1,0:T(8,128)(2,1)S(1)}, bf16[1,129,256]{2,1,0:T(8,128)(2,1)S(1)}, u32[]{:S(2)}, u32[]{:S(2)}) collective-permute-start(bf16[1,129,256]{2,1,0:T(8,128)(2,1)S(1)} %fusion.19), channel_id=1, source_target_pairs={{0,8},{8,16},{16,24},{24,32},{32,40},{40,48},{48,56},{56,64},{64,7... | collective-permute-start | bytes 198152 | tf_op jit(solution)/shard_map/ppermute | solution.py:30
  40.4 49.2 %copy-start.5 = (bf16[128,8,64]{2,0,1:T(8,128)(2,1)}, bf16[128,8,64]{2,0,1:T(8,128)(2,1)S(1)}, u32[]{:S(2)}) copy-start(bf16[128,8,64]{2,0,1:T(8,128)(2,1)S(1)} %get-tuple-element.35) | copy-start | bytes 393220
  40.4 49.2 %copy-start.7 = (bf16[128,8,64]{2,0,1:T(8,128)(2,1)}, bf16[128,8,64]{2,0,1:T(8,128)(2,1)S(1)}, u32[]{:S(2)}) copy-start(bf16[128,8,64]{2,0,1:T(8,128)(2,1)S(1)} %get-tuple-element.36) | copy-start | bytes 393220
  50.4 12.5 %collective-permute-start.9 = (bf16[2,129,256]{2,1,0:T(8,128)(2,1)S(1)}, bf16[2,129,256]{2,1,0:T(8,128)(2,1)S(1)}, u32[]{:S(2)}, u32[]{:S(2)}) collective-permute-start(bf16[2,129,256]{2,1,0:T(8,128)(2,1)S(1)} %pad_maximum_fusion.4), channel_id=1, source_target_pairs={{0,16},{8,24},{16,32},{24,40},{32,48},{40,56},{48,64},{56,72},{64,... | collective-permute-start | bytes 396296 | tf_op jit(solution)/shard_map/ppermute | solution.py:30
  52.3 12.7 %collective-permute-start.8 = (bf16[2,129,256]{2,1,0:T(8,128)(2,1)S(1)}, bf16[2,129,256]{2,1,0:T(8,128)(2,1)S(1)}, u32[]{:S(2)}, u32[]{:S(2)}) collective-permute-start(bf16[2,129,256]{2,1,0:T(8,128)(2,1)S(1)} %pad_maximum_fusion.4), channel_id=1, source_target_pairs={{0,64},{8,72},{16,80},{24,88},{32,96},{40,104},{48,112},{56,120},{... | collective-permute-start | bytes 396296 | tf_op jit(solution)/shard_map/ppermute | solution.py:30
  62.8 12.4 %collective-permute-start.14 = (bf16[128,1024]{0,1:T(8,128)(2,1)S(1)}, bf16[128,1024]{0,1:T(8,128)(2,1)S(1)}, u32[]{:S(2)}, u32[]{:S(2)}) collective-permute-start(bf16[128,1024]{0,1:T(8,128)(2,1)S(1)} %copy.39), channel_id=1, source_target_pairs={{0,4},{1,5},{2,6},{3,7},{4,0},{5,1},{6,2},{7,3},{8,12},{9,13},{10,... | collective-permute-start | bytes 786440 | tf_op jit(solution)/shard_map/ppermute | solution.py:142
  65.0 10.9 %collective-permute-start.15 = (bf16[128,1024]{0,1:T(8,128)(2,1)S(1)}, bf16[128,1024]{0,1:T(8,128)(2,1)S(1)}, u32[]{:S(2)}, u32[]{:S(2)}) collective-permute-start(bf16[128,1024]{0,1:T(8,128)(2,1)S(1)} %copy.39), channel_id=1, source_target_pairs={{0,3},{1,4},{2,5},{3,6},{4,7},{5,0},{6,1},{7,2},{8,11},{9,12},{10,... | collective-permute-start | bytes 786440 | tf_op jit(solution)/shard_map/ppermute | solution.py:142
  65.1 11.6 %collective-permute-start.16 = (bf16[128,1024]{0,1:T(8,128)(2,1)S(1)}, bf16[128,1024]{0,1:T(8,128)(2,1)S(1)}, u32[]{:S(2)}, u32[]{:S(2)}) collective-permute-start(bf16[128,1024]{0,1:T(8,128)(2,1)S(1)} %copy.39), channel_id=1, source_target_pairs={{0,2},{1,3},{2,4},{3,5},{4,6},{5,7},{6,0},{7,1},{8,10},{9,11},{10,... | collective-permute-start | bytes 786440 | tf_op jit(solution)/shard_map/ppermute | solution.py:142
  66.1 11.3 %collective-permute-start.17 = (bf16[128,1024]{0,1:T(8,128)(2,1)S(1)}, bf16[128,1024]{0,1:T(8,128)(2,1)S(1)}, u32[]{:S(2)}, u32[]{:S(2)}) collective-permute-start(bf16[128,1024]{0,1:T(8,128)(2,1)S(1)} %copy.39), channel_id=1, source_target_pairs={{0,1},{1,2},{2,3},{3,4},{4,5},{5,6},{6,7},{7,0},{8,9},{9,10},{10,1... | collective-permute-start | bytes 786440 | tf_op jit(solution)/shard_map/ppermute | solution.py:142
  67.3 20.5 %collective-permute-start.10 = (bf16[4,129,256]{2,1,0:T(8,128)(2,1)S(1)}, bf16[4,129,256]{2,1,0:T(8,128)(2,1)S(1)}, u32[]{:S(2)}, u32[]{:S(2)}) collective-permute-start(bf16[4,129,256]{2,1,0:T(8,128)(2,1)S(1)} %pad_maximum_fusion.1), channel_id=1, source_target_pairs={{0,32},{8,40},{16,48},{24,56},{32,64},{40,72},{48,80},{56,88},{64,... | collective-permute-start | bytes 792584 | tf_op jit(solution)/shard_map/ppermute | solution.py:30
  189.4 22.5 %collective-permute-start.25 = (bf16[4,128,256]{2,1,0:T(8,128)(2,1)S(1)}, bf16[4,128,256]{2,1,0:T(8,128)(2,1)S(1)}, u32[]{:S(2)}, u32[]{:S(2)}) collective-permute-start(bf16[4,128,256]{2,1,0:T(8,128)(2,1)S(1)} %slice.125), channel_id=1, source_target_pairs={{32,0},{40,8},{48,16},{56,24},{64,32},{72,40},{80,48},{88,56},{96,... | collective-permute-start | bytes 786440 | tf_op jit(solution)/shard_map/ppermute | solution.py:30
  191.4 24.6 %collective-permute-start.27 = (bf16[2,128,256]{2,1,0:T(8,128)(2,1)S(1)}, bf16[2,128,256]{2,1,0:T(8,128)(2,1)S(1)}, u32[]{:S(2)}, u32[]{:S(2)}) collective-permute-start(bf16[2,128,256]{2,1,0:T(8,128)(2,1)S(1)} %slice.128), channel_id=1, source_target_pairs={{64,0},{72,8},{80,16},{88,24},{96,32},{104,40},{112,48},{120,56},{... | collective-permute-start | bytes 393224 | tf_op jit(solution)/shard_map/ppermute | solution.py:30
  194.4 16.4 %copy-start.4 = (bf16[10,128,128]{2,1,0:T(8,128)(2,1)S(1)}, bf16[10,128,128]{2,1,0:T(8,128)(2,1)}, u32[]{:S(2)}) copy-start(bf16[10,128,128]{2,1,0:T(8,128)(2,1)} %copy-done.3) | copy-start | bytes 983044
  204.8 10.9 %copy-start.13 = (f32[128,64]{1,0:T(8,128)S(1)}, f32[128,64]{1,0:T(8,128)}, u32[]{:S(2)}) copy-start(f32[128,64]{1,0:T(8,128)} %get-tuple-element.54) | copy-start | bytes 98308
  206.0 12.1 %collective-permute-start.18 = (bf16[128,32,32]{0,2,1:T(8,128)(2,1)S(1)}, bf16[128,32,32]{0,2,1:T(8,128)(2,1)S(1)}, u32[]{:S(2)}, u32[]{:S(2)}) collective-permute-start(bf16[128,32,32]{0,2,1:T(8,128)(2,1)S(1)} %get-tuple-element.28), channel_id=1, source_target_pairs={{0,1},{1,2},{2,3},{3,4},{4,5},{5,6},{6,7},{7,0},{8,9},{9,10},{10,1... | collective-permute-start | bytes 786440 | tf_op jit(solution)/shard_map/ppermute | solution.py:195
  207.2 12.5 %collective-permute-start.19 = (bf16[128,32,32]{0,2,1:T(8,128)(2,1)S(1)}, bf16[128,32,32]{0,2,1:T(8,128)(2,1)S(1)}, u32[]{:S(2)}, u32[]{:S(2)}) collective-permute-start(bf16[128,32,32]{0,2,1:T(8,128)(2,1)S(1)} %get-tuple-element.32), channel_id=1, source_target_pairs={{0,2},{1,3},{2,4},{3,5},{4,6},{5,7},{6,0},{7,1},{8,10},{9,11},{10,... | collective-permute-start | bytes 786440 | tf_op jit(solution)/shard_map/ppermute | solution.py:195
  209.6 27.6 %collective-permute-start.20 = (bf16[128,32,32]{0,2,1:T(8,128)(2,1)}, bf16[128,32,32]{0,2,1:T(8,128)(2,1)}, u32[]{:S(2)}, u32[]{:S(2)}) collective-permute-start(bf16[128,32,32]{0,2,1:T(8,128)(2,1)} %get-tuple-element.31), channel_id=1, source_target_pairs={{0,3},{1,4},{2,5},{3,6},{4,7},{5,0},{6,1},{7,2},{8,11},{9,12},{10,... | collective-permute-start | bytes 786440 | tf_op jit(solution)/shard_map/ppermute | solution.py:195
  212.9 9.2 %collective-permute-start.26 = (bf16[2,128,256]{2,1,0:T(8,128)(2,1)S(1)}, bf16[2,128,256]{2,1,0:T(8,128)(2,1)S(1)}, u32[]{:S(2)}, u32[]{:S(2)}) collective-permute-start(bf16[2,128,256]{2,1,0:T(8,128)(2,1)S(1)} %slice.180), channel_id=1, source_target_pairs={{16,0},{24,8},{32,16},{40,24},{48,32},{56,40},{64,48},{72,56},{80,... | collective-permute-start | bytes 393224 | tf_op jit(solution)/shard_map/ppermute | solution.py:30
  216.0 19.0 %copy-start.14 = (bf16[2,128,256]{2,1,0:T(8,128)(2,1)}, bf16[2,128,256]{2,1,0:T(8,128)(2,1)S(1)}, u32[]{:S(2)}) copy-start(bf16[2,128,256]{2,1,0:T(8,128)(2,1)S(1)} %collective-permute-done.27) | copy-start | bytes 393220
  216.0 25.9 %collective-permute-start.21 = (bf16[128,32,32]{0,2,1:T(8,128)(2,1)}, bf16[128,32,32]{0,2,1:T(8,128)(2,1)S(1)}, u32[]{:S(2)}, u32[]{:S(2)}) collective-permute-start(bf16[128,32,32]{0,2,1:T(8,128)(2,1)} %get-tuple-element.30), channel_id=1, source_target_pairs={{0,4},{1,5},{2,6},{3,7},{4,0},{5,1},{6,2},{7,3},{8,12},{9,13},{10,... | collective-permute-start | bytes 786440 | tf_op jit(solution)/shard_map/ppermute | solution.py:195
  218.1 16.9 %copy-start.9 = (bf16[128,32,32]{0,2,1:T(8,128)(2,1)}, bf16[128,32,32]{0,2,1:T(8,128)(2,1)S(1)}, u32[]{:S(2)}) copy-start(bf16[128,32,32]{0,2,1:T(8,128)(2,1)S(1)} %collective-permute-done.18) | copy-start | bytes 786436
  218.1 23.8 %collective-permute-start.22 = (bf16[128,32,32]{0,2,1:T(8,128)(2,1)}, bf16[128,32,32]{0,2,1:T(8,128)(2,1)S(1)}, u32[]{:S(2)}, u32[]{:S(2)}) collective-permute-start(bf16[128,32,32]{0,2,1:T(8,128)(2,1)} %get-tuple-element.29), channel_id=1, source_target_pairs={{0,5},{1,6},{2,7},{3,0},{4,1},{5,2},{6,3},{7,4},{8,13},{9,14},{10,... | collective-permute-start | bytes 786440 | tf_op jit(solution)/shard_map/ppermute | solution.py:195
  219.7 15.3 %copy-start.10 = (bf16[128,32,32]{0,2,1:T(8,128)(2,1)}, bf16[128,32,32]{0,2,1:T(8,128)(2,1)S(1)}, u32[]{:S(2)}) copy-start(bf16[128,32,32]{0,2,1:T(8,128)(2,1)S(1)} %collective-permute-done.19) | copy-start | bytes 786436
  219.7 22.2 %collective-permute-start.23 = (bf16[128,32,32]{0,2,1:T(8,128)(2,1)}, bf16[128,32,32]{0,2,1:T(8,128)(2,1)S(1)}, u32[]{:S(2)}, u32[]{:S(2)}) collective-permute-start(bf16[128,32,32]{0,2,1:T(8,128)(2,1)} %get-tuple-element.34), channel_id=1, source_target_pairs={{0,6},{1,7},{2,0},{3,1},{4,2},{5,3},{6,4},{7,5},{8,14},{9,15},{10,... | collective-permute-start | bytes 786440 | tf_op jit(solution)/shard_map/ppermute | solution.py:195
  222.1 12.9 %copy-start.15 = (bf16[2,128,256]{2,1,0:T(8,128)(2,1)}, bf16[2,128,256]{2,1,0:T(8,128)(2,1)S(1)}, u32[]{:S(2)}) copy-start(bf16[2,128,256]{2,1,0:T(8,128)(2,1)S(1)} %collective-permute-done.26) | copy-start | bytes 393220
  222.1 19.8 %collective-permute-start.24 = (bf16[128,32,32]{0,2,1:T(8,128)(2,1)}, bf16[128,32,32]{0,2,1:T(8,128)(2,1)}, u32[]{:S(2)}, u32[]{:S(2)}) collective-permute-start(bf16[128,32,32]{0,2,1:T(8,128)(2,1)} %get-tuple-element.33), channel_id=1, source_target_pairs={{0,7},{1,0},{2,1},{3,2},{4,3},{5,4},{6,5},{7,6},{8,15},{9,8},{10,9... | collective-permute-start | bytes 786440 | tf_op jit(solution)/shard_map/ppermute | solution.py:195
  237.3 8.2 %collective-permute-start.28 = (bf16[1,128,256]{2,1,0:T(8,128)(2,1)S(1)}, bf16[1,128,256]{2,1,0:T(8,128)(2,1)S(1)}, u32[]{:S(2)}, u32[]{:S(2)}) collective-permute-start(bf16[1,128,256]{2,1,0:T(8,128)(2,1)S(1)} %slice.181), channel_id=1, source_target_pairs={{8,0},{16,8},{24,16},{32,24},{40,32},{48,40},{56,48},{64,56},{72,6... | collective-permute-start | bytes 196616 | tf_op jit(solution)/shard_map/ppermute | solution.py:30
  (6 other events, 19.0 us)
Sparse Core Ops, SparseCore 0:
  23.3 150.8 all-gather.1

commit v6 on v1

--- a/solution.py
+++ b/solution.py
@@ -99,12 +99,14 @@
     return jnp.concatenate([far, four], axis=0)
 
 
-def return_window(pieces):
+def return_window(pieces, held):
     far = shifted(pieces[:2].astype(jnp.bfloat16), -8).astype(jnp.float32)
     four = pieces[2:]
     two = four[4:] + shifted(four[:4].astype(jnp.bfloat16), -4).astype(jnp.float32)
     one = two[2:] + shifted(two[:2].astype(jnp.bfloat16), -2).astype(jnp.float32) + far
-    return one[1] + shifted(one[:1].astype(jnp.bfloat16), -1).astype(jnp.float32)[0]
+    total = one[1] + shifted(one[:1].astype(jnp.bfloat16), -1).astype(jnp.float32)[0]
+    one, held = lax.optimization_barrier((one, held))
+    return total, held
 
 
 def per_device(queries, keys, values, out_weight, out_grad, doc_ids, block_mask, positions):
@@ -183,6 +185,7 @@
         stripes.reshape(attn.shape[1], n_seq, kv_count, col_w),
         preferred_element_type=jnp.float32,
     ).astype(jnp.bfloat16)
+    dkv_total, lo_part = return_window(dkv, lo_part)
     total = lax.dynamic_index_in_dim(lo_part, kv_me, 0, keepdims=False).astype(jnp.float32)
     for j in range(1, kv_count):
         dest = (kv_me + j) % kv_count
@@ -190,7 +193,6 @@
         got = lax.ppermute(piece, "kv", [(i, (i + j) % kv_count) for i in range(kv_count)])
         total = total + got.astype(jnp.float32)
     layer_out = total.reshape(length, n_seq * col_w).astype(jnp.bfloat16)
-    dkv_total = return_window(dkv)
     dk_total = dkv_total[:, :HD]
     dv_total = dkv_total[:, HD:]
     query_grad = rotate(dq_rot, cosine, sine, -1.0).astype(jnp.bfloat16).reshape(length, heads * HD)

time: 252 us -> 266 us (1.056)
  waiting for transfers between devices: 93.7 us -> 114 us
  starting transfers between devices: 58 us -> 52.4 us
    ppermute x7, waiting for transfers between devices: 2.05 us -> 20.3 us  [per_device(): lax.ppermute(piece, 'kv', [(i, (i + j) % kv_count) for i in range(kv_coun...]
    ppermute x7, starting transfers between devices: 20.8 us -> 17 us  [per_device(): lax.ppermute(piece, 'kv', [(i, (i + j) % kv_count) for i in range(kv_coun...]
    unnamed x65 -> x63, local copies, waits for them, and re-layouts: 16.8 us -> 17.9 us
  transfers between devices with their start and end apart: 23 -> 23, of which waited for: 8 -> 11; matrix products, arithmetic and copies ran while one was open for 20% -> 18% of each run, Pallas kernels for 0% -> 0%
where the time goes in v6:
time: 266 us; the launch traced here: 264 us
  waiting for transfers between devices  114 us (43%)
  starting transfers between devices  52.4 us (20%)
  local copies, waits for them, and re-layouts  27.5 us (10%)
  matrix products  26.5 us (10%)
  other arithmetic  15 us (6%)
  between operations  14.8 us (6%)
  blocking collectives  13.7 us (5%)
    all_gather x1, waiting for transfers between devices, per_device(): stripes = lax.all_gather(pieces, SEQ, axis=1, tiled=True)  71.8 us
    ppermute x8, starting transfers between devices, shifted(): return lax.ppermute(block, SEQ, route)  30.5 us
    ppermute x7, waiting for transfers between devices, per_device(): lax.ppermute(piece, 'kv', [(i, (i + j) % kv_count) for i in range(kv_coun...  20.3 us
    ppermute x8, waiting for transfers between devices, shifted(): return lax.ppermute(block, SEQ, route)  19.8 us
    unnamed x63, local copies, waits for them, and re-layouts  17.9 us
    ppermute x7, starting transfers between devices, per_device(): lax.ppermute(piece, 'kv', [(i, (i + j) % kv_count) for i in range(kv_coun...  17 us
    all_to_all x1, blocking collectives, per_device(): lax.all_to_all(out_weight, 'kv', split_axis=0, concat_axis=1, tiled=True)  13.7 us
    dot_general x1, matrix products, per_device(): lax.dot_general(og_perm, stripes, contract, preferred_element_type=jnp.fl...  8.76 us
  transfers between devices with their start and end apart: 23, of which 11 were waited for; matrix products, arithmetic and copies ran while one was open for 18% of the time, Pallas kernels for 0%

profile of v6, /device:TPU:97, one launch (start us, length us, event | category | flops | bytes accessed | tf_op | source)
XLA Modules:
  0.0 263.8 jit_solution(13202057793623129686)
XLA Ops:
  7.2 1.1 copy.127
  8.3 13.7 %all_to_all.19 = bf16[8,1024,32]{1,2,0:T(8,128)(2,1)} all-to-all(bf16[8,1024,32]{1,2,0:T(8,128)(2,1)S(1)} %bitcast.139), channel_id=1, replica_groups=mesh['sz'=16,'core'=2,'kv'=8] {'kv'}, dimensions={0} | all-to-all | bytes 1048576 | tf_op jit(solution)/shard_map/all_to_all | solution.py:135
  22.0 1.1 copy.88
  23.1 1.9 collective-permute-start.4
  25.0 1.2 collective-permute-start.5
  27.6 1.3 fusion.32
  30.9 6.8 %collective-permute-start = (bf16[1,129,256]{2,1,0:T(8,128)(2,1)S(1)}, bf16[1,129,256]{2,1,0:T(8,128)(2,1)S(1)}, u32[]{:S(2)}, u32[]{:S(2)}) collective-permute-start(bf16[1,129,256]{2,1,0:T(8,128)(2,1)S(1)} %fusion.17), channel_id=1, source_target_pairs={{0,8},{8,16},{16,24},{24,32},{32,40},{40,48},{48,56},{56,64},{64,7... | collective-permute-start | bytes 198152 | tf_op jit(solution)/shard_map/ppermute | solution.py:30
  37.8 1.1 copy.83
  40.2 1.0 broadcast_multiply_fusion
  41.4 9.2 %collective-permute-done = bf16[1,129,256]{2,1,0:T(8,128)(2,1)S(1)} collective-permute-done((bf16[1,129,256]{2,1,0:T(8,128)(2,1)S(1)}, bf16[1,129,256]{2,1,0:T(8,128)(2,1)S(1)}, u32[]{:S(2)}, u32[]{:S(2)}) %collective-permute-start) | collective-permute-done | bytes 66080 | tf_op jit(solution)/shard_map/ppermute | solution.py:30
  50.6 1.9 collective-permute-start.2
  52.6 5.2 %collective-permute-start.1 = (bf16[2,129,256]{2,1,0:T(8,128)(2,1)S(1)}, bf16[2,129,256]{2,1,0:T(8,128)(2,1)S(1)}, u32[]{:S(2)}, u32[]{:S(2)}) collective-permute-start(bf16[2,129,256]{2,1,0:T(8,128)(2,1)S(1)} %pad_maximum_fusion.4), channel_id=1, source_target_pairs={{0,64},{8,72},{16,80},{24,88},{32,96},{40,104},{48,112},{56,120},{... | collective-permute-start | bytes 396296 | tf_op jit(solution)/shard_map/ppermute | solution.py:30
  57.9 5.3 %collective-permute-done.2 = bf16[2,129,256]{2,1,0:T(8,128)(2,1)S(1)} collective-permute-done((bf16[2,129,256]{2,1,0:T(8,128)(2,1)S(1)}, bf16[2,129,256]{2,1,0:T(8,128)(2,1)S(1)}, u32[]{:S(2)}, u32[]{:S(2)}) %collective-permute-start.2) | collective-permute-done | bytes 132128 | tf_op jit(solution)/shard_map/ppermute | solution.py:30
  63.2 1.1 collective-permute-done.1
  65.2 1.6 collective-permute-start.10
  67.6 6.1 %collective-permute-start.3 = (bf16[4,129,256]{2,1,0:T(8,128)(2,1)S(1)}, bf16[4,129,256]{2,1,0:T(8,128)(2,1)S(1)}, u32[]{:S(2)}, u32[]{:S(2)}) collective-permute-start(bf16[4,129,256]{2,1,0:T(8,128)(2,1)S(1)} %pad_maximum_fusion.1), channel_id=1, source_target_pairs={{0,32},{8,40},{16,48},{24,56},{32,64},{40,72},{48,80},{56,88},{64,... | collective-permute-start | bytes 792584 | tf_op jit(solution)/shard_map/ppermute | solution.py:30
  76.6 2.2 collective-permute-done.10
  85.2 2.0 constant_dynamic-slice_fusion
  87.3 1.9 copy.96
  89.6 1.4 or_and_fusion
  91.1 4.2 %exponential_reduce_fusion = (f32[8,128]{1,0:T(8,128)S(1)}, f32[8,128,1280]{1,2,0:T(8,128)}) fusion(bf16[1280,128,1]{1,0,2:T(8,128)(2,1)S(1)} %bitcast.140, pred[128,1280]{0,1:T(8,128)(4,1)S(1)} %or_and_fusion, bf16[128,8,64]{2,0,1:T(8,128)(2,1)S(1)} %get-tuple-element.46, bf16[128,8,64]{2,0,1:T(8,128)(2,1)S(1)} %get-tuple-element.45), kind=kOutput, calls=%fused_computation.7 | convolution fusion | flops 341312768 | bytes 6000640 | tf_op jit(solution)/shard_map/sub | solution.py:168
  95.3 3.2 %divide_convert_fusion = bf16[8,128,1280]{1,2,0:T(8,128)(2,1)S(1)} fusion(f32[8,128,1280]{1,2,0:T(8,128)} %get-tuple-element.64, f32[8,128]{1,0:T(8,128)S(1)} %get-tuple-element.63), kind=kLoop, calls=%fused_computation.6 | loop fusion | flops 2621440 | bytes 7868416 | tf_op jit(solution)/shard_map/convert_element_type | solution.py:169
  98.5 71.8 %all-gather.2.cloned.1.call-done = bf16[1024,8192]{0,1:T(8,128)(2,1)} async-done(((bf16[1024,256]{0,1:T(8,128)(2,1)}), bf16[1024,8192]{0,1:T(8,128)(2,1)}) %all-gather.2.cloned.1.call-update) | async-done | bytes 16777232 | tf_op jit(solution)/shard_map/all_gather | solution.py:136
  170.2 8.8 %convolution_convert_fusion.1 = bf16[128,1024]{1,0:T(8,128)(2,1)S(1)} fusion(bf16[128,8192]{0,1:T(8,128)(2,1)} %bitcast.128, bf16[1024,8192]{0,1:T(8,128)(2,1)} %all-gather.2.cloned.1.call-done), kind=kOutput, calls=%fused_computation.16 | convolution fusion | flops 2147614720 | bytes 19136512 | tf_op jit(solution)/shard_map/dot_general | solution.py:144
  179.2 1.3 multiply_reduce_fusion
  180.4 1.0 convolution_bitcast_fusion
  182.3 1.5 copy-done
  183.7 1.1 fusion.4
  186.1 1.9 collective-permute-start.11
  188.0 3.0 %collective-permute-start.13 = (bf16[2,128,256]{2,1,0:T(8,128)(2,1)}, bf16[2,128,256]{2,1,0:T(8,128)(2,1)}, u32[]{:S(2)}, u32[]{:S(2)}) collective-permute-start(bf16[2,128,256]{2,1,0:T(8,128)(2,1)} %slice.126), channel_id=1, source_target_pairs={{64,0},{72,8},{80,16},{88,24},{96,32},{104,40},{112,48},{120,56},{... | collective-permute-start | bytes 393224 | tf_op jit(solution)/shard_map/ppermute | solution.py:30
  191.1 8.3 %fusion.38 = f32[128,8192]{0,1:S(1)} fusion(bf16[1024,8192]{0,1:T(8,128)(2,1)} %all-gather.2.cloned.1.call-done, bf16[128,1024]{0,1:T(8,128)(2,1)S(1)} %bitcast.142), kind=kOutput, calls=%fused_computation.135 | convolution fusion | flops 2147483648 | bytes 21233664
  199.9 1.2 copy-done.1
  201.1 1.1 fusion.5
  203.1 1.0 slice.180
  204.0 1.9 collective-permute-start.12
  206.6 0.9 copy.110
  207.5 4.2 %collective-permute-done.12 = bf16[2,128,256]{2,1,0:T(8,128)(2,1)S(1)} collective-permute-done((bf16[2,128,256]{2,1,0:T(8,128)(2,1)S(1)}, bf16[2,128,256]{2,1,0:T(8,128)(2,1)S(1)}, u32[]{:S(2)}, u32[]{:S(2)}) %collective-permute-start.12) | collective-permute-done | bytes 131104 | tf_op jit(solution)/shard_map/ppermute | solution.py:30
  211.7 1.0 fusion.13
  212.7 3.6 %collective-permute-start.21 = (bf16[1,128,256]{2,1,0:T(8,128)(2,1)S(1)}, bf16[1,128,256]{2,1,0:T(8,128)(2,1)S(1)}, u32[]{:S(2)}, u32[]{:S(2)}) collective-permute-start(bf16[1,128,256]{2,1,0:T(8,128)(2,1)S(1)} %slice.181), channel_id=1, source_target_pairs={{8,0},{16,8},{24,16},{32,24},{40,32},{48,40},{56,48},{64,56},{72,6... | collective-permute-start | bytes 196616 | tf_op jit(solution)/shard_map/ppermute | solution.py:30
  216.8 2.5 collective-permute-start.20
  219.8 1.5 collective-permute-start.18
  221.6 2.1 collective-permute-start.16
  224.3 5.1 %collective-permute-done.20 = bf16[128,32,32]{0,2,1:T(8,128)(2,1)S(1)} collective-permute-done((bf16[128,32,32]{0,2,1:T(8,128)(2,1)S(1)}, bf16[128,32,32]{0,2,1:T(8,128)(2,1)S(1)}, u32[]{:S(2)}, u32[]{:S(2)}) %collective-permute-start.20) | collective-permute-done | bytes 262176 | tf_op jit(solution)/shard_map/ppermute | solution.py:193
  229.4 8.9 %collective-permute-done.19 = bf16[128,32,32]{0,2,1:T(8,128)(2,1)S(1)} collective-permute-done((bf16[128,32,32]{0,2,1:T(8,128)(2,1)S(1)}, bf16[128,32,32]{0,2,1:T(8,128)(2,1)S(1)}, u32[]{:S(2)}, u32[]{:S(2)}) %collective-permute-start.19) | collective-permute-done | bytes 262176 | tf_op jit(solution)/shard_map/ppermute | solution.py:193
  238.3 10.1 %collective-permute-start.14 = (bf16[128,32,32]{0,2,1:T(8,128)(2,1)S(1)}, bf16[128,32,32]{0,2,1:T(8,128)(2,1)S(1)}, u32[]{:S(2)}, u32[]{:S(2)}) collective-permute-start(bf16[128,32,32]{0,2,1:T(8,128)(2,1)S(1)} %get-tuple-element.38), channel_id=1, source_target_pairs={{0,1},{1,2},{2,3},{3,4},{4,5},{5,6},{6,7},{7,0},{8,9},{9,10},{10,1... | collective-permute-start | bytes 786440 | tf_op jit(solution)/shard_map/ppermute | solution.py:193
  249.5 2.9 %collective-permute-done.17 = bf16[128,32,32]{0,2,1:T(8,128)(2,1)S(1)} collective-permute-done((bf16[128,32,32]{0,2,1:T(8,128)(2,1)S(1)}, bf16[128,32,32]{0,2,1:T(8,128)(2,1)S(1)}, u32[]{:S(2)}, u32[]{:S(2)}) %collective-permute-start.17) | collective-permute-done | bytes 262176 | tf_op jit(solution)/shard_map/ppermute | solution.py:193
  252.4 2.5 collective-permute-done.15
  254.8 1.0 collective-permute-done.14
  (121 shorter events, 24.7 us)
Async XLA Ops:
  7.2 32.2 %copy-start.18 = (s32[1,32]{1,0:T(1,128)S(1)}, s32[1,32]{1,0:T(1,128)}, u32[]{:S(2)}) copy-start(s32[1,32]{1,0:T(1,128)} %param.16) | copy-start | bytes 388
  7.2 163.0 %all-gather.2.cloned.1.call-start = ((), (), s32[]{:S(2)}) async-start(), calls=%async_computation.1 | async-start | bytes 17301504 | tf_op jit(solution)/shard_map/all_gather | solution.py:136
  23.1 41.3 %collective-permute-start.4 = (bf16[128,1024]{0,1:T(8,128)(2,1)S(1)}, bf16[128,1024]{0,1:T(8,128)(2,1)S(1)}, u32[]{:S(2)}, u32[]{:S(2)}) collective-permute-start(bf16[128,1024]{0,1:T(8,128)(2,1)S(1)} %copy.88), channel_id=1, source_target_pairs={{0,7},{1,0},{2,1},{3,2},{4,3},{5,4},{6,5},{7,6},{8,15},{9,8},{10,9... | collective-permute-start | bytes 786440 | tf_op jit(solution)/shard_map/ppermute | solution.py:139
  25.0 40.3 %collective-permute-start.5 = (bf16[128,1024]{0,1:T(8,128)(2,1)S(1)}, bf16[128,1024]{0,1:T(8,128)(2,1)S(1)}, u32[]{:S(2)}, u32[]{:S(2)}) collective-permute-start(bf16[128,1024]{0,1:T(8,128)(2,1)S(1)} %copy.88), channel_id=1, source_target_pairs={{0,6},{1,7},{2,0},{3,1},{4,2},{5,3},{6,4},{7,5},{8,14},{9,15},{10,... | collective-permute-start | bytes 786440 | tf_op jit(solution)/shard_map/ppermute | solution.py:139
  26.2 41.3 %collective-permute-start.6 = (bf16[128,1024]{0,1:T(8,128)(2,1)S(1)}, bf16[128,1024]{0,1:T(8,128)(2,1)S(1)}, u32[]{:S(2)}, u32[]{:S(2)}) collective-permute-start(bf16[128,1024]{0,1:T(8,128)(2,1)S(1)} %copy.88), channel_id=1, source_target_pairs={{0,5},{1,6},{2,7},{3,0},{4,1},{5,2},{6,3},{7,4},{8,13},{9,14},{10,... | collective-permute-start | bytes 786440 | tf_op jit(solution)/shard_map/ppermute | solution.py:139
  27.5 23.1 %copy-start.11 = (pred[64]{0:T(512)(128)(4,1)}, pred[64]{0:T(512)(128)(4,1)S(1)}, u32[]{:S(2)}) copy-start(pred[64]{0:T(512)(128)(4,1)S(1)} %broadcast_compare_fusion.2) | copy-start | bytes 196
  27.6 40.0 %copy-start.13 = (pred[64]{0:T(512)(128)(4,1)}, pred[64]{0:T(512)(128)(4,1)S(1)}, u32[]{:S(2)}) copy-start(pred[64]{0:T(512)(128)(4,1)S(1)} %get-tuple-element.67) | copy-start | bytes 196
  27.6 40.0 %copy-start.15 = (pred[64]{0:T(512)(128)(4,1)}, pred[64]{0:T(512)(128)(4,1)S(1)}, u32[]{:S(2)}) copy-start(pred[64]{0:T(512)(128)(4,1)S(1)} %get-tuple-element.68) | copy-start | bytes 196
  30.9 19.7 %collective-permute-start = (bf16[1,129,256]{2,1,0:T(8,128)(2,1)S(1)}, bf16[1,129,256]{2,1,0:T(8,128)(2,1)S(1)}, u32[]{:S(2)}, u32[]{:S(2)}) collective-permute-start(bf16[1,129,256]{2,1,0:T(8,128)(2,1)S(1)} %fusion.17), channel_id=1, source_target_pairs={{0,8},{8,16},{16,24},{24,32},{32,40},{40,48},{48,56},{56,64},{64,7... | collective-permute-start | bytes 198152 | tf_op jit(solution)/shard_map/ppermute | solution.py:30
  41.4 49.7 %copy-start.5 = (bf16[128,8,64]{2,0,1:T(8,128)(2,1)}, bf16[128,8,64]{2,0,1:T(8,128)(2,1)S(1)}, u32[]{:S(2)}) copy-start(bf16[128,8,64]{2,0,1:T(8,128)(2,1)S(1)} %get-tuple-element.45) | copy-start | bytes 393220
  41.4 49.7 %copy-start.7 = (bf16[128,8,64]{2,0,1:T(8,128)(2,1)}, bf16[128,8,64]{2,0,1:T(8,128)(2,1)S(1)}, u32[]{:S(2)}) copy-start(bf16[128,8,64]{2,0,1:T(8,128)(2,1)S(1)} %get-tuple-element.46) | copy-start | bytes 393220
  50.6 12.6 %collective-permute-start.2 = (bf16[2,129,256]{2,1,0:T(8,128)(2,1)S(1)}, bf16[2,129,256]{2,1,0:T(8,128)(2,1)S(1)}, u32[]{:S(2)}, u32[]{:S(2)}) collective-permute-start(bf16[2,129,256]{2,1,0:T(8,128)(2,1)S(1)} %pad_maximum_fusion.4), channel_id=1, source_target_pairs={{0,16},{8,24},{16,32},{24,40},{32,48},{40,56},{48,64},{56,72},{64,... | collective-permute-start | bytes 396296 | tf_op jit(solution)/shard_map/ppermute | solution.py:30
  52.6 11.8 %collective-permute-start.1 = (bf16[2,129,256]{2,1,0:T(8,128)(2,1)S(1)}, bf16[2,129,256]{2,1,0:T(8,128)(2,1)S(1)}, u32[]{:S(2)}, u32[]{:S(2)}) collective-permute-start(bf16[2,129,256]{2,1,0:T(8,128)(2,1)S(1)} %pad_maximum_fusion.4), channel_id=1, source_target_pairs={{0,64},{8,72},{16,80},{24,88},{32,96},{40,104},{48,112},{56,120},{... | collective-permute-start | bytes 396296 | tf_op jit(solution)/shard_map/ppermute | solution.py:30
  63.2 11.2 %collective-permute-start.7 = (bf16[128,1024]{0,1:T(8,128)(2,1)S(1)}, bf16[128,1024]{0,1:T(8,128)(2,1)S(1)}, u32[]{:S(2)}, u32[]{:S(2)}) collective-permute-start(bf16[128,1024]{0,1:T(8,128)(2,1)S(1)} %copy.88), channel_id=1, source_target_pairs={{0,4},{1,5},{2,6},{3,7},{4,0},{5,1},{6,2},{7,3},{8,12},{9,13},{10,... | collective-permute-start | bytes 786440 | tf_op jit(solution)/shard_map/ppermute | solution.py:139
  64.4 10.7 %collective-permute-start.8 = (bf16[128,1024]{0,1:T(8,128)(2,1)S(1)}, bf16[128,1024]{0,1:T(8,128)(2,1)S(1)}, u32[]{:S(2)}, u32[]{:S(2)}) collective-permute-start(bf16[128,1024]{0,1:T(8,128)(2,1)S(1)} %copy.88), channel_id=1, source_target_pairs={{0,3},{1,4},{2,5},{3,6},{4,7},{5,0},{6,1},{7,2},{8,11},{9,12},{10,... | collective-permute-start | bytes 786440 | tf_op jit(solution)/shard_map/ppermute | solution.py:139
  64.4 11.4 %collective-permute-start.9 = (bf16[128,1024]{0,1:T(8,128)(2,1)S(1)}, bf16[128,1024]{0,1:T(8,128)(2,1)S(1)}, u32[]{:S(2)}, u32[]{:S(2)}) collective-permute-start(bf16[128,1024]{0,1:T(8,128)(2,1)S(1)} %copy.88), channel_id=1, source_target_pairs={{0,2},{1,3},{2,4},{3,5},{4,6},{5,7},{6,0},{7,1},{8,10},{9,11},{10,... | collective-permute-start | bytes 786440 | tf_op jit(solution)/shard_map/ppermute | solution.py:139
  65.2 13.5 %collective-permute-start.10 = (bf16[128,1024]{0,1:T(8,128)(2,1)S(1)}, bf16[128,1024]{0,1:T(8,128)(2,1)S(1)}, u32[]{:S(2)}, u32[]{:S(2)}) collective-permute-start(bf16[128,1024]{0,1:T(8,128)(2,1)S(1)} %copy.88), channel_id=1, source_target_pairs={{0,1},{1,2},{2,3},{3,4},{4,5},{5,6},{6,7},{7,0},{8,9},{9,10},{10,1... | collective-permute-start | bytes 786440 | tf_op jit(solution)/shard_map/ppermute | solution.py:139
  67.6 21.7 %collective-permute-start.3 = (bf16[4,129,256]{2,1,0:T(8,128)(2,1)S(1)}, bf16[4,129,256]{2,1,0:T(8,128)(2,1)S(1)}, u32[]{:S(2)}, u32[]{:S(2)}) collective-permute-start(bf16[4,129,256]{2,1,0:T(8,128)(2,1)S(1)} %pad_maximum_fusion.1), channel_id=1, source_target_pairs={{0,32},{8,40},{16,48},{24,56},{32,64},{40,72},{48,80},{56,88},{64,... | collective-permute-start | bytes 792584 | tf_op jit(solution)/shard_map/ppermute | solution.py:30
  85.2 4.1 %copy-start.10 = (bf16[128,128]{1,0:T(8,128)(2,1)S(1)}, bf16[128,128]{1,0:T(8,128)(2,1)}, u32[]{:S(2)}) copy-start(bf16[128,128]{1,0:T(8,128)(2,1)} %param.12) | copy-start | bytes 98308
  87.3 2.4 copy-start.17
  89.6 5.7 %copy-start.2 = (bf16[10,128,128]{2,1,0:T(8,128)(2,1)}, bf16[10,128,128]{2,1,0:T(8,128)(2,1)S(1)}, u32[]{:S(2)}) copy-start(bf16[10,128,128]{2,1,0:T(8,128)(2,1)S(1)} %get-tuple-element.47) | copy-start | bytes 983044
  181.4 2.3 copy-start.6
  181.4 2.3 copy-start.8
  182.3 1.5 copy-start
  184.8 6.2 %copy-start.4 = (bf16[128,8,128]{2,0,1:T(8,128)(2,1)S(1)}, bf16[128,8,128]{2,0,1:T(8,128)(2,1)}, u32[]{:S(2)}) copy-start(bf16[128,8,128]{2,0,1:T(8,128)(2,1)} %get-tuple-element.66) | copy-start | bytes 786436
  186.1 16.1 %collective-permute-start.11 = (bf16[4,128,256]{2,1,0:T(8,128)(2,1)S(1)}, bf16[4,128,256]{2,1,0:T(8,128)(2,1)S(1)}, u32[]{:S(2)}, u32[]{:S(2)}) collective-permute-start(bf16[4,128,256]{2,1,0:T(8,128)(2,1)S(1)} %slice.123), channel_id=1, source_target_pairs={{32,0},{40,8},{48,16},{56,24},{64,32},{72,40},{80,48},{88,56},{96,... | collective-permute-start | bytes 786440 | tf_op jit(solution)/shard_map/ppermute | solution.py:30
  188.0 19.5 %collective-permute-start.13 = (bf16[2,128,256]{2,1,0:T(8,128)(2,1)}, bf16[2,128,256]{2,1,0:T(8,128)(2,1)}, u32[]{:S(2)}, u32[]{:S(2)}) collective-permute-start(bf16[2,128,256]{2,1,0:T(8,128)(2,1)} %slice.126), channel_id=1, source_target_pairs={{64,0},{72,8},{80,16},{88,24},{96,32},{104,40},{112,48},{120,56},{... | collective-permute-start | bytes 393224 | tf_op jit(solution)/shard_map/ppermute | solution.py:30
  199.3 1.7 copy-start.1
  199.3 1.8 copy-start.3
  199.3 6.6 %copy-start.9 = (f32[128,64]{1,0:T(8,128)S(1)}, f32[128,64]{1,0:T(8,128)}, u32[]{:S(2)}) copy-start(f32[128,64]{1,0:T(8,128)} %get-tuple-element.57) | copy-start | bytes 98308
  204.0 7.6 %collective-permute-start.12 = (bf16[2,128,256]{2,1,0:T(8,128)(2,1)S(1)}, bf16[2,128,256]{2,1,0:T(8,128)(2,1)S(1)}, u32[]{:S(2)}, u32[]{:S(2)}) collective-permute-start(bf16[2,128,256]{2,1,0:T(8,128)(2,1)S(1)} %slice.180), channel_id=1, source_target_pairs={{16,0},{24,8},{32,16},{40,24},{48,32},{56,40},{64,48},{72,56},{80,... | collective-permute-start | bytes 393224 | tf_op jit(solution)/shard_map/ppermute | solution.py:30
  206.0 42.4 %copy-start.12 = (pred[64]{0:T(512)(128)(4,1)S(1)}, pred[64]{0:T(512)(128)(4,1)}, u32[]{:S(2)}) copy-start(pred[64]{0:T(512)(128)(4,1)} %copy-done.11) | copy-start | bytes 196
  206.0 42.4 %copy-start.14 = (pred[64]{0:T(512)(128)(4,1)S(1)}, pred[64]{0:T(512)(128)(4,1)}, u32[]{:S(2)}) copy-start(pred[64]{0:T(512)(128)(4,1)} %copy-done.13) | copy-start | bytes 196
  206.0 42.4 %copy-start.16 = (pred[64]{0:T(512)(128)(4,1)S(1)}, pred[64]{0:T(512)(128)(4,1)}, u32[]{:S(2)}) copy-start(pred[64]{0:T(512)(128)(4,1)} %copy-done.15) | copy-start | bytes 196
  212.7 8.9 %collective-permute-start.21 = (bf16[1,128,256]{2,1,0:T(8,128)(2,1)S(1)}, bf16[1,128,256]{2,1,0:T(8,128)(2,1)S(1)}, u32[]{:S(2)}, u32[]{:S(2)}) collective-permute-start(bf16[1,128,256]{2,1,0:T(8,128)(2,1)S(1)} %slice.181), channel_id=1, source_target_pairs={{8,0},{16,8},{24,16},{32,24},{40,32},{48,40},{56,48},{64,56},{72,6... | collective-permute-start | bytes 196616 | tf_op jit(solution)/shard_map/ppermute | solution.py:30
  216.8 12.7 %collective-permute-start.20 = (bf16[128,32,32]{0,2,1:T(8,128)(2,1)S(1)}, bf16[128,32,32]{0,2,1:T(8,128)(2,1)S(1)}, u32[]{:S(2)}, u32[]{:S(2)}) collective-permute-start(bf16[128,32,32]{0,2,1:T(8,128)(2,1)S(1)} %get-tuple-element.39), channel_id=1, source_target_pairs={{0,7},{1,0},{2,1},{3,2},{4,3},{5,4},{6,5},{7,6},{8,15},{9,8},{10,9... | collective-permute-start | bytes 786440 | tf_op jit(solution)/shard_map/ppermute | solution.py:193
  219.3 19.0 %collective-permute-start.19 = (bf16[128,32,32]{0,2,1:T(8,128)(2,1)S(1)}, bf16[128,32,32]{0,2,1:T(8,128)(2,1)S(1)}, u32[]{:S(2)}, u32[]{:S(2)}) collective-permute-start(bf16[128,32,32]{0,2,1:T(8,128)(2,1)S(1)} %get-tuple-element.40), channel_id=1, source_target_pairs={{0,6},{1,7},{2,0},{3,1},{4,2},{5,3},{6,4},{7,5},{8,14},{9,15},{10,... | collective-permute-start | bytes 786440 | tf_op jit(solution)/shard_map/ppermute | solution.py:193
  219.8 29.7 %collective-permute-start.18 = (bf16[128,32,32]{0,2,1:T(8,128)(2,1)S(1)}, bf16[128,32,32]{0,2,1:T(8,128)(2,1)S(1)}, u32[]{:S(2)}, u32[]{:S(2)}) collective-permute-start(bf16[128,32,32]{0,2,1:T(8,128)(2,1)S(1)} %get-tuple-element.41), channel_id=1, source_target_pairs={{0,5},{1,6},{2,7},{3,0},{4,1},{5,2},{6,3},{7,4},{8,13},{9,14},{10,... | collective-permute-start | bytes 786440 | tf_op jit(solution)/shard_map/ppermute | solution.py:193
  221.3 31.0 %collective-permute-start.17 = (bf16[128,32,32]{0,2,1:T(8,128)(2,1)S(1)}, bf16[128,32,32]{0,2,1:T(8,128)(2,1)S(1)}, u32[]{:S(2)}, u32[]{:S(2)}) collective-permute-start(bf16[128,32,32]{0,2,1:T(8,128)(2,1)S(1)} %get-tuple-element.42), channel_id=1, source_target_pairs={{0,4},{1,5},{2,6},{3,7},{4,0},{5,1},{6,2},{7,3},{8,12},{9,13},{10,... | collective-permute-start | bytes 786440 | tf_op jit(solution)/shard_map/ppermute | solution.py:193
  221.6 30.8 %collective-permute-start.16 = (bf16[128,32,32]{0,2,1:T(8,128)(2,1)S(1)}, bf16[128,32,32]{0,2,1:T(8,128)(2,1)S(1)}, u32[]{:S(2)}, u32[]{:S(2)}) collective-permute-start(bf16[128,32,32]{0,2,1:T(8,128)(2,1)S(1)} %get-tuple-element.43), channel_id=1, source_target_pairs={{0,3},{1,4},{2,5},{3,6},{4,7},{5,0},{6,1},{7,2},{8,11},{9,12},{10,... | collective-permute-start | bytes 786440 | tf_op jit(solution)/shard_map/ppermute | solution.py:193
  229.4 25.4 %collective-permute-start.15 = (bf16[128,32,32]{0,2,1:T(8,128)(2,1)S(1)}, bf16[128,32,32]{0,2,1:T(8,128)(2,1)S(1)}, u32[]{:S(2)}, u32[]{:S(2)}) collective-permute-start(bf16[128,32,32]{0,2,1:T(8,128)(2,1)S(1)} %get-tuple-element.44), channel_id=1, source_target_pairs={{0,2},{1,3},{2,4},{3,5},{4,6},{5,7},{6,0},{7,1},{8,10},{9,11},{10,... | collective-permute-start | bytes 786440 | tf_op jit(solution)/shard_map/ppermute | solution.py:193
  238.3 17.5 %collective-permute-start.14 = (bf16[128,32,32]{0,2,1:T(8,128)(2,1)S(1)}, bf16[128,32,32]{0,2,1:T(8,128)(2,1)S(1)}, u32[]{:S(2)}, u32[]{:S(2)}) collective-permute-start(bf16[128,32,32]{0,2,1:T(8,128)(2,1)S(1)} %get-tuple-element.38), channel_id=1, source_target_pairs={{0,1},{1,2},{2,3},{3,4},{4,5},{5,6},{6,7},{7,0},{8,9},{9,10},{10,1... | collective-permute-start | bytes 786440 | tf_op jit(solution)/shard_map/ppermute | solution.py:193
Sparse Core Ops, SparseCore 0:
  22.1 148.0 all-gather.1

commit v7 on v1

--- a/solution.py
+++ b/solution.py
@@ -184,7 +184,7 @@
         preferred_element_type=jnp.float32,
     ).astype(jnp.bfloat16)
     total = lax.dynamic_index_in_dim(lo_part, kv_me, 0, keepdims=False).astype(jnp.float32)
-    for j in range(1, kv_count):
+    for j in range(kv_count - 1, 0, -1):
         dest = (kv_me + j) % kv_count
         piece = lax.dynamic_index_in_dim(lo_part, dest, 0, keepdims=False)
         got = lax.ppermute(piece, "kv", [(i, (i + j) % kv_count) for i in range(kv_count)])

time: 252 us -> 254 us (level)
  starting transfers between devices: 58 us -> 52.6 us
  waiting for transfers between devices: 93.7 us -> 98.7 us
    ppermute x7, starting transfers between devices: 20.8 us -> 16 us  [per_device(): lax.ppermute(piece, 'kv', [(i, (i + j) % kv_count) for i in range(kv_coun...]
    ppermute x7, waiting for transfers between devices: 2.05 us -> 5.42 us  [per_device(): lax.ppermute(piece, 'kv', [(i, (i + j) % kv_count) for i in range(kv_coun...]
where the time goes in v7:
time: 254 us; the launch traced here: 250 us
  waiting for transfers between devices  98.7 us (39%)
  starting transfers between devices  52.6 us (21%)
  local copies, waits for them, and re-layouts  27.1 us (11%)
  matrix products  26.5 us (10%)
  other arithmetic  16.9 us (7%)
  between operations  14.8 us (6%)
  blocking collectives  13.7 us (5%)
    all_gather x1, waiting for transfers between devices, per_device(): stripes = lax.all_gather(pieces, SEQ, axis=1, tiled=True)  71.7 us
    ppermute x8, starting transfers between devices, shifted(): return lax.ppermute(block, SEQ, route)  31.8 us
    ppermute x8, waiting for transfers between devices, shifted(): return lax.ppermute(block, SEQ, route)  19.4 us
    unnamed x65, local copies, waits for them, and re-layouts  17.5 us
    ppermute x7, starting transfers between devices, per_device(): lax.ppermute(piece, 'kv', [(i, (i + j) % kv_count) for i in range(kv_coun...  16 us
    all_to_all x1, blocking collectives, per_device(): lax.all_to_all(out_weight, 'kv', split_axis=0, concat_axis=1, tiled=True)  13.7 us
    dot_general x1, matrix products, per_device(): lax.dot_general(og_perm, stripes, contract, preferred_element_type=jnp.fl...  8.76 us
    unnamed x1, matrix products  8.26 us
  transfers between devices with their start and end apart: 23, of which 8 were waited for; matrix products, arithmetic and copies ran while one was open for 20% of the time, Pallas kernels for 0%

profile of v7, /device:TPU:97, one launch (start us, length us, event | category | flops | bytes accessed | tf_op | source)
XLA Modules:
  0.0 250.3 jit_solution(17095628520514498254)
XLA Ops:
  7.2 1.1 copy.127
  8.3 13.7 %all_to_all.19 = bf16[8,1024,32]{1,2,0:T(8,128)(2,1)} all-to-all(bf16[8,1024,32]{1,2,0:T(8,128)(2,1)S(1)} %bitcast.137), channel_id=1, replica_groups=mesh['sz'=16,'core'=2,'kv'=8] {'kv'}, dimensions={0} | all-to-all | bytes 1048576 | tf_op jit(solution)/shard_map/all_to_all | solution.py:133
  22.0 1.1 copy.88
  23.1 1.9 collective-permute-start.4
  25.0 1.2 collective-permute-start.5
  27.6 1.3 fusion.32
  30.9 6.8 %collective-permute-start = (bf16[1,129,256]{2,1,0:T(8,128)(2,1)S(1)}, bf16[1,129,256]{2,1,0:T(8,128)(2,1)S(1)}, u32[]{:S(2)}, u32[]{:S(2)}) collective-permute-start(bf16[1,129,256]{2,1,0:T(8,128)(2,1)S(1)} %fusion.17), channel_id=1, source_target_pairs={{0,8},{8,16},{16,24},{24,32},{32,40},{40,48},{48,56},{56,64},{64,7... | collective-permute-start | bytes 198152 | tf_op jit(solution)/shard_map/ppermute | solution.py:30
  37.8 1.1 copy.83
  40.2 1.0 broadcast_multiply_fusion
  41.4 9.2 %collective-permute-done = bf16[1,129,256]{2,1,0:T(8,128)(2,1)S(1)} collective-permute-done((bf16[1,129,256]{2,1,0:T(8,128)(2,1)S(1)}, bf16[1,129,256]{2,1,0:T(8,128)(2,1)S(1)}, u32[]{:S(2)}, u32[]{:S(2)}) %collective-permute-start) | collective-permute-done | bytes 66080 | tf_op jit(solution)/shard_map/ppermute | solution.py:30
  50.6 1.9 collective-permute-start.2
  52.6 5.2 %collective-permute-start.1 = (bf16[2,129,256]{2,1,0:T(8,128)(2,1)S(1)}, bf16[2,129,256]{2,1,0:T(8,128)(2,1)S(1)}, u32[]{:S(2)}, u32[]{:S(2)}) collective-permute-start(bf16[2,129,256]{2,1,0:T(8,128)(2,1)S(1)} %pad_maximum_fusion.4), channel_id=1, source_target_pairs={{0,64},{8,72},{16,80},{24,88},{32,96},{40,104},{48,112},{56,120},{... | collective-permute-start | bytes 396296 | tf_op jit(solution)/shard_map/ppermute | solution.py:30
  57.9 5.3 %collective-permute-done.2 = bf16[2,129,256]{2,1,0:T(8,128)(2,1)S(1)} collective-permute-done((bf16[2,129,256]{2,1,0:T(8,128)(2,1)S(1)}, bf16[2,129,256]{2,1,0:T(8,128)(2,1)S(1)}, u32[]{:S(2)}, u32[]{:S(2)}) %collective-permute-start.2) | collective-permute-done | bytes 132128 | tf_op jit(solution)/shard_map/ppermute | solution.py:30
  63.2 1.1 collective-permute-done.1
  65.2 1.6 collective-permute-start.10
  67.6 6.1 %collective-permute-start.3 = (bf16[4,129,256]{2,1,0:T(8,128)(2,1)S(1)}, bf16[4,129,256]{2,1,0:T(8,128)(2,1)S(1)}, u32[]{:S(2)}, u32[]{:S(2)}) collective-permute-start(bf16[4,129,256]{2,1,0:T(8,128)(2,1)S(1)} %pad_maximum_fusion.1), channel_id=1, source_target_pairs={{0,32},{8,40},{16,48},{24,56},{32,64},{40,72},{48,80},{56,88},{64,... | collective-permute-start | bytes 792584 | tf_op jit(solution)/shard_map/ppermute | solution.py:30
  76.6 2.1 collective-permute-done.10
  85.3 2.0 constant_dynamic-slice_fusion
  87.3 1.9 copy.96
  89.7 1.4 or_and_fusion
  91.1 4.2 %exponential_reduce_fusion = (f32[8,128]{1,0:T(8,128)S(1)}, f32[8,128,1280]{1,2,0:T(8,128)}) fusion(bf16[1280,128,1]{1,0,2:T(8,128)(2,1)S(1)} %bitcast.138, pred[128,1280]{0,1:T(8,128)(4,1)S(1)} %or_and_fusion, bf16[128,8,64]{2,0,1:T(8,128)(2,1)S(1)} %get-tuple-element.44, bf16[128,8,64]{2,0,1:T(8,128)(2,1)S(1)} %get-tuple-element.43), kind=kOutput, calls=%fused_computation.7 | convolution fusion | flops 341312768 | bytes 6000640 | tf_op jit(solution)/shard_map/sub | solution.py:166
  95.3 3.2 %divide_convert_fusion = bf16[8,128,1280]{1,2,0:T(8,128)(2,1)S(1)} fusion(f32[8,128,1280]{1,2,0:T(8,128)} %get-tuple-element.62, f32[8,128]{1,0:T(8,128)S(1)} %get-tuple-element.61), kind=kLoop, calls=%fused_computation.6 | loop fusion | flops 2621440 | bytes 7868416 | tf_op jit(solution)/shard_map/convert_element_type | solution.py:167
  98.5 71.7 %all-gather.2.cloned.1.call-done = bf16[1024,8192]{0,1:T(8,128)(2,1)} async-done(((bf16[1024,256]{0,1:T(8,128)(2,1)}), bf16[1024,8192]{0,1:T(8,128)(2,1)}) %all-gather.2.cloned.1.call-update) | async-done | bytes 16777232 | tf_op jit(solution)/shard_map/all_gather | solution.py:134
  170.2 8.8 %convolution_convert_fusion.1 = bf16[128,1024]{1,0:T(8,128)(2,1)S(1)} fusion(bf16[128,8192]{0,1:T(8,128)(2,1)} %bitcast.126, bf16[1024,8192]{0,1:T(8,128)(2,1)} %all-gather.2.cloned.1.call-done), kind=kOutput, calls=%fused_computation.15 | convolution fusion | flops 2147614720 | bytes 19136512 | tf_op jit(solution)/shard_map/dot_general | solution.py:142
  179.2 1.3 multiply_reduce_fusion
  180.4 1.0 convolution_bitcast_fusion
  182.3 1.5 copy-done
  183.7 1.1 fusion.4
  185.5 1.9 collective-permute-start.18
  187.4 3.0 %collective-permute-start.20 = (bf16[2,128,256]{2,1,0:T(8,128)(2,1)S(1)}, bf16[2,128,256]{2,1,0:T(8,128)(2,1)S(1)}, u32[]{:S(2)}, u32[]{:S(2)}) collective-permute-start(bf16[2,128,256]{2,1,0:T(8,128)(2,1)S(1)} %slice.128), channel_id=1, source_target_pairs={{64,0},{72,8},{80,16},{88,24},{96,32},{104,40},{112,48},{120,56},{... | collective-permute-start | bytes 393224 | tf_op jit(solution)/shard_map/ppermute | solution.py:30
  190.4 8.3 %fusion.38 = f32[128,8192]{0,1:S(1)} fusion(bf16[1024,8192]{0,1:T(8,128)(2,1)} %all-gather.2.cloned.1.call-done, bf16[128,1024]{0,1:T(8,128)(2,1)S(1)} %bitcast.140), kind=kOutput, calls=%fused_computation.134 | convolution fusion | flops 2147483648 | bytes 21233664
  199.3 1.2 dynamic-slice_bitcast_fusion.6
  200.5 2.5 collective-permute-start.11
  203.5 1.5 collective-permute-start.13
  205.0 1.1 fusion.5
  206.1 0.9 convert_add_fusion.1
  207.0 1.0 slice.180
  208.0 1.9 collective-permute-start.19
  210.8 5.0 %collective-permute-start.15 = (bf16[128,32,32]{0,2,1:T(8,128)(2,1)}, bf16[128,32,32]{0,2,1:T(8,128)(2,1)S(1)}, u32[]{:S(2)}, u32[]{:S(2)}) collective-permute-start(bf16[128,32,32]{0,2,1:T(8,128)(2,1)} %get-tuple-element.39), channel_id=1, source_target_pairs={{0,3},{1,4},{2,5},{3,6},{4,7},{5,0},{6,1},{7,2},{8,11},{9,12},{10,... | collective-permute-start | bytes 786440 | tf_op jit(solution)/shard_map/ppermute | solution.py:190
  215.9 4.1 %collective-permute-done.12 = bf16[128,32,32]{0,2,1:T(8,128)(2,1)S(1)} collective-permute-done((bf16[128,32,32]{0,2,1:T(8,128)(2,1)S(1)}, bf16[128,32,32]{0,2,1:T(8,128)(2,1)S(1)}, u32[]{:S(2)}, u32[]{:S(2)}) %collective-permute-start.12) | collective-permute-done | bytes 262176 | tf_op jit(solution)/shard_map/ppermute | solution.py:190
  219.9 5.9 %collective-permute-start.16 = (bf16[128,32,32]{0,2,1:T(8,128)(2,1)}, bf16[128,32,32]{0,2,1:T(8,128)(2,1)S(1)}, u32[]{:S(2)}, u32[]{:S(2)}) collective-permute-start(bf16[128,32,32]{0,2,1:T(8,128)(2,1)} %get-tuple-element.38), channel_id=1, source_target_pairs={{0,2},{1,3},{2,4},{3,5},{4,6},{5,7},{6,0},{7,1},{8,10},{9,11},{10,... | collective-permute-start | bytes 786440 | tf_op jit(solution)/shard_map/ppermute | solution.py:190
  225.8 3.8 %collective-permute-done.19 = bf16[2,128,256]{2,1,0:T(8,128)(2,1)S(1)} collective-permute-done((bf16[2,128,256]{2,1,0:T(8,128)(2,1)S(1)}, bf16[2,128,256]{2,1,0:T(8,128)(2,1)S(1)}, u32[]{:S(2)}, u32[]{:S(2)}) %collective-permute-start.19) | collective-permute-done | bytes 131104 | tf_op jit(solution)/shard_map/ppermute | solution.py:30
  230.6 0.9 copy.110
  231.4 1.1 fusion.13
  232.6 4.8 %collective-permute-start.21 = (bf16[1,128,256]{2,1,0:T(8,128)(2,1)S(1)}, bf16[1,128,256]{2,1,0:T(8,128)(2,1)S(1)}, u32[]{:S(2)}, u32[]{:S(2)}) collective-permute-start(bf16[1,128,256]{2,1,0:T(8,128)(2,1)S(1)} %slice.181), channel_id=1, source_target_pairs={{8,0},{16,8},{24,16},{32,24},{40,32},{48,40},{56,48},{64,56},{72,6... | collective-permute-start | bytes 196616 | tf_op jit(solution)/shard_map/ppermute | solution.py:30
  237.4 1.3 collective-permute-done.17
  238.8 1.5 fusion.12
  241.7 1.0 fusion.25
  (123 shorter events, 23.1 us)
Async XLA Ops:
  7.2 32.2 %copy-start.19 = (s32[1,32]{1,0:T(1,128)S(1)}, s32[1,32]{1,0:T(1,128)}, u32[]{:S(2)}) copy-start(s32[1,32]{1,0:T(1,128)} %param.16) | copy-start | bytes 388
  7.2 163.0 %all-gather.2.cloned.1.call-start = ((), (), s32[]{:S(2)}) async-start(), calls=%async_computation.1 | async-start | bytes 17301504 | tf_op jit(solution)/shard_map/all_gather | solution.py:134
  23.1 41.3 %collective-permute-start.4 = (bf16[128,1024]{0,1:T(8,128)(2,1)S(1)}, bf16[128,1024]{0,1:T(8,128)(2,1)S(1)}, u32[]{:S(2)}, u32[]{:S(2)}) collective-permute-start(bf16[128,1024]{0,1:T(8,128)(2,1)S(1)} %copy.88), channel_id=1, source_target_pairs={{0,7},{1,0},{2,1},{3,2},{4,3},{5,4},{6,5},{7,6},{8,15},{9,8},{10,9... | collective-permute-start | bytes 786440 | tf_op jit(solution)/shard_map/ppermute | solution.py:137
  25.0 40.3 %collective-permute-start.5 = (bf16[128,1024]{0,1:T(8,128)(2,1)S(1)}, bf16[128,1024]{0,1:T(8,128)(2,1)S(1)}, u32[]{:S(2)}, u32[]{:S(2)}) collective-permute-start(bf16[128,1024]{0,1:T(8,128)(2,1)S(1)} %copy.88), channel_id=1, source_target_pairs={{0,6},{1,7},{2,0},{3,1},{4,2},{5,3},{6,4},{7,5},{8,14},{9,15},{10,... | collective-permute-start | bytes 786440 | tf_op jit(solution)/shard_map/ppermute | solution.py:137
  26.2 41.4 %collective-permute-start.6 = (bf16[128,1024]{0,1:T(8,128)(2,1)S(1)}, bf16[128,1024]{0,1:T(8,128)(2,1)S(1)}, u32[]{:S(2)}, u32[]{:S(2)}) collective-permute-start(bf16[128,1024]{0,1:T(8,128)(2,1)S(1)} %copy.88), channel_id=1, source_target_pairs={{0,5},{1,6},{2,7},{3,0},{4,1},{5,2},{6,3},{7,4},{8,13},{9,14},{10,... | collective-permute-start | bytes 786440 | tf_op jit(solution)/shard_map/ppermute | solution.py:137
  27.5 23.1 %copy-start.15 = (f32[64]{0:T(128)}, f32[64]{0:T(128)S(1)}, u32[]{:S(2)}) copy-start(f32[64]{0:T(128)S(1)} %multiply_exponential_fusion) | copy-start | bytes 772
  27.6 40.0 %copy-start.16 = (pred[64]{0:T(512)(128)(4,1)}, pred[64]{0:T(512)(128)(4,1)S(1)}, u32[]{:S(2)}) copy-start(pred[64]{0:T(512)(128)(4,1)S(1)} %get-tuple-element.65) | copy-start | bytes 196
  27.6 40.0 %copy-start.17 = (pred[64]{0:T(512)(128)(4,1)}, pred[64]{0:T(512)(128)(4,1)S(1)}, u32[]{:S(2)}) copy-start(pred[64]{0:T(512)(128)(4,1)S(1)} %get-tuple-element.66) | copy-start | bytes 196
  30.9 19.7 %collective-permute-start = (bf16[1,129,256]{2,1,0:T(8,128)(2,1)S(1)}, bf16[1,129,256]{2,1,0:T(8,128)(2,1)S(1)}, u32[]{:S(2)}, u32[]{:S(2)}) collective-permute-start(bf16[1,129,256]{2,1,0:T(8,128)(2,1)S(1)} %fusion.17), channel_id=1, source_target_pairs={{0,8},{8,16},{16,24},{24,32},{32,40},{40,48},{48,56},{56,64},{64,7... | collective-permute-start | bytes 198152 | tf_op jit(solution)/shard_map/ppermute | solution.py:30
  41.4 49.7 %copy-start.5 = (bf16[128,8,64]{2,0,1:T(8,128)(2,1)}, bf16[128,8,64]{2,0,1:T(8,128)(2,1)S(1)}, u32[]{:S(2)}) copy-start(bf16[128,8,64]{2,0,1:T(8,128)(2,1)S(1)} %get-tuple-element.43) | copy-start | bytes 393220
  41.4 49.7 %copy-start.7 = (bf16[128,8,64]{2,0,1:T(8,128)(2,1)}, bf16[128,8,64]{2,0,1:T(8,128)(2,1)S(1)}, u32[]{:S(2)}) copy-start(bf16[128,8,64]{2,0,1:T(8,128)(2,1)S(1)} %get-tuple-element.44) | copy-start | bytes 393220
  50.6 12.6 %collective-permute-start.2 = (bf16[2,129,256]{2,1,0:T(8,128)(2,1)S(1)}, bf16[2,129,256]{2,1,0:T(8,128)(2,1)S(1)}, u32[]{:S(2)}, u32[]{:S(2)}) collective-permute-start(bf16[2,129,256]{2,1,0:T(8,128)(2,1)S(1)} %pad_maximum_fusion.4), channel_id=1, source_target_pairs={{0,16},{8,24},{16,32},{24,40},{32,48},{40,56},{48,64},{56,72},{64,... | collective-permute-start | bytes 396296 | tf_op jit(solution)/shard_map/ppermute | solution.py:30
  52.6 11.8 %collective-permute-start.1 = (bf16[2,129,256]{2,1,0:T(8,128)(2,1)S(1)}, bf16[2,129,256]{2,1,0:T(8,128)(2,1)S(1)}, u32[]{:S(2)}, u32[]{:S(2)}) collective-permute-start(bf16[2,129,256]{2,1,0:T(8,128)(2,1)S(1)} %pad_maximum_fusion.4), channel_id=1, source_target_pairs={{0,64},{8,72},{16,80},{24,88},{32,96},{40,104},{48,112},{56,120},{... | collective-permute-start | bytes 396296 | tf_op jit(solution)/shard_map/ppermute | solution.py:30
  63.2 11.2 %collective-permute-start.7 = (bf16[128,1024]{0,1:T(8,128)(2,1)S(1)}, bf16[128,1024]{0,1:T(8,128)(2,1)S(1)}, u32[]{:S(2)}, u32[]{:S(2)}) collective-permute-start(bf16[128,1024]{0,1:T(8,128)(2,1)S(1)} %copy.88), channel_id=1, source_target_pairs={{0,4},{1,5},{2,6},{3,7},{4,0},{5,1},{6,2},{7,3},{8,12},{9,13},{10,... | collective-permute-start | bytes 786440 | tf_op jit(solution)/shard_map/ppermute | solution.py:137
  64.4 10.8 %collective-permute-start.8 = (bf16[128,1024]{0,1:T(8,128)(2,1)S(1)}, bf16[128,1024]{0,1:T(8,128)(2,1)S(1)}, u32[]{:S(2)}, u32[]{:S(2)}) collective-permute-start(bf16[128,1024]{0,1:T(8,128)(2,1)S(1)} %copy.88), channel_id=1, source_target_pairs={{0,3},{1,4},{2,5},{3,6},{4,7},{5,0},{6,1},{7,2},{8,11},{9,12},{10,... | collective-permute-start | bytes 786440 | tf_op jit(solution)/shard_map/ppermute | solution.py:137
  64.4 11.5 %collective-permute-start.9 = (bf16[128,1024]{0,1:T(8,128)(2,1)S(1)}, bf16[128,1024]{0,1:T(8,128)(2,1)S(1)}, u32[]{:S(2)}, u32[]{:S(2)}) collective-permute-start(bf16[128,1024]{0,1:T(8,128)(2,1)S(1)} %copy.88), channel_id=1, source_target_pairs={{0,2},{1,3},{2,4},{3,5},{4,6},{5,7},{6,0},{7,1},{8,10},{9,11},{10,... | collective-permute-start | bytes 786440 | tf_op jit(solution)/shard_map/ppermute | solution.py:137
  65.2 13.5 %collective-permute-start.10 = (bf16[128,1024]{0,1:T(8,128)(2,1)S(1)}, bf16[128,1024]{0,1:T(8,128)(2,1)S(1)}, u32[]{:S(2)}, u32[]{:S(2)}) collective-permute-start(bf16[128,1024]{0,1:T(8,128)(2,1)S(1)} %copy.88), channel_id=1, source_target_pairs={{0,1},{1,2},{2,3},{3,4},{4,5},{5,6},{6,7},{7,0},{8,9},{9,10},{10,1... | collective-permute-start | bytes 786440 | tf_op jit(solution)/shard_map/ppermute | solution.py:137
  67.6 21.7 %collective-permute-start.3 = (bf16[4,129,256]{2,1,0:T(8,128)(2,1)S(1)}, bf16[4,129,256]{2,1,0:T(8,128)(2,1)S(1)}, u32[]{:S(2)}, u32[]{:S(2)}) collective-permute-start(bf16[4,129,256]{2,1,0:T(8,128)(2,1)S(1)} %pad_maximum_fusion.1), channel_id=1, source_target_pairs={{0,32},{8,40},{16,48},{24,56},{32,64},{40,72},{48,80},{56,88},{64,... | collective-permute-start | bytes 792584 | tf_op jit(solution)/shard_map/ppermute | solution.py:30
  85.3 4.1 %copy-start.14 = (bf16[128,128]{1,0:T(8,128)(2,1)S(1)}, bf16[128,128]{1,0:T(8,128)(2,1)}, u32[]{:S(2)}) copy-start(bf16[128,128]{1,0:T(8,128)(2,1)} %param.12) | copy-start | bytes 98308
  87.3 2.3 copy-start.18
  89.7 5.7 %copy-start.2 = (bf16[10,128,128]{2,1,0:T(8,128)(2,1)}, bf16[10,128,128]{2,1,0:T(8,128)(2,1)S(1)}, u32[]{:S(2)}) copy-start(bf16[10,128,128]{2,1,0:T(8,128)(2,1)S(1)} %get-tuple-element.45) | copy-start | bytes 983044
  181.4 2.3 copy-start.6
  181.4 2.3 copy-start.8
  182.3 1.5 copy-start
  184.8 5.6 %copy-start.4 = (bf16[128,8,128]{2,0,1:T(8,128)(2,1)S(1)}, bf16[128,8,128]{2,0,1:T(8,128)(2,1)}, u32[]{:S(2)}) copy-start(bf16[128,8,128]{2,0,1:T(8,128)(2,1)} %get-tuple-element.64) | copy-start | bytes 786436
  185.5 20.7 %collective-permute-start.18 = (bf16[4,128,256]{2,1,0:T(8,128)(2,1)S(1)}, bf16[4,128,256]{2,1,0:T(8,128)(2,1)S(1)}, u32[]{:S(2)}, u32[]{:S(2)}) collective-permute-start(bf16[4,128,256]{2,1,0:T(8,128)(2,1)S(1)} %slice.125), channel_id=1, source_target_pairs={{32,0},{40,8},{48,16},{56,24},{64,32},{72,40},{80,48},{88,56},{96,... | collective-permute-start | bytes 786440 | tf_op jit(solution)/shard_map/ppermute | solution.py:30
  187.4 22.8 %collective-permute-start.20 = (bf16[2,128,256]{2,1,0:T(8,128)(2,1)S(1)}, bf16[2,128,256]{2,1,0:T(8,128)(2,1)S(1)}, u32[]{:S(2)}, u32[]{:S(2)}) collective-permute-start(bf16[2,128,256]{2,1,0:T(8,128)(2,1)S(1)} %slice.128), channel_id=1, source_target_pairs={{64,0},{72,8},{80,16},{88,24},{96,32},{104,40},{112,48},{120,56},{... | collective-permute-start | bytes 393224 | tf_op jit(solution)/shard_map/ppermute | solution.py:30
  198.7 6.3 %copy-start.1 = (bf16[8,128,1280]{1,2,0:T(8,128)(2,1)S(1)}, bf16[8,128,1280]{1,2,0:T(8,128)(2,1)}, u32[]{:S(2)}) copy-start(bf16[8,128,1280]{1,2,0:T(8,128)(2,1)} %copy-done) | copy-start | bytes 7864324
  198.7 6.3 %copy-start.3 = (bf16[10,128,128]{2,1,0:T(8,128)(2,1)S(1)}, bf16[10,128,128]{2,1,0:T(8,128)(2,1)}, u32[]{:S(2)}) copy-start(bf16[10,128,128]{2,1,0:T(8,128)(2,1)} %copy-done.2) | copy-start | bytes 983044
  199.3 10.6 %copy-start.11 = (f32[128,64]{1,0:T(8,128)S(1)}, f32[128,64]{1,0:T(8,128)}, u32[]{:S(2)}) copy-start(f32[128,64]{1,0:T(8,128)} %get-tuple-element.55) | copy-start | bytes 98308
  200.5 10.3 %collective-permute-start.11 = (bf16[128,32,32]{0,2,1:T(8,128)(2,1)S(1)}, bf16[128,32,32]{0,2,1:T(8,128)(2,1)S(1)}, u32[]{:S(2)}, u32[]{:S(2)}) collective-permute-start(bf16[128,32,32]{0,2,1:T(8,128)(2,1)S(1)} %get-tuple-element.36), channel_id=1, source_target_pairs={{0,7},{1,0},{2,1},{3,2},{4,3},{5,4},{6,5},{7,6},{8,15},{9,8},{10,9... | collective-permute-start | bytes 786440 | tf_op jit(solution)/shard_map/ppermute | solution.py:190
  203.0 17.0 %collective-permute-start.12 = (bf16[128,32,32]{0,2,1:T(8,128)(2,1)S(1)}, bf16[128,32,32]{0,2,1:T(8,128)(2,1)S(1)}, u32[]{:S(2)}, u32[]{:S(2)}) collective-permute-start(bf16[128,32,32]{0,2,1:T(8,128)(2,1)S(1)} %get-tuple-element.42), channel_id=1, source_target_pairs={{0,6},{1,7},{2,0},{3,1},{4,2},{5,3},{6,4},{7,5},{8,14},{9,15},{10,... | collective-permute-start | bytes 786440 | tf_op jit(solution)/shard_map/ppermute | solution.py:190
  203.5 29.1 %collective-permute-start.13 = (bf16[128,32,32]{0,2,1:T(8,128)(2,1)}, bf16[128,32,32]{0,2,1:T(8,128)(2,1)}, u32[]{:S(2)}, u32[]{:S(2)}) collective-permute-start(bf16[128,32,32]{0,2,1:T(8,128)(2,1)} %get-tuple-element.41), channel_id=1, source_target_pairs={{0,5},{1,6},{2,7},{3,0},{4,1},{5,2},{6,3},{7,4},{8,13},{9,14},{10,... | collective-permute-start | bytes 786440 | tf_op jit(solution)/shard_map/ppermute | solution.py:190
  208.0 21.6 %collective-permute-start.19 = (bf16[2,128,256]{2,1,0:T(8,128)(2,1)S(1)}, bf16[2,128,256]{2,1,0:T(8,128)(2,1)S(1)}, u32[]{:S(2)}, u32[]{:S(2)}) collective-permute-start(bf16[2,128,256]{2,1,0:T(8,128)(2,1)S(1)} %slice.180), channel_id=1, source_target_pairs={{16,0},{24,8},{32,16},{40,24},{48,32},{56,40},{64,48},{72,56},{80,... | collective-permute-start | bytes 393224 | tf_op jit(solution)/shard_map/ppermute | solution.py:30
  210.2 20.1 %copy-start.12 = (bf16[2,128,256]{2,1,0:T(8,128)(2,1)}, bf16[2,128,256]{2,1,0:T(8,128)(2,1)S(1)}, u32[]{:S(2)}) copy-start(bf16[2,128,256]{2,1,0:T(8,128)(2,1)S(1)} %collective-permute-done.20) | copy-start | bytes 393220
  210.2 27.2 %collective-permute-start.14 = (bf16[128,32,32]{0,2,1:T(8,128)(2,1)}, bf16[128,32,32]{0,2,1:T(8,128)(2,1)S(1)}, u32[]{:S(2)}, u32[]{:S(2)}) collective-permute-start(bf16[128,32,32]{0,2,1:T(8,128)(2,1)} %get-tuple-element.40), channel_id=1, source_target_pairs={{0,4},{1,5},{2,6},{3,7},{4,0},{5,1},{6,2},{7,3},{8,12},{9,13},{10,... | collective-permute-start | bytes 786440 | tf_op jit(solution)/shard_map/ppermute | solution.py:190
  210.8 19.4 %copy-start.9 = (bf16[128,32,32]{0,2,1:T(8,128)(2,1)}, bf16[128,32,32]{0,2,1:T(8,128)(2,1)S(1)}, u32[]{:S(2)}) copy-start(bf16[128,32,32]{0,2,1:T(8,128)(2,1)S(1)} %collective-permute-done.11) | copy-start | bytes 786436
  210.8 26.6 %collective-permute-start.15 = (bf16[128,32,32]{0,2,1:T(8,128)(2,1)}, bf16[128,32,32]{0,2,1:T(8,128)(2,1)S(1)}, u32[]{:S(2)}, u32[]{:S(2)}) collective-permute-start(bf16[128,32,32]{0,2,1:T(8,128)(2,1)} %get-tuple-element.39), channel_id=1, source_target_pairs={{0,3},{1,4},{2,5},{3,6},{4,7},{5,0},{6,1},{7,2},{8,11},{9,12},{10,... | collective-permute-start | bytes 786440 | tf_op jit(solution)/shard_map/ppermute | solution.py:190
  219.9 10.3 %copy-start.10 = (bf16[128,32,32]{0,2,1:T(8,128)(2,1)}, bf16[128,32,32]{0,2,1:T(8,128)(2,1)S(1)}, u32[]{:S(2)}) copy-start(bf16[128,32,32]{0,2,1:T(8,128)(2,1)S(1)} %collective-permute-done.12) | copy-start | bytes 786436
  219.9 17.5 %collective-permute-start.16 = (bf16[128,32,32]{0,2,1:T(8,128)(2,1)}, bf16[128,32,32]{0,2,1:T(8,128)(2,1)S(1)}, u32[]{:S(2)}, u32[]{:S(2)}) collective-permute-start(bf16[128,32,32]{0,2,1:T(8,128)(2,1)} %get-tuple-element.38), channel_id=1, source_target_pairs={{0,2},{1,3},{2,4},{3,5},{4,6},{5,7},{6,0},{7,1},{8,10},{9,11},{10,... | collective-permute-start | bytes 786440 | tf_op jit(solution)/shard_map/ppermute | solution.py:190
  229.6 0.7 copy-start.13
  229.6 9.2 %collective-permute-start.17 = (bf16[128,32,32]{0,2,1:T(8,128)(2,1)}, bf16[128,32,32]{0,2,1:T(8,128)(2,1)}, u32[]{:S(2)}, u32[]{:S(2)}) collective-permute-start(bf16[128,32,32]{0,2,1:T(8,128)(2,1)} %get-tuple-element.37), channel_id=1, source_target_pairs={{0,1},{1,2},{2,3},{3,4},{4,5},{5,6},{6,7},{7,0},{8,9},{9,10},{10,1... | collective-permute-start | bytes 786440 | tf_op jit(solution)/shard_map/ppermute | solution.py:190
  232.6 8.5 %collective-permute-start.21 = (bf16[1,128,256]{2,1,0:T(8,128)(2,1)S(1)}, bf16[1,128,256]{2,1,0:T(8,128)(2,1)S(1)}, u32[]{:S(2)}, u32[]{:S(2)}) collective-permute-start(bf16[1,128,256]{2,1,0:T(8,128)(2,1)S(1)} %slice.181), channel_id=1, source_target_pairs={{8,0},{16,8},{24,16},{32,24},{40,32},{48,40},{56,48},{64,56},{72,6... | collective-permute-start | bytes 196616 | tf_op jit(solution)/shard_map/ppermute | solution.py:30
Sparse Core Ops, SparseCore 0:
  22.1 148.0 all-gather.1
